TPU v7x, 512 devices: a whole 4x4x16 slice. The times are simulated.
512 devices in a mesh: mesh: 64 (over y, z), band: 8 (over x, core).
Axes of the slice: x: 4, y: 4, z: 16, core: 2. Of those that a mesh axis runs over, the one named last changes fastest.
Arguments:
- state: bfloat16 [65536, 2048], P('mesh', 'band'), may hold values from -6 to 6
- prev_state: bfloat16 [65536, 2048], P('mesh', 'band'), may hold values from -6 to 6
- mass: float32 [65536], P('mesh'), may hold values from 0.1 to 1.9
- cell_nodes: int32 [256, 512], P('mesh'), may hold values from 0 to 1279, as said below
- cell_live: int32 [64], P('mesh'), may hold values from 1 to 4, 192 in all
- cell_scale: float32 [256], P('mesh'), may hold values from 0.5 to 2
- potential: float32 [256, 512], P('mesh'), may hold values from -6 to 6
- stiffness: bfloat16 [512, 512], replicated, may hold values from -0.25 to 0.25
- shape_values: bfloat16 [512, 512], replicated, may hold values from -0.25 to 0.25
- cell_proj: bfloat16 [256, 512, 128], P('mesh', 'band'), may hold values from -0.25 to 0.25
- cell_owner: int32 [256, 8], P('mesh'), may hold values from 0 to 63, as said below
- cell_slot: int32 [256, 8], P('mesh'), may hold values from 0 to 7, as said below
- coupling: float32 [512, 16], P('mesh'), may hold values from -6 to 6
- send_rows: int32 [64, 256], P('mesh'), may hold values from 0 to 1023, as said below
Outputs:
- filtered_one: bfloat16 [65536, 2048], P('mesh', 'band')
- filtered_two: bfloat16 [65536, 2048], P('mesh', 'band')
Inputs may be any that keep to these rules, and one draw needn't show every extreme that they name: `cell_nodes`: the 512 entries of a cell are distinct; entries below 256 name the partition's ghost rows, the others its own node (entry minus 256); every entry value of a partition is named by some cell of it. `cell_live`: slots at or after this count are padding. `cell_owner`: the owners lie within two partitions of the cell's own; the 8 atoms of a cell are distinct. `cell_slot`: an atom's index among the 8 atoms of its owner. `send_rows`: each row holds distinct indices of the partition's own nodes; the last partition's row is not read.
All inputs are finite; a program needn't handle non-finite values. No bound on the sum of `cell_live` on one device may be relied on, other than what follows from the above.
Results may differ from a plain program's by a relative error of at most 0.0085.
Values may be sent and summed in bfloat16 or wider, within the bound.
No kernel may reach another device: no remote copies, remote signals or barrier semaphores. Data moves between devices by JAX's collectives and lax.ppermute only.
A program may use at most 64 MiB of HBM per device.

v0:
```python
import jax
import jax.numpy as jnp
from jax import lax
from jax.experimental import pallas as pl
from jax.experimental.pallas import tpu as pltpu
from jax.sharding import PartitionSpec as P


APC = 8
FLIPS = (0, 1, 3, 2)
F32 = jnp.float32
BF16 = jnp.bfloat16
LANES = 128

filter_scale = 0.6
filter_shift = 1.0

VMEM = pl.BlockSpec(memory_space=pltpu.VMEM)
SMEM = pl.BlockSpec(memory_space=pltpu.SMEM)


def from_behind(block, axis, distance):
    devices = range(lax.axis_size(axis))
    route = [(i - distance, i) for i in devices if i - distance in devices]
    return lax.ppermute(block, axis, route)


def dot(a, b):
    return jnp.dot(a, b, preferred_element_type=F32)


def column(row):
    n = row.shape[1]
    parts = [
        jnp.transpose(jnp.broadcast_to(row[:, i : i + LANES], (LANES, LANES)))
        for i in range(0, n, LANES)
    ]
    return jnp.concatenate(parts, axis=0)


def widen(col, width):
    return jnp.concatenate([col] * (width // LANES), axis=1)


def hot_rows(row, width):
    col = column(row.astype(F32)).astype(jnp.int32)
    lane = lax.broadcasted_iota(jnp.int32, col.shape, 1)
    parts = [(col == lane + i).astype(F32).astype(BF16) for i in range(0, width, LANES)]
    return jnp.concatenate(parts, axis=1)


def hot_columns(row, height):
    n = row.shape[1]
    line = lax.broadcasted_iota(jnp.int32, (height, n), 0)
    return (line == row).astype(F32).astype(BF16)


def split_rows(row):
    high = row.astype(BF16).astype(F32)
    middle = (row - high).astype(BF16).astype(F32)
    low = row - high - middle
    line = lax.broadcasted_iota(jnp.int32, (16, row.shape[1]), 0)
    parts = jnp.where(line == 0, high, jnp.where(line == 1, middle, jnp.where(line == 2, low, 0.0)))
    return parts.astype(BF16)


def is_left():
    return lax.rem(lax.axis_index("mesh"), 2) == 0


def start_kernel(state, mass, send, coupling, scaled, outgoing, strengths):
    atoms, per_atom = coupling.shape
    width = atoms * per_atom
    spread = jnp.concatenate(
        [jnp.broadcast_to(coupling[a : a + 1, :], (per_atom, per_atom)) for a in range(atoms)], axis=0
    )
    line = lax.broadcasted_iota(jnp.int32, spread.shape, 0)
    lane = lax.broadcasted_iota(jnp.int32, spread.shape, 1)
    tall = jnp.sum(jnp.where(line % per_atom == lane, spread, 0.0), axis=1, keepdims=True)
    square = (width, width)
    diagonal = lax.broadcasted_iota(jnp.int32, square, 0) == lax.broadcasted_iota(jnp.int32, square, 1)
    row = jnp.sum(jnp.where(diagonal, jnp.broadcast_to(tall, square), 0.0), axis=0, keepdims=True)
    strengths[...] = jnp.concatenate([split_rows(row)] * (strengths.shape[1] // width), axis=1)
    m = widen(column(mass[...]), state.shape[1])
    scaled[...] = (m * state[...].astype(F32)).astype(BF16)
    face = send.shape[1]
    outgoing[0:face, :] = dot(hot_rows(send[...], state.shape[0]), scaled[...]).astype(BF16)
    outgoing[face : face + 16, :] = dot(
        split_rows(mass[...]), hot_columns(send[...], state.shape[0])
    ).astype(BF16)


def hot_kernel(nodes, pick, place):
    cells, per_cell = nodes.shape
    extended = place.shape[0]
    for c in range(cells):
        row = nodes[c : c + 1, :]
        pick[c * per_cell : (c + 1) * per_cell, :] = hot_rows(row, extended)
        place[:, c * per_cell : (c + 1) * per_cell] = hot_columns(row, extended)


def operator_kernel(potential, stiffness, shape_values, live, scale, operator):
    values = shape_values[...].astype(F32)
    turned = jnp.transpose(shape_values[...])
    for c in range(potential.shape[0]):
        points = column(potential[c : c + 1, :])
        weighted = (widen(points, values.shape[1]) * values).astype(BF16)
        alive = jnp.where(c < live[0], 1.0, 0.0)
        local = 0.5 * scale[c] * stiffness[...].astype(F32) + dot(turned, weighted)
        operator[c] = (alive * local).astype(BF16)


def store_sums(table, field, sent, outward, base):
    sums = dot(table[...], field[...])
    n = sent.shape[0]
    left = is_left()
    sent[...] = jnp.where(left, sums[4 * n :, :], sums[0:n, :]).astype(BF16)
    outward[...] = jnp.where(left, sums[0 : 2 * n, :], sums[3 * n :, :]).astype(BF16)
    base[...] = jnp.where(left, sums[2 * n : 4 * n, :], sums[n : 3 * n, :])


def table_kernel(
    projectors, pick, owner, slot, live, ghost, scaled,
    table, sent, outward, base, wide, field, nodes,
):
    here, x = lax.axis_index("mesh"), lax.axis_index("band") // 2
    cells, per_atom = owner.shape[0], table.shape[0] // (5 * APC)
    per_cell = pick.shape[0] // cells
    share = projectors.shape[3]
    face = scaled.shape[0] // 4
    wide[...] = jnp.zeros_like(wide)
    field[0:face, :] = ghost[0:face, :]
    field[face:, :] = scaled[...]
    for c in range(cells):
        for i, flip in enumerate(FLIPS):
            for core in range(2):
                band = (x ^ flip) * 2 + core
                rows = pl.ds(pl.multiple_of(band * share, share), share)
                nodes[rows, :] = projectors[core, i, c].astype(F32)
        block = jnp.transpose(nodes[...]).astype(BF16)
        at_nodes = dot(block, pick[c * per_cell : (c + 1) * per_cell, :])
        at_nodes = at_nodes * jnp.where(c < live[0], 1.0, 0.0)
        for j in range(APC):
            target = (owner[c, j] - here + 2) * APC + slot[c, j]
            rows = pl.ds(pl.multiple_of(target * per_atom, per_atom), per_atom)
            wide[rows, :] = wide[rows, :] + at_nodes[per_atom * j : per_atom * (j + 1), :]
    table[...] = wide[...].astype(BF16)
    store_sums(table, field, sent, outward, base)


def turn_kernel(table, turned):
    turned[...] = jnp.transpose(table[...])


def gather_kernel(pick, operator, ghost, scaled, terms, field):
    face = scaled.shape[0] // 4
    cells, per_cell = operator.shape[0], operator.shape[1]
    field[0:face, :] = ghost[0:face, :]
    field[face:, :] = scaled[...]
    for c in range(cells):
        rows = slice(c * per_cell, (c + 1) * per_cell)
        cell = dot(pick[rows, :], field[...]).astype(BF16)
        terms[rows, :] = dot(operator[c], cell).astype(BF16)


def scatter_kernel(place, terms, out):
    out[...] = dot(place[...], terms[...])


def join_kernel(base, both, far, strengths, mine, message):
    n = far.shape[0]
    left = is_left()
    here = lax.axis_index("mesh")
    inside = jnp.logical_and(here > 0, here < lax.axis_size("mesh") - 1)
    inward = jnp.where(left, both[0], both[1]).astype(F32)
    total = base[...] + jnp.where(inside, inward, 0.0)
    added = far[...].astype(F32)
    mine[0:n, :] = total[0:n, :] + jnp.where(left, added, 0.0)
    mine[n:, :] = total[n:, :] + jnp.where(left, 0.0, added)
    message[0 : 2 * n, :] = mine[...].astype(BF16)
    message[2 * n :, :] = strengths[...]


def couple_kernel(mine, message, strengths, pair, sent):
    n = sent.shape[0]

    def tall(rows):
        split = rows[...].astype(F32)
        return column(split[0:1, 0:n] + split[1:2, 0:n] + split[2:3, 0:n])

    own, other = tall(strengths), tall(message.at[2 * n : 2 * n + 16, :])
    left = is_left()
    for i in range(2):
        at = slice(i * n, (i + 1) * n)
        total = mine[at, :] + message[at, :].astype(F32)
        factor = jnp.where(left, own, other) if i == 0 else jnp.where(left, other, own)
        pair[at, :] = (widen(factor, total.shape[1]) * total).astype(BF16)
    sent[...] = jnp.where(left, pair[0:n, :], pair[n:, :])


def window_values(pair, both, far):
    left = is_left()
    n = far.shape[0]
    beside = jnp.where(left, both[0], both[1])
    return jnp.concatenate(
        [
            jnp.where(left, beside[0:n], far[...]),
            jnp.where(left, beside[n:], pair[0:n, :]),
            jnp.where(left, pair[0:n, :], pair[n:, :]),
            jnp.where(left, pair[n:, :], beside[0:n]),
            jnp.where(left, far[...], beside[n:]),
        ]
    )


def apply_out(turned, pair, both, far, local):
    return local[...] + dot(turned[...], window_values(pair, both, far))


def middle_kernel(
    turned, pair, both, far, local, state, prev, mass, send, returned, own, edge, message
):
    face = send.shape[1]
    total = apply_out(turned, pair, both, far, local)
    returned[...] = total[0:face, :].astype(BF16)
    own[...] = total[face:, :]
    m = widen(column(mass[...]), state.shape[1])
    current = state[...].astype(F32)
    partial = filter_scale * (m * own[...] - filter_shift * current) - prev[...].astype(F32)
    edge[...] = dot(hot_rows(send[...], state.shape[0]), (m * partial).astype(BF16)).astype(BF16)
    left = is_left()
    message[0] = jnp.where(left, edge[...], returned[...])
    message[1] = jnp.where(left, returned[...], edge[...])


def next_kernel(
    own, inner, outer, returned, ghost, state, prev, mass, send, table,
    first, scaled, ghost_next, sent, outward, base, field,
):
    face = send.shape[1]
    m = widen(column(mass[...]), state.shape[1])
    left = is_left()
    within = jnp.where(left, inner[1], inner[0])
    received = jnp.where(left, within, outer[...])
    edge = jnp.where(left, outer[...], within)
    owned = own[...] + dot(hot_columns(send[...], state.shape[0]), received)
    current = state[...].astype(F32)
    one = filter_scale * (m * owned - filter_shift * current) - prev[...].astype(F32)
    first[...] = one.astype(BF16)
    scaled[...] = (m * first[...].astype(F32)).astype(BF16)
    split = ghost[face : face + 16, :].astype(F32)
    g = widen(column(split[0:1, :] + split[1:2, :] + split[2:3, :]), state.shape[1])
    ghost_next[...] = (
        edge.astype(F32) + (filter_scale * g * g) * returned[...].astype(F32)
    ).astype(BF16)
    field[0:face, :] = ghost_next[...]
    field[face:, :] = scaled[...]
    store_sums(table, field, sent, outward, base)


def end_kernel(turned, pair, both, far, local, returned, own):
    face = returned.shape[0]
    total = apply_out(turned, pair, both, far, local)
    returned[...] = total[0:face, :].astype(BF16)
    own[...] = total[face:, :]


def last_kernel(own, received, state, first, mass, send, second):
    m = widen(column(mass[...]), state.shape[1])
    owned = own[...] + dot(hot_columns(send[...], state.shape[0]), received[...])
    two = filter_scale * (m * owned - filter_shift * first[...].astype(F32))
    second[...] = (two - state[...].astype(F32)).astype(BF16)


def call(kernel, outs, args, specs=None, scratch=(), mib=8):
    return pl.pallas_call(
        kernel,
        out_shape=[
            kept[0](*kept[1:]) if kept else jax.ShapeDtypeStruct(shape, kind)
            for shape, kind, *kept in outs
        ],
        in_specs=specs or [VMEM] * len(args),
        out_specs=[VMEM] * len(outs),
        scratch_shapes=list(scratch),
        compiler_params=pltpu.CompilerParams(vmem_limit_bytes=mib << 20),
    )(*args)


def kept(shape, kind):
    return (shape, kind, pltpu.VMEM, shape, kind)


def hold(block):
    return pltpu.with_memory_space_constraint(block, pltpu.VMEM)


def leave(block):
    return pltpu.with_memory_space_constraint(block, pltpu.HBM)


def inner_pairs(block):
    n = lax.axis_size("mesh")
    groups = [[i, i + 1] for i in range(0, n, 2)]
    return lax.all_gather(block, "mesh", axis=0, axis_index_groups=groups)


def outer_pairs(block):
    n, m = lax.axis_size("mesh"), lax.axis_size("band")
    groups = [[i * m + k, (i + 1) * m + k] for i in range(1, n - 1, 2) for k in range(m)]
    groups += [[i * m + k, i * m + k + 1] for i in (0, n - 1) for k in range(0, m, 2)]
    return lax.all_gather(block, ("mesh", "band"), axis=0, axis_index_groups=groups)


def outer_swap(block):
    n = lax.axis_size("mesh")
    route = [(i, i + 1 if i % 2 else i - 1) for i in range(1, n - 1)]
    return lax.ppermute(block, "mesh", route)


def two_away(block, way):
    n = lax.axis_size("mesh")
    route = [(i, i + (2 * way if i % 2 == 0 else -2 * way)) for i in range(n)]
    return lax.ppermute(block, "mesh", [(i, j) for i, j in route if 0 <= j < n])


def swap(block, axis, mask):
    return lax.ppermute(block, axis, [(i, i ^ mask) for i in range(lax.axis_size(axis))])


def shards(
    state,
    prev_state,
    mass,
    cell_nodes,
    cell_live,
    cell_scale,
    potential,
    stiffness,
    shape_values,
    cell_proj,
    cell_owner,
    cell_slot,
    coupling,
    send_rows,
):
    own_rows, orbitals = state.shape
    cells, per_cell = cell_nodes.shape
    atoms, per_atom = coupling.shape
    face = send_rows.shape[1]
    extended = own_rows + face
    block = atoms * per_atom
    window = 5 * block
    mass_row = mass.reshape(1, own_rows)
    other = swap(cell_proj, "band", 2)
    start = call
    scaled, outgoing, strengths = start(
        start_kernel,
        [
            ((own_rows, orbitals), BF16),
            ((face + 16, orbitals), BF16),
            ((16, orbitals), BF16),
        ],
        [leave(block) for block in (state, mass_row, send_rows, coupling)],
    )
    ghost = from_behind(outgoing, "mesh", 1)

    pick, place = call(
        hot_kernel,
        [kept((cells * per_cell, extended), BF16), kept((extended, cells * per_cell), BF16)],
        (leave(cell_nodes),),
    )
    pick, place = hold(pick), hold(place)
    near = jnp.stack([cell_proj, other])
    far = swap(near, "band", 6)
    (operator,) = call(
        operator_kernel,
        [kept((cells, per_cell, per_cell), BF16)],
        (leave(potential), leave(stiffness), leave(shape_values), cell_live, cell_scale),
        specs=[VMEM, VMEM, VMEM, SMEM, SMEM],
    )
    operator = hold(operator)
    projectors = lax.all_gather(
        jnp.concatenate([near, far], axis=0),
        "band",
        axis=0,
        axis_index_groups=[[0, 1], [2, 3], [4, 5], [6, 7]],
    )

    sums_of = [((block, orbitals), BF16), ((2 * block, orbitals), BF16), ((2 * block, orbitals), F32)]
    table, *sums = call(
        table_kernel,
        [kept((window, extended), BF16)] + sums_of,
        (projectors, pick, cell_owner, cell_slot, cell_live, ghost, scaled),
        specs=[VMEM, VMEM, SMEM, SMEM, SMEM, VMEM, VMEM],
        scratch=[
            pltpu.VMEM((window, extended), F32),
            pltpu.VMEM((extended, orbitals), BF16),
            pltpu.VMEM((per_cell, block), F32),
        ],
    )
    table = hold(table)
    (turned,) = call(turn_kernel, [kept((extended, window), BF16)], (table,))
    turned = hold(turned)

    def atom_values(sums, terms):
        sent, outward, base = sums
        far = two_away(sent, 1)
        both = outer_pairs(outward)
        mine, message = call(
            join_kernel,
            [((2 * block, orbitals), F32), ((2 * block + 16, orbitals), BF16)],
            (base, both, far, strengths),
        )
        message, terms = lax.optimization_barrier((swap(message, "mesh", 1), terms))
        pair, sent = call(
            couple_kernel,
            [((2 * block, orbitals), BF16), ((block, orbitals), BF16)],
            (mine, message, strengths),
        )
        far = two_away(sent, -1)
        both = outer_pairs(pair)
        (local,) = call(scatter_kernel, [((extended, orbitals), F32)], (place, terms))
        return (pair, both, far), local

    def cell_terms(ghost, scaled):
        (terms,) = call(
            gather_kernel,
            [((cells * per_cell, orbitals), BF16)],
            (pick, operator, ghost, scaled),
            scratch=[pltpu.VMEM((extended, orbitals), BF16)],
        )
        return terms

    nodal = ((own_rows, orbitals), BF16)
    shared = ((face, orbitals), BF16)
    own_wide = ((own_rows, orbitals), F32)

    values, local = atom_values(sums, cell_terms(ghost, scaled))
    returned, own, _, message = call(
        middle_kernel,
        [shared, own_wide, shared, ((2, face, orbitals), BF16)],
        (turned, *values, local, state, prev_state, mass_row, send_rows),
    )
    outer = outer_swap(message[1])
    inner = inner_pairs(message[0])
    first, scaled_one, ghost_one, *sums_one = call(
        next_kernel,
        [nodal, nodal, shared] + sums_of,
        (own, inner, outer, returned, ghost, state, prev_state, mass_row, send_rows, table),
        scratch=[pltpu.VMEM((extended, orbitals), BF16)],
    )
    terms_one = cell_terms(ghost_one, scaled_one)
    values_one, local_one = atom_values(sums_one, terms_one)
    returned_one, own_one = call(
        end_kernel, [shared, own_wide], (turned, *values_one, local_one)
    )
    received_one = from_behind(returned_one, "mesh", -1)
    (second,) = call(
        last_kernel, [nodal], (own_one, received_one, state, first, mass_row, send_rows)
    )
    return (first, second)


def solution(mesh):
    placed = (
        P("mesh", "band"),
        P("mesh", "band"),
        P("mesh"),
        P("mesh", None),
        P("mesh"),
        P("mesh"),
        P("mesh", None),
        P(),
        P(),
        P("mesh", "band", None),
        P("mesh", None),
        P("mesh", None),
        P("mesh", None),
        P("mesh", None),
    )

    return jax.shard_map(
        shards,
        mesh=mesh,
        in_specs=placed,
        out_specs=(P("mesh", "band"), P("mesh", "band")),
        check_vma=False,
    )
```

profile of v0, /device:TPU:24, one launch (start us, length us, event | category | flops | bytes accessed | tf_op | source)
XLA Modules:
  0.0 124.3 jit_solution(9032097119802147329)
XLA Ops:
  0.6 3.5 %collective-permute-start = (bf16[4,64,128]{2,1,0:T(8,128)(2,1)}, bf16[4,64,128]{2,1,0:T(8,128)(2,1)S(1)}, u32[]{:S(2)}, u32[]{:S(2)}) collective-permute-start(bf16[4,64,128]{2,1,0:T(8,128)(2,1)} %param.23), channel_id=1, source_target_pairs={{0,2},{1,3},{2,0},{3,1},{4,6},{5,7},{6,4},{7,5},{8,10},{9,11},{10,... | collective-permute-start | bytes 196616 | tf_op jit(solution)/shard_map/ppermute | solution.py:327
  4.2 3.0 %collective-permute-done = bf16[4,64,128]{2,1,0:T(8,128)(2,1)S(1)} collective-permute-done((bf16[4,64,128]{2,1,0:T(8,128)(2,1)}, bf16[4,64,128]{2,1,0:T(8,128)(2,1)S(1)}, u32[]{:S(2)}, u32[]{:S(2)}) %collective-permute-start) | collective-permute-done | bytes 65568 | tf_op jit(solution)/shard_map/ppermute | solution.py:327
  7.2 0.9 pad_maximum_fusion.1
  8.0 4.7 %collective-permute-start.1 = (bf16[2,4,64,128]{3,2,1,0:T(8,128)(2,1)S(1)}, bf16[2,4,64,128]{3,2,1,0:T(8,128)(2,1)S(1)}, u32[]{:S(2)}, u32[]{:S(2)}) collective-permute-start(bf16[2,4,64,128]{3,2,1,0:T(8,128)(2,1)S(1)} %pad_maximum_fusion.1), channel_id=1, source_target_pairs={{0,6},{1,7},{2,4},{3,5},{4,2},{5,3},{6,0},{7,1},{8,14},{9,15},{10,... | collective-permute-start | bytes 393224 | tf_op jit(solution)/shard_map/ppermute | solution.py:327
  12.7 1.6 %shard_map.150 = (bf16[1024,256]{1,0:T(8,128)(2,1)S(1)}, bf16[272,256]{1,0:T(8,128)(2,1)S(1)}, bf16[16,256]{1,0:T(8,128)(2,1)S(1)}) custom-call(bf16[1024,256]{1,0:T(8,128)(2,1)} %state.7, f32[1,1024]{1,0:T(1,128)} %bitcast.15, s32[1,256]{1,0:T(1,128)} %send.7, f32[8,16]{1,0:T(8,128)} %coupling.1), custom_call_target="tpu_custom_call" | custom-call | tf_op jit(solution)/shard_map/pallas_call | solution.py:276
  14.3 3.8 %collective-permute-start.2 = (bf16[272,256]{1,0:T(8,128)(2,1)S(1)}, bf16[272,256]{1,0:T(8,128)(2,1)S(1)}, u32[]{:S(2)}, u32[]{:S(2)}) collective-permute-start(bf16[272,256]{1,0:T(8,128)(2,1)S(1)} %get-tuple-element.35), channel_id=1, source_target_pairs={{0,8},{8,16},{16,24},{24,32},{32,40},{40,48},{48,56},{56,64},{64,7... | collective-permute-start | bytes 417800 | tf_op jit(solution)/shard_map/ppermute | solution.py:25
  18.7 4.2 %shard_map.149 = (bf16[2048,1280]{1,0:T(8,128)(2,1)S(1)}, bf16[1280,2048]{1,0:T(8,128)(2,1)S(1)}) custom-call(s32[4,512]{1,0:T(4,128)} %nodes.1), custom_call_target="tpu_custom_call" | custom-call | tf_op jit(solution)/shard_map/pallas_call | solution.py:276
  23.0 0.0 collective-permute-done.1
  23.0 0.9 pad_maximum_fusion
  23.8 2.2 %all-gather = bf16[8,4,64,128]{3,2,1,0:T(8,128)(2,1)S(1)} all-gather(bf16[4,4,64,128]{3,2,1,0:T(8,128)(2,1)S(1)} %pad_maximum_fusion), channel_id=2, replica_groups={{0,1},{2,3},{4,5},{6,7},{8,9},{10,11},{12,13},{14,15},{16,17},{18,19},{..., dimensions={0}, use_global_device_ids=true | all-gather | bytes 786432 | tf_op jit(solution)/shard_map/all_gather | solution.py:382
  26.0 2.9 %collective-permute-done.2.ghost = bf16[272,256]{1,0:T(8,128)(2,1)S(1)} collective-permute-done((bf16[272,256]{1,0:T(8,128)(2,1)S(1)}, bf16[272,256]{1,0:T(8,128)(2,1)S(1)}, u32[]{:S(2)}, u32[]{:S(2)}) %collective-permute-start.2) | collective-permute-done | bytes 139296 | tf_op jit(solution)/shard_map/ppermute | solution.py:25
  28.9 2.6 %shard_map.151 = (bf16[640,1280]{1,0:T(8,128)(2,1)S(1)}, bf16[128,256]{1,0:T(8,128)(2,1)S(1)}, bf16[256,256]{1,0:T(8,128)(2,1)S(1)}, f32[256,256]{1,0:T(8,128)S(1)}) custom-call(bf16[2,4,4,64,128]{4,3,2,1,0:T(8,128)(2,1)S(1)} %bitcast.10, bf16[2048,1280]{1,0:T(8,128)(2,1)S(1)} %get-tuple-element.34.pick, s32[4,8]{1,0:T(4,128)S(1)} %copy-done.5, ...), custom_call_target="tpu_custom_call" | custom-call | tf_op jit(solution)/shard_map/pallas_call | solution.py:276
  31.5 2.3 %collective-permute-start.3 = (bf16[128,256]{1,0:T(8,128)(2,1)S(1)}, bf16[128,256]{1,0:T(8,128)(2,1)S(1)}, u32[]{:S(2)}, u32[]{:S(2)}) collective-permute-start(bf16[128,256]{1,0:T(8,128)(2,1)S(1)} %get-tuple-element.40), channel_id=1, source_target_pairs={{0,16},{16,32},{24,8},{32,48},{40,24},{48,64},{56,40},{64,80},{72,... | collective-permute-start | bytes 196616 | tf_op jit(solution)/shard_map/ppermute | solution.py:323
  33.8 11.1 %all-gather.1 = bf16[512,256]{1,0:T(8,128)(2,1)S(1)} all-gather(bf16[256,256]{1,0:T(8,128)(2,1)S(1)} %get-tuple-element.39), channel_id=3, replica_groups={{8,16},{9,17},{10,18},{11,19},{12,20},{13,21},{14,22},{15,23},{24,32},{..., dimensions={0}, use_global_device_ids=true | all-gather | bytes 393216 | tf_op jit(solution)/shard_map/all_gather | solution.py:311
  45.0 0.0 collective-permute-done.3.far
  45.0 0.1 shard_map.153
  45.1 2.7 %collective-permute-start.4 = (bf16[272,256]{1,0:T(8,128)(2,1)S(1)}, bf16[272,256]{1,0:T(8,128)(2,1)S(1)}, u32[]{:S(2)}, u32[]{:S(2)}) collective-permute-start(bf16[272,256]{1,0:T(8,128)(2,1)S(1)} %get-tuple-element.43), channel_id=1, source_target_pairs={{0,8},{8,0},{16,24},{24,16},{32,40},{40,32},{48,56},{56,48},{64,72... | collective-permute-start | bytes 417800 | tf_op jit(solution)/shard_map/ppermute | solution.py:327
  47.7 2.6 %shard_map.154.operator = bf16[4,512,512]{2,1,0:T(8,128)(2,1)S(1)} custom-call(f32[4,512]{1,0:T(4,128)} %potential.1, bf16[512,512]{1,0:T(8,128)(2,1)} %stiffness.1, bf16[512,512]{1,0:T(8,128)(2,1)} %shape_values.1, s32[1]{0:T(128)S(6)} %copy.16.live, f32[4]{0:T(128)S(1)} %copy-done.7), custom_call_target="tpu_custom_call" | custom-call | tf_op jit(solution)/shard_map/pallas_call | solution.py:276
  50.3 4.1 %shard_map.155.terms = bf16[2048,256]{1,0:T(8,128)(2,1)S(1)} custom-call(bf16[2048,1280]{1,0:T(8,128)(2,1)S(1)} %get-tuple-element.34.pick, bf16[4,512,512]{2,1,0:T(8,128)(2,1)S(1)} %shard_map.154.operator, bf16[272,256]{1,0:T(8,128)(2,1)S(1)} %collective-permute-done.2.ghost, bf16[1024,256]{1,0:T(8,128)(2,1)S(1)} %get-tuple-element.36.scaled), custom_call_target="tpu_custom_call" | custom-call | tf_op jit(solution)/shard_map/pallas_call | solution.py:276
  54.5 0.5 shard_map.152.turned
  55.0 0.1 shard_map.156
  55.1 6.5 %collective-permute-start.5 = (bf16[128,256]{1,0:T(8,128)(2,1)S(1)}, bf16[128,256]{1,0:T(8,128)(2,1)S(1)}, u32[]{:S(2)}, u32[]{:S(2)}) collective-permute-start(bf16[128,256]{1,0:T(8,128)(2,1)S(1)} %get-tuple-element.46), channel_id=1, source_target_pairs={{8,24},{16,0},{24,40},{32,16},{40,56},{48,32},{56,72},{64,48},{72,... | collective-permute-start | bytes 196616 | tf_op jit(solution)/shard_map/ppermute | solution.py:323
  61.6 0.0 copy-start
  61.6 0.0 copy-start.1
  61.6 0.0 copy-start.3
  61.6 0.0 copy-start.4
  61.6 1.5 %shard_map.157.local = f32[1280,256]{1,0:T(8,128)S(1)} custom-call(bf16[1280,2048]{1,0:T(8,128)(2,1)S(1)} %get-tuple-element.47.place, bf16[2048,256]{1,0:T(8,128)(2,1)S(1)} %shard_map.155.terms), custom_call_target="tpu_custom_call" | custom-call | tf_op jit(solution)/shard_map/pallas_call | solution.py:276
  63.2 7.9 %all-gather.2 = bf16[512,256]{1,0:T(8,128)(2,1)S(1)} all-gather(bf16[256,256]{1,0:T(8,128)(2,1)S(1)} %get-tuple-element.45.pair), channel_id=4, replica_groups={{8,16},{9,17},{10,18},{11,19},{12,20},{13,21},{14,22},{15,23},{24,32},{..., dimensions={0}, use_global_device_ids=true | all-gather | bytes 393216 | tf_op jit(solution)/shard_map/all_gather | solution.py:311
  71.1 0.0 collective-permute-done.5.far
  71.1 1.8 %shard_map.158 = (bf16[256,256]{1,0:T(8,128)(2,1)S(1)}, f32[1024,256]{1,0:T(8,128)S(1)}, bf16[256,256]{1,0:T(8,128)(2,1)}, bf16[2,256,256]{2,1,0:T(8,128)(2,1)S(1)}) custom-call(bf16[1280,640]{1,0:T(8,128)(2,1)S(1)} %shard_map.152.turned, bf16[256,256]{1,0:T(8,128)(2,1)S(1)} %get-tuple-element.45.pair, bf16[2,256,256]{2,1,0:T(8,128)(2,1)S(1)} %bitcast.11, ...), custom_call_target="tpu_custom_call" | custom-call | tf_op jit(solution)/shard_map/pallas_call | solution.py:276
  73.0 2.2 %collective-permute-start.6 = (bf16[256,256]{1,0:T(8,128)(2,1)S(1)}, bf16[256,256]{1,0:T(8,128)(2,1)S(1)}, u32[]{:S(2)}, u32[]{:S(2)}) collective-permute-start(bf16[256,256]{1,0:T(8,128)(2,1)S(1)} %get-tuple-element.66), channel_id=1, source_target_pairs={{8,16},{16,8},{24,32},{32,24},{40,48},{48,40},{56,64},{64,56},{72,... | collective-permute-start | bytes 393224 | tf_op jit(solution)/shard_map/ppermute | solution.py:317
  75.2 5.6 %all_gather.39.inner = bf16[2,256,256]{2,1,0:T(8,128)(2,1)S(1)} all-gather(bf16[1,256,256]{2,1,0:T(8,128)(2,1)S(1)} %get-tuple-element.67), channel_id=1, replica_groups={{0,8},{16,24},{32,40},{48,56},{64,72},{80,88},{96,104},{112,120},{128,1..., dimensions={0}, use_global_device_ids=true | all-gather | bytes 393216 | tf_op jit(solution)/shard_map/all_gather | solution.py:304
  80.8 1.1 collective-permute-done.6.outer
  81.9 1.5 %shard_map.159 = (bf16[1024,256]{1,0:T(8,128)(2,1)}, bf16[1024,256]{1,0:T(8,128)(2,1)S(1)}, bf16[256,256]{1,0:T(8,128)(2,1)S(1)}, bf16[128,256]{1,0:T(8,128)(2,1...) custom-call(f32[1024,256]{1,0:T(8,128)S(1)} %get-tuple-element.49.own, ...), custom_call_target="tpu_custom_call" | custom-call | tf_op jit(solution)/shard_map/pallas_call | solution.py:276
  83.4 1.9 %collective-permute-start.7 = (bf16[128,256]{1,0:T(8,128)(2,1)S(1)}, bf16[128,256]{1,0:T(8,128)(2,1)S(1)}, u32[]{:S(2)}, u32[]{:S(2)}) collective-permute-start(bf16[128,256]{1,0:T(8,128)(2,1)S(1)} %get-tuple-element.55), channel_id=1, source_target_pairs={{0,16},{16,32},{24,8},{32,48},{40,24},{48,64},{56,40},{64,80},{72,... | collective-permute-start | bytes 196616 | tf_op jit(solution)/shard_map/ppermute | solution.py:323
  85.3 8.4 %all-gather.3 = bf16[512,256]{1,0:T(8,128)(2,1)S(1)} all-gather(bf16[256,256]{1,0:T(8,128)(2,1)S(1)} %get-tuple-element.54), channel_id=5, replica_groups={{8,16},{9,17},{10,18},{11,19},{12,20},{13,21},{14,22},{15,23},{24,32},{..., dimensions={0}, use_global_device_ids=true | all-gather | bytes 393216 | tf_op jit(solution)/shard_map/all_gather | solution.py:311
  93.8 0.0 collective-permute-done.7.far
  93.8 0.1 shard_map.160
  93.9 3.3 %collective-permute-start.8 = (bf16[272,256]{1,0:T(8,128)(2,1)S(1)}, bf16[272,256]{1,0:T(8,128)(2,1)S(1)}, u32[]{:S(2)}, u32[]{:S(2)}) collective-permute-start(bf16[272,256]{1,0:T(8,128)(2,1)S(1)} %get-tuple-element.57), channel_id=1, source_target_pairs={{0,8},{8,0},{16,24},{24,16},{32,40},{40,32},{48,56},{56,48},{64,72... | collective-permute-start | bytes 417800 | tf_op jit(solution)/shard_map/ppermute | solution.py:327
  97.2 4.1 %shard_map.161.terms = bf16[2048,256]{1,0:T(8,128)(2,1)S(1)} custom-call(bf16[2048,1280]{1,0:T(8,128)(2,1)S(1)} %get-tuple-element.34.pick, bf16[4,512,512]{2,1,0:T(8,128)(2,1)S(1)} %shard_map.154.operator, bf16[256,256]{1,0:T(8,128)(2,1)S(1)} %get-tuple-element.58.ghost, bf16[1024,256]{1,0:T(8,128)(2,1)S(1)} %get-tuple-element.59.scaled), custom_call_target="tpu_custom_call" | custom-call | tf_op jit(solution)/shard_map/pallas_call | solution.py:276
  101.3 1.5 %shard_map.163.local = f32[1280,256]{1,0:T(8,128)S(1)} custom-call(bf16[1280,2048]{1,0:T(8,128)(2,1)S(1)} %get-tuple-element.47.place, bf16[2048,256]{1,0:T(8,128)(2,1)S(1)} %shard_map.161.terms), custom_call_target="tpu_custom_call" | custom-call | tf_op jit(solution)/shard_map/pallas_call | solution.py:276
  102.8 0.1 shard_map.162
  103.0 4.7 %collective-permute-start.9 = (bf16[128,256]{1,0:T(8,128)(2,1)S(1)}, bf16[128,256]{1,0:T(8,128)(2,1)S(1)}, u32[]{:S(2)}, u32[]{:S(2)}) collective-permute-start(bf16[128,256]{1,0:T(8,128)(2,1)S(1)} %get-tuple-element.62), channel_id=1, source_target_pairs={{8,24},{16,0},{24,40},{32,16},{40,56},{48,32},{56,72},{64,48},{72,... | collective-permute-start | bytes 196616 | tf_op jit(solution)/shard_map/ppermute | solution.py:323
  107.7 7.7 %all-gather.4 = bf16[512,256]{1,0:T(8,128)(2,1)S(1)} all-gather(bf16[256,256]{1,0:T(8,128)(2,1)S(1)} %get-tuple-element.61.pair), channel_id=6, replica_groups={{8,16},{9,17},{10,18},{11,19},{12,20},{13,21},{14,22},{15,23},{24,32},{..., dimensions={0}, use_global_device_ids=true | all-gather | bytes 393216 | tf_op jit(solution)/shard_map/all_gather | solution.py:311
  115.5 0.7 shard_map.164
  116.2 3.5 %collective-permute-start.10 = (bf16[256,256]{1,0:T(8,128)(2,1)S(1)}, bf16[256,256]{1,0:T(8,128)(2,1)S(1)}, u32[]{:S(2)}, u32[]{:S(2)}) collective-permute-start(bf16[256,256]{1,0:T(8,128)(2,1)S(1)} %get-tuple-element.65), channel_id=1, source_target_pairs={{8,0},{16,8},{24,16},{32,24},{40,32},{48,40},{56,48},{64,56},{72,6... | collective-permute-start | bytes 393224 | tf_op jit(solution)/shard_map/ppermute | solution.py:25
  119.7 3.3 %collective-permute-done.10.received = bf16[256,256]{1,0:T(8,128)(2,1)S(1)} collective-permute-done((bf16[256,256]{1,0:T(8,128)(2,1)S(1)}, bf16[256,256]{1,0:T(8,128)(2,1)S(1)}, u32[]{:S(2)}, u32[]{:S(2)}) %collective-permute-start.10) | collective-permute-done | bytes 131104 | tf_op jit(solution)/shard_map/ppermute | solution.py:25
  123.0 1.2 %shard_map.165 = bf16[1024,256]{1,0:T(8,128)(2,1)} custom-call(f32[1024,256]{1,0:T(8,128)S(1)} %get-tuple-element.64.own, bf16[256,256]{1,0:T(8,128)(2,1)S(1)} %collective-permute-done.10.received, bf16[1024,256]{1,0:T(8,128)(2,1)S(1)} %copy-done, bf16[1024,256]{1,0:T(8,128)(2,1)S(1)} %copy-done.2, f32[1,1024]{1,0:T(1,128)S(1)} %bitcast.18, ...), custom_call_target="tpu_custom_call" | custom-call | tf_op jit(solution)/shard_map/pallas_call | solution.py:276
  (16 shorter events, 0.1 us)
Async XLA Ops:
  0.6 28.2 %copy-start.6 = (s32[4,8]{1,0:T(4,128)S(1)}, s32[4,8]{1,0:T(4,128)}, u32[]{:S(2)}) copy-start(s32[4,8]{1,0:T(4,128)} %slot.1) | copy-start | bytes 388
  0.6 28.2 %copy-start.5 = (s32[4,8]{1,0:T(4,128)S(1)}, s32[4,8]{1,0:T(4,128)}, u32[]{:S(2)}) copy-start(s32[4,8]{1,0:T(4,128)} %owner.1) | copy-start | bytes 388
  0.6 6.5 %collective-permute-start = (bf16[4,64,128]{2,1,0:T(8,128)(2,1)}, bf16[4,64,128]{2,1,0:T(8,128)(2,1)S(1)}, u32[]{:S(2)}, u32[]{:S(2)}) collective-permute-start(bf16[4,64,128]{2,1,0:T(8,128)(2,1)} %param.23), channel_id=1, source_target_pairs={{0,2},{1,3},{2,0},{3,1},{4,6},{5,7},{6,4},{7,5},{8,10},{9,11},{10,... | collective-permute-start | bytes 196616 | tf_op jit(solution)/shard_map/ppermute | solution.py:327
  8.0 14.9 %collective-permute-start.1 = (bf16[2,4,64,128]{3,2,1,0:T(8,128)(2,1)S(1)}, bf16[2,4,64,128]{3,2,1,0:T(8,128)(2,1)S(1)}, u32[]{:S(2)}, u32[]{:S(2)}) collective-permute-start(bf16[2,4,64,128]{3,2,1,0:T(8,128)(2,1)S(1)} %pad_maximum_fusion.1), channel_id=1, source_target_pairs={{0,6},{1,7},{2,4},{3,5},{4,2},{5,3},{6,0},{7,1},{8,14},{9,15},{10,... | collective-permute-start | bytes 393224 | tf_op jit(solution)/shard_map/ppermute | solution.py:327
  14.3 14.6 %collective-permute-start.2 = (bf16[272,256]{1,0:T(8,128)(2,1)S(1)}, bf16[272,256]{1,0:T(8,128)(2,1)S(1)}, u32[]{:S(2)}, u32[]{:S(2)}) collective-permute-start(bf16[272,256]{1,0:T(8,128)(2,1)S(1)} %get-tuple-element.35), channel_id=1, source_target_pairs={{0,8},{8,16},{16,24},{24,32},{32,40},{40,48},{48,56},{56,64},{64,7... | collective-permute-start | bytes 417800 | tf_op jit(solution)/shard_map/ppermute | solution.py:25
  28.9 18.8 %copy-start.7 = (f32[4]{0:T(128)S(1)}, f32[4]{0:T(128)}, u32[]{:S(2)}) copy-start(f32[4]{0:T(128)} %scale.1) | copy-start | bytes 52
  31.5 13.5 %collective-permute-start.3 = (bf16[128,256]{1,0:T(8,128)(2,1)S(1)}, bf16[128,256]{1,0:T(8,128)(2,1)S(1)}, u32[]{:S(2)}, u32[]{:S(2)}) collective-permute-start(bf16[128,256]{1,0:T(8,128)(2,1)S(1)} %get-tuple-element.40), channel_id=1, source_target_pairs={{0,16},{16,32},{24,8},{32,48},{40,24},{48,64},{56,40},{64,80},{72,... | collective-permute-start | bytes 196616 | tf_op jit(solution)/shard_map/ppermute | solution.py:323
  45.1 9.9 %collective-permute-start.4 = (bf16[272,256]{1,0:T(8,128)(2,1)S(1)}, bf16[272,256]{1,0:T(8,128)(2,1)S(1)}, u32[]{:S(2)}, u32[]{:S(2)}) collective-permute-start(bf16[272,256]{1,0:T(8,128)(2,1)S(1)} %get-tuple-element.43), channel_id=1, source_target_pairs={{0,8},{8,0},{16,24},{24,16},{32,40},{40,32},{48,56},{56,48},{64,72... | collective-permute-start | bytes 417800 | tf_op jit(solution)/shard_map/ppermute | solution.py:327
  55.1 16.0 %collective-permute-start.5 = (bf16[128,256]{1,0:T(8,128)(2,1)S(1)}, bf16[128,256]{1,0:T(8,128)(2,1)S(1)}, u32[]{:S(2)}, u32[]{:S(2)}) collective-permute-start(bf16[128,256]{1,0:T(8,128)(2,1)S(1)} %get-tuple-element.46), channel_id=1, source_target_pairs={{8,24},{16,0},{24,40},{32,16},{40,56},{48,32},{56,72},{64,48},{72,... | collective-permute-start | bytes 196616 | tf_op jit(solution)/shard_map/ppermute | solution.py:323
  61.6 9.5 %copy-start = (bf16[1024,256]{1,0:T(8,128)(2,1)S(1)}, bf16[1024,256]{1,0:T(8,128)(2,1)}, u32[]{:S(2)}) copy-start(bf16[1024,256]{1,0:T(8,128)(2,1)} %state.7) | copy-start | bytes 1572868
  61.6 9.5 %copy-start.1 = (bf16[1024,256]{1,0:T(8,128)(2,1)S(1)}, bf16[1024,256]{1,0:T(8,128)(2,1)}, u32[]{:S(2)}) copy-start(bf16[1024,256]{1,0:T(8,128)(2,1)} %prev.3) | copy-start | bytes 1572868
  61.6 9.5 %copy-start.3 = (f32[1024]{0:T(1024)S(1)}, f32[1024]{0:T(1024)}, u32[]{:S(2)}) copy-start(f32[1024]{0:T(1024)} %param.16) | copy-start | bytes 12292
  61.6 9.5 %copy-start.4 = (s32[1,256]{1,0:T(1,128)S(1)}, s32[1,256]{1,0:T(1,128)}, u32[]{:S(2)}) copy-start(s32[1,256]{1,0:T(1,128)} %send.7) | copy-start | bytes 3076
  73.0 9.0 %collective-permute-start.6 = (bf16[256,256]{1,0:T(8,128)(2,1)S(1)}, bf16[256,256]{1,0:T(8,128)(2,1)S(1)}, u32[]{:S(2)}, u32[]{:S(2)}) collective-permute-start(bf16[256,256]{1,0:T(8,128)(2,1)S(1)} %get-tuple-element.66), channel_id=1, source_target_pairs={{8,16},{16,8},{24,32},{32,24},{40,48},{48,40},{56,64},{64,56},{72,... | collective-permute-start | bytes 393224 | tf_op jit(solution)/shard_map/ppermute | solution.py:317
  83.4 10.4 %collective-permute-start.7 = (bf16[128,256]{1,0:T(8,128)(2,1)S(1)}, bf16[128,256]{1,0:T(8,128)(2,1)S(1)}, u32[]{:S(2)}, u32[]{:S(2)}) collective-permute-start(bf16[128,256]{1,0:T(8,128)(2,1)S(1)} %get-tuple-element.55), channel_id=1, source_target_pairs={{0,16},{16,32},{24,8},{32,48},{40,24},{48,64},{56,40},{64,80},{72,... | collective-permute-start | bytes 196616 | tf_op jit(solution)/shard_map/ppermute | solution.py:323
  93.9 7.4 %collective-permute-start.8 = (bf16[272,256]{1,0:T(8,128)(2,1)S(1)}, bf16[272,256]{1,0:T(8,128)(2,1)S(1)}, u32[]{:S(2)}, u32[]{:S(2)}) collective-permute-start(bf16[272,256]{1,0:T(8,128)(2,1)S(1)} %get-tuple-element.57), channel_id=1, source_target_pairs={{0,8},{8,0},{16,24},{24,16},{32,40},{40,32},{48,56},{56,48},{64,72... | collective-permute-start | bytes 417800 | tf_op jit(solution)/shard_map/ppermute | solution.py:327
  103.0 12.5 %collective-permute-start.9 = (bf16[128,256]{1,0:T(8,128)(2,1)S(1)}, bf16[128,256]{1,0:T(8,128)(2,1)S(1)}, u32[]{:S(2)}, u32[]{:S(2)}) collective-permute-start(bf16[128,256]{1,0:T(8,128)(2,1)S(1)} %get-tuple-element.62), channel_id=1, source_target_pairs={{8,24},{16,0},{24,40},{32,16},{40,56},{48,32},{56,72},{64,48},{72,... | collective-permute-start | bytes 196616 | tf_op jit(solution)/shard_map/ppermute | solution.py:323
  115.5 7.6 %copy-start.2 = (bf16[1024,256]{1,0:T(8,128)(2,1)S(1)}, bf16[1024,256]{1,0:T(8,128)(2,1)}, u32[]{:S(2)}) copy-start(bf16[1024,256]{1,0:T(8,128)(2,1)} %get-tuple-element.32.first) | copy-start | bytes 1572868
  116.2 6.9 %collective-permute-start.10 = (bf16[256,256]{1,0:T(8,128)(2,1)S(1)}, bf16[256,256]{1,0:T(8,128)(2,1)S(1)}, u32[]{:S(2)}, u32[]{:S(2)}) collective-permute-start(bf16[256,256]{1,0:T(8,128)(2,1)S(1)} %get-tuple-element.65), channel_id=1, source_target_pairs={{8,0},{16,8},{24,16},{32,24},{40,32},{48,40},{56,48},{64,56},{72,6... | collective-permute-start | bytes 393224 | tf_op jit(solution)/shard_map/ppermute | solution.py:25
where the time goes:
time: 125 us; the launch traced here: 124 us
  blocking collectives  43.1 us (34%)
  starting transfers between devices  39.1 us (31%)
  Pallas kernels  28.4 us (23%)
  waiting for transfers between devices  10.3 us (8%)
  other arithmetic  1.72 us (1%)
  between operations  1.58 us (1%)
    all_gather x4, blocking collectives, outer_pairs(): lax.all_gather(block, ('mesh', 'band'), axis=0, axis_index_groups=groups)  35.2 us
    pallas_call x17, Pallas kernels, call(): pl.pallas_call(kernel, out_shape=[kept[0](*kept[1:]) if kept else jax.Sha...  28.4 us
    ppermute x4, starting transfers between devices, two_away(): return lax.ppermute(block, 'mesh', [(i, j) for i, j in route if 0 <= j < n])  15.4 us
    ppermute x4, starting transfers between devices, swap(): lax.ppermute(block, axis, [(i, i ^ mask) for i in range(lax.axis_size(axi...  14.1 us
    ppermute x2, starting transfers between devices, from_behind(): return lax.ppermute(block, axis, route)  7.37 us
    ppermute x2, waiting for transfers between devices, from_behind(): return lax.ppermute(block, axis, route)  6.17 us
    all_gather x1, blocking collectives, inner_pairs(): return lax.all_gather(block, 'mesh', axis=0, axis_index_groups=groups)  5.64 us
    ppermute x4, waiting for transfers between devices, swap(): lax.ppermute(block, axis, [(i, i ^ mask) for i in range(lax.axis_size(axi...  2.97 us
  transfers between devices with their start and end apart: 11, of which 4 were waited for; matrix products, arithmetic and copies ran while one was open for 1% of the time, Pallas kernels for 15%

commit v1 on v0

--- a/solution.py
+++ b/solution.py
@@ -90,13 +90,18 @@
     ).astype(BF16)
 
 
-def hot_kernel(nodes, pick, place):
+def pick_kernel(nodes, pick):
     cells, per_cell = nodes.shape
-    extended = place.shape[0]
     for c in range(cells):
         row = nodes[c : c + 1, :]
-        pick[c * per_cell : (c + 1) * per_cell, :] = hot_rows(row, extended)
-        place[:, c * per_cell : (c + 1) * per_cell] = hot_columns(row, extended)
+        pick[c * per_cell : (c + 1) * per_cell, :] = hot_rows(row, pick.shape[1])
+
+
+def place_kernel(nodes, place):
+    cells, per_cell = nodes.shape
+    for c in range(cells):
+        row = nodes[c : c + 1, :]
+        place[:, c * per_cell : (c + 1) * per_cell] = hot_columns(row, place.shape[0])
 
 
 def operator_kernel(potential, stiffness, shape_values, live, scale, operator):
@@ -152,28 +157,25 @@
     turned[...] = jnp.transpose(table[...])
 
 
-def gather_kernel(pick, operator, ghost, scaled, terms, field):
+def gather_kernel(pick, operator, ghost, scaled, terms, field, held):
     face = scaled.shape[0] // 4
     cells, per_cell = operator.shape[0], operator.shape[1]
     field[0:face, :] = ghost[0:face, :]
     field[face:, :] = scaled[...]
+    held[...] = dot(pick[...], field[...]).astype(BF16)
     for c in range(cells):
         rows = slice(c * per_cell, (c + 1) * per_cell)
-        cell = dot(pick[rows, :], field[...]).astype(BF16)
-        terms[rows, :] = dot(operator[c], cell).astype(BF16)
+        terms[rows, :] = dot(operator[c], held[rows, :]).astype(BF16)
 
 
 def scatter_kernel(place, terms, out):
     out[...] = dot(place[...], terms[...])
 
 
-def join_kernel(base, both, far, strengths, mine, message):
+def join_kernel(base, near, far, strengths, mine, message):
     n = far.shape[0]
     left = is_left()
-    here = lax.axis_index("mesh")
-    inside = jnp.logical_and(here > 0, here < lax.axis_size("mesh") - 1)
-    inward = jnp.where(left, both[0], both[1]).astype(F32)
-    total = base[...] + jnp.where(inside, inward, 0.0)
+    total = base[...] + near[...].astype(F32)
     added = far[...].astype(F32)
     mine[0:n, :] = total[0:n, :] + jnp.where(left, added, 0.0)
     mine[n:, :] = total[n:, :] + jnp.where(left, 0.0, added)
@@ -181,47 +183,47 @@
     message[2 * n :, :] = strengths[...]
 
 
-def couple_kernel(mine, message, strengths, pair, sent):
+def couple_kernel(mine, both, strengths, pair, sent):
     n = sent.shape[0]
 
-    def tall(rows):
-        split = rows[...].astype(F32)
+    def tall(split):
+        split = split.astype(F32)
         return column(split[0:1, 0:n] + split[1:2, 0:n] + split[2:3, 0:n])
 
-    own, other = tall(strengths), tall(message.at[2 * n : 2 * n + 16, :])
+    message = jnp.where(is_left(), both[1], both[0]).astype(F32)
+    own, other = tall(strengths[...]), tall(message[2 * n :, :])
     left = is_left()
     for i in range(2):
         at = slice(i * n, (i + 1) * n)
-        total = mine[at, :] + message[at, :].astype(F32)
+        total = mine[at, :] + message[at, :]
         factor = jnp.where(left, own, other) if i == 0 else jnp.where(left, other, own)
         pair[at, :] = (widen(factor, total.shape[1]) * total).astype(BF16)
     sent[...] = jnp.where(left, pair[0:n, :], pair[n:, :])
 
 
-def window_values(pair, both, far):
+def window_values(pair, beside, far):
     left = is_left()
     n = far.shape[0]
-    beside = jnp.where(left, both[0], both[1])
     return jnp.concatenate(
         [
-            jnp.where(left, beside[0:n], far[...]),
-            jnp.where(left, beside[n:], pair[0:n, :]),
+            jnp.where(left, beside[0:n, :], far[...]),
+            jnp.where(left, beside[n:, :], pair[0:n, :]),
             jnp.where(left, pair[0:n, :], pair[n:, :]),
-            jnp.where(left, pair[n:, :], beside[0:n]),
-            jnp.where(left, far[...], beside[n:]),
+            jnp.where(left, pair[n:, :], beside[0:n, :]),
+            jnp.where(left, far[...], beside[n:, :]),
         ]
     )
 
 
-def apply_out(turned, pair, both, far, local):
-    return local[...] + dot(turned[...], window_values(pair, both, far))
+def apply_out(turned, pair, near, far, local):
+    return local[...] + dot(turned[...], window_values(pair, near, far))
 
 
 def middle_kernel(
-    turned, pair, both, far, local, state, prev, mass, send, returned, own, edge, message
+    turned, pair, near, far, local, state, prev, mass, send, returned, own, edge, message
 ):
     face = send.shape[1]
-    total = apply_out(turned, pair, both, far, local)
+    total = apply_out(turned, pair, near, far, local)
     returned[...] = total[0:face, :].astype(BF16)
     own[...] = total[face:, :]
     m = widen(column(mass[...]), state.shape[1])
@@ -258,9 +260,9 @@
     store_sums(table, field, sent, outward, base)
 
 
-def end_kernel(turned, pair, both, far, local, returned, own):
+def end_kernel(turned, pair, near, far, local, returned, own):
     face = returned.shape[0]
-    total = apply_out(turned, pair, both, far, local)
+    total = apply_out(turned, pair, near, far, local)
     returned[...] = total[0:face, :].astype(BF16)
     own[...] = total[face:, :]
 
@@ -302,13 +304,6 @@
     n = lax.axis_size("mesh")
     groups = [[i, i + 1] for i in range(0, n, 2)]
     return lax.all_gather(block, "mesh", axis=0, axis_index_groups=groups)
-
-
-def outer_pairs(block):
-    n, m = lax.axis_size("mesh"), lax.axis_size("band")
-    groups = [[i * m + k, (i + 1) * m + k] for i in range(1, n - 1, 2) for k in range(m)]
-    groups += [[i * m + k, i * m + k + 1] for i in (0, n - 1) for k in range(0, m, 2)]
-    return lax.all_gather(block, ("mesh", "band"), axis=0, axis_index_groups=groups)
 
 
 def outer_swap(block):
@@ -364,12 +359,8 @@
     )
     ghost = from_behind(outgoing, "mesh", 1)
 
-    pick, place = call(
-        hot_kernel,
-        [kept((cells * per_cell, extended), BF16), kept((extended, cells * per_cell), BF16)],
-        (leave(cell_nodes),),
-    )
-    pick, place = hold(pick), hold(place)
+    (pick,) = call(pick_kernel, [kept((cells * per_cell, extended), BF16)], (leave(cell_nodes),))
+    pick = hold(pick)
     near = jnp.stack([cell_proj, other])
     far = swap(near, "band", 6)
     (operator,) = call(
@@ -401,33 +392,38 @@
     table = hold(table)
     (turned,) = call(turn_kernel, [kept((extended, window), BF16)], (table,))
     turned = hold(turned)
+    (place,) = call(place_kernel, [kept((extended, cells * per_cell), BF16)], (cell_nodes,))
+    place = hold(place)
 
     def atom_values(sums, terms):
         sent, outward, base = sums
         far = two_away(sent, 1)
-        both = outer_pairs(outward)
+        near = outer_swap(outward)
         mine, message = call(
             join_kernel,
             [((2 * block, orbitals), F32), ((2 * block + 16, orbitals), BF16)],
-            (base, both, far, strengths),
+            (base, near, far, strengths),
         )
-        message, terms = lax.optimization_barrier((swap(message, "mesh", 1), terms))
+        both = inner_pairs(message)
         pair, sent = call(
             couple_kernel,
             [((2 * block, orbitals), BF16), ((block, orbitals), BF16)],
-            (mine, message, strengths),
+            (mine, both, strengths),
         )
         far = two_away(sent, -1)
-        both = outer_pairs(pair)
+        near = outer_swap(pair)
         (local,) = call(scatter_kernel, [((extended, orbitals), F32)], (place, terms))
-        return (pair, both, far), local
+        return (pair, near, far), local
 
     def cell_terms(ghost, scaled):
         (terms,) = call(
             gather_kernel,
             [((cells * per_cell, orbitals), BF16)],
             (pick, operator, ghost, scaled),
-            scratch=[pltpu.VMEM((extended, orbitals), BF16)],
+            scratch=[
+                pltpu.VMEM((extended, orbitals), BF16),
+                pltpu.VMEM((cells * per_cell, orbitals), BF16),
+            ],
         )
         return terms
 

time: 125 us -> 120 us (0.960)
  blocking collectives: 43.1 us -> 19.4 us
  waiting for transfers between devices: 10.3 us -> 28.1 us
  starting transfers between devices: 39.1 us -> 43.5 us
  Pallas kernels: 28.4 us -> 24.6 us
    all_gather x4 -> x0, blocking collectives: 35.2 us -> none  [outer_pairs(): lax.all_gather(block, ('mesh', 'band'), axis=0, axis_index_groups=groups)]
    ppermute x1 -> x5, starting transfers between devices: 2.19 us -> 19.2 us  [outer_swap(): return lax.ppermute(block, 'mesh', route)]
    ppermute x4, waiting for transfers between devices: 0.01 us -> 16.1 us  [two_away(): return lax.ppermute(block, 'mesh', [(i, j) for i, j in route if 0 <= j < n])]
    all_gather x1 -> x3, blocking collectives: 5.64 us -> 17.3 us  [inner_pairs(): return lax.all_gather(block, 'mesh', axis=0, axis_index_groups=groups)]
    ppermute x4, starting transfers between devices: 15.4 us -> 8.47 us  [two_away(): return lax.ppermute(block, 'mesh', [(i, j) for i, j in route if 0 <= j < n])]
    ppermute x4 -> x2, starting transfers between devices: 14.1 us -> 8.07 us  [swap(): lax.ppermute(block, axis, [(i, i ^ mask) for i in range(lax.axis_size(axi...]
    pallas_call x17 -> x18, Pallas kernels: 28.4 us -> 24.6 us  [call(): pl.pallas_call(kernel, out_shape=[kept[0](*kept[1:]) if kept else jax.Sha...]
    ppermute x2, waiting for transfers between devices: 6.17 us -> 9.05 us  [from_behind(): return lax.ppermute(block, axis, route)]
  transfers between devices with their start and end apart: 11 -> 13, of which waited for: 4 -> 6; matrix products, arithmetic and copies ran while one was open for 1% -> 0% of each run, Pallas kernels for 15% -> 14%
where the time goes in v1:
time: 120 us; the launch traced here: 119 us
  starting transfers between devices  43.5 us (36%)
  waiting for transfers between devices  28.1 us (23%)
  Pallas kernels  24.6 us (20%)
  blocking collectives  19.4 us (16%)
  between operations  1.63 us (1%)
    pallas_call x18, Pallas kernels, call(): pl.pallas_call(kernel, out_shape=[kept[0](*kept[1:]) if kept else jax.Sha...  24.6 us
    ppermute x5, starting transfers between devices, outer_swap(): return lax.ppermute(block, 'mesh', route)  19.2 us
    all_gather x3, blocking collectives, inner_pairs(): return lax.all_gather(block, 'mesh', axis=0, axis_index_groups=groups)  17.3 us
    ppermute x4, waiting for transfers between devices, two_away(): return lax.ppermute(block, 'mesh', [(i, j) for i, j in route if 0 <= j < n])  16.1 us
    ppermute x2, waiting for transfers between devices, from_behind(): return lax.ppermute(block, axis, route)  9.05 us
    ppermute x4, starting transfers between devices, two_away(): return lax.ppermute(block, 'mesh', [(i, j) for i, j in route if 0 <= j < n])  8.47 us
    ppermute x2, starting transfers between devices, swap(): lax.ppermute(block, axis, [(i, i ^ mask) for i in range(lax.axis_size(axi...  8.07 us
    ppermute x2, starting transfers between devices, from_behind(): return lax.ppermute(block, axis, route)  7.75 us
  transfers between devices with their start and end apart: 13, of which 6 were waited for; matrix products, arithmetic and copies ran while one was open for 0% of the time, Pallas kernels for 14%

profile of v1, /device:TPU:24, one launch (start us, length us, event | category | flops | bytes accessed | tf_op | source)
XLA Modules:
  0.0 118.9 jit_solution(7563067336502276582)
XLA Ops:
  0.6 3.4 %collective-permute-start = (bf16[4,64,128]{2,1,0:T(8,128)(2,1)}, bf16[4,64,128]{2,1,0:T(8,128)(2,1)S(1)}, u32[]{:S(2)}, u32[]{:S(2)}) collective-permute-start(bf16[4,64,128]{2,1,0:T(8,128)(2,1)} %param.23), channel_id=1, source_target_pairs={{0,2},{1,3},{2,0},{3,1},{4,6},{5,7},{6,4},{7,5},{8,10},{9,11},{10,... | collective-permute-start | bytes 196616 | tf_op jit(solution)/shard_map/ppermute | solution.py:322
  4.0 3.0 %collective-permute-done = bf16[4,64,128]{2,1,0:T(8,128)(2,1)S(1)} collective-permute-done((bf16[4,64,128]{2,1,0:T(8,128)(2,1)}, bf16[4,64,128]{2,1,0:T(8,128)(2,1)S(1)}, u32[]{:S(2)}, u32[]{:S(2)}) %collective-permute-start) | collective-permute-done | bytes 65568 | tf_op jit(solution)/shard_map/ppermute | solution.py:322
  7.0 0.9 pad_maximum_fusion.1
  7.9 4.7 %collective-permute-start.1 = (bf16[2,4,64,128]{3,2,1,0:T(8,128)(2,1)S(1)}, bf16[2,4,64,128]{3,2,1,0:T(8,128)(2,1)S(1)}, u32[]{:S(2)}, u32[]{:S(2)}) collective-permute-start(bf16[2,4,64,128]{3,2,1,0:T(8,128)(2,1)S(1)} %pad_maximum_fusion.1), channel_id=1, source_target_pairs={{0,6},{1,7},{2,4},{3,5},{4,2},{5,3},{6,0},{7,1},{8,14},{9,15},{10,... | collective-permute-start | bytes 393224 | tf_op jit(solution)/shard_map/ppermute | solution.py:322
  12.5 1.6 %shard_map.150 = (bf16[1024,256]{1,0:T(8,128)(2,1)S(1)}, bf16[272,256]{1,0:T(8,128)(2,1)S(1)}, bf16[16,256]{1,0:T(8,128)(2,1)S(1)}) custom-call(bf16[1024,256]{1,0:T(8,128)(2,1)} %state.7, f32[1,1024]{1,0:T(1,128)} %bitcast.11, s32[1,256]{1,0:T(1,128)} %send.7, f32[8,16]{1,0:T(8,128)} %coupling.1), custom_call_target="tpu_custom_call" | custom-call | tf_op jit(solution)/shard_map/pallas_call | solution.py:278
  14.1 3.8 %collective-permute-start.2 = (bf16[272,256]{1,0:T(8,128)(2,1)S(1)}, bf16[272,256]{1,0:T(8,128)(2,1)S(1)}, u32[]{:S(2)}, u32[]{:S(2)}) collective-permute-start(bf16[272,256]{1,0:T(8,128)(2,1)S(1)} %get-tuple-element.28), channel_id=1, source_target_pairs={{0,8},{8,16},{16,24},{24,32},{32,40},{40,48},{48,56},{56,64},{64,7... | collective-permute-start | bytes 417800 | tf_op jit(solution)/shard_map/ppermute | solution.py:25
  18.6 0.0 copy-start.9
  18.6 0.0 copy-start.6
  18.6 1.7 %shard_map.149.pick = bf16[2048,1280]{1,0:T(8,128)(2,1)S(1)} custom-call(s32[4,512]{1,0:T(4,128)} %nodes.3), custom_call_target="tpu_custom_call" | custom-call | tf_op jit(solution)/shard_map/pallas_call | solution.py:278
  20.4 2.2 %all-gather = bf16[8,4,64,128]{3,2,1,0:T(8,128)(2,1)S(1)} all-gather(bf16[4,4,64,128]{3,2,1,0:T(8,128)(2,1)S(1)} %pad_maximum_fusion), channel_id=2, replica_groups={{0,1},{2,3},{4,5},{6,7},{8,9},{10,11},{12,13},{14,15},{16,17},{18,19},{..., dimensions={0}, use_global_device_ids=true | all-gather | bytes 786432 | tf_op jit(solution)/shard_map/all_gather | solution.py:373
  22.6 6.1 %collective-permute-done.2.ghost = bf16[272,256]{1,0:T(8,128)(2,1)S(1)} collective-permute-done((bf16[272,256]{1,0:T(8,128)(2,1)S(1)}, bf16[272,256]{1,0:T(8,128)(2,1)S(1)}, u32[]{:S(2)}, u32[]{:S(2)}) %collective-permute-start.2) | collective-permute-done | bytes 139296 | tf_op jit(solution)/shard_map/ppermute | solution.py:25
  28.7 2.7 %shard_map.151 = (bf16[640,1280]{1,0:T(8,128)(2,1)S(1)}, bf16[128,256]{1,0:T(8,128)(2,1)S(1)}, bf16[256,256]{1,0:T(8,128)(2,1)S(1)}, f32[256,256]{1,0:T(8,128)S(1)}) custom-call(bf16[2,4,4,64,128]{4,3,2,1,0:T(8,128)(2,1)S(1)} %bitcast.8, bf16[2048,1280]{1,0:T(8,128)(2,1)S(1)} %shard_map.149.pick, s32[4,8]{1,0:T(4,128)S(1)} %copy-done.6, ...), custom_call_target="tpu_custom_call" | custom-call | tf_op jit(solution)/shard_map/pallas_call | solution.py:278
  31.4 3.9 %collective-permute-start.3 = (bf16[256,256]{1,0:T(8,128)(2,1)S(1)}, bf16[256,256]{1,0:T(8,128)(2,1)S(1)}, u32[]{:S(2)}, u32[]{:S(2)}) collective-permute-start(bf16[256,256]{1,0:T(8,128)(2,1)S(1)} %get-tuple-element.32), channel_id=1, source_target_pairs={{8,16},{16,8},{24,32},{32,24},{40,48},{48,40},{56,64},{64,56},{72,... | collective-permute-start | bytes 393224 | tf_op jit(solution)/shard_map/ppermute | solution.py:312
  35.4 1.9 %collective-permute-start.4 = (bf16[128,256]{1,0:T(8,128)(2,1)S(1)}, bf16[128,256]{1,0:T(8,128)(2,1)S(1)}, u32[]{:S(2)}, u32[]{:S(2)}) collective-permute-start(bf16[128,256]{1,0:T(8,128)(2,1)S(1)} %get-tuple-element.33), channel_id=1, source_target_pairs={{0,16},{16,32},{24,8},{32,48},{40,24},{48,64},{56,40},{64,80},{72,... | collective-permute-start | bytes 196616 | tf_op jit(solution)/shard_map/ppermute | solution.py:318
  37.3 7.2 %collective-permute-done.4.far = bf16[128,256]{1,0:T(8,128)(2,1)S(1)} collective-permute-done((bf16[128,256]{1,0:T(8,128)(2,1)S(1)}, bf16[128,256]{1,0:T(8,128)(2,1)S(1)}, u32[]{:S(2)}, u32[]{:S(2)}) %collective-permute-start.4) | collective-permute-done | bytes 65568 | tf_op jit(solution)/shard_map/ppermute | solution.py:318
  44.5 0.1 shard_map.153
  44.6 5.7 %all-gather.1 = bf16[544,256]{1,0:T(8,128)(2,1)S(1)} all-gather(bf16[272,256]{1,0:T(8,128)(2,1)S(1)} %get-tuple-element.36), channel_id=3, replica_groups={{0,8},{16,24},{32,40},{48,56},{64,72},{80,88},{96,104},{112,120},{128,1..., dimensions={0}, use_global_device_ids=true | all-gather | bytes 417792 | tf_op jit(solution)/shard_map/all_gather | solution.py:306
  50.3 0.1 shard_map.154
  50.5 4.0 %collective-permute-start.5 = (bf16[256,256]{1,0:T(8,128)(2,1)S(1)}, bf16[256,256]{1,0:T(8,128)(2,1)S(1)}, u32[]{:S(2)}, u32[]{:S(2)}) collective-permute-start(bf16[256,256]{1,0:T(8,128)(2,1)S(1)} %get-tuple-element.37.pair), channel_id=1, source_target_pairs={{8,16},{16,8},{24,32},{32,24},{40,48},{48,40},{56,64},{64,56},{72,... | collective-permute-start | bytes 393224 | tf_op jit(solution)/shard_map/ppermute | solution.py:312
  54.5 2.2 %collective-permute-start.6 = (bf16[128,256]{1,0:T(8,128)(2,1)S(1)}, bf16[128,256]{1,0:T(8,128)(2,1)S(1)}, u32[]{:S(2)}, u32[]{:S(2)}) collective-permute-start(bf16[128,256]{1,0:T(8,128)(2,1)S(1)} %get-tuple-element.38), channel_id=1, source_target_pairs={{8,24},{16,0},{24,40},{32,16},{40,56},{48,32},{56,72},{64,48},{72,... | collective-permute-start | bytes 196616 | tf_op jit(solution)/shard_map/ppermute | solution.py:318
  56.7 1.1 shard_map.155.place
  57.8 2.6 %shard_map.156.operator = bf16[4,512,512]{2,1,0:T(8,128)(2,1)S(1)} custom-call(f32[4,512]{1,0:T(4,128)} %potential.1, bf16[512,512]{1,0:T(8,128)(2,1)} %stiffness.1, bf16[512,512]{1,0:T(8,128)(2,1)} %shape_values.1, s32[1]{0:T(128)S(6)} %copy.16.live, f32[4]{0:T(128)S(1)} %copy-done.8), custom_call_target="tpu_custom_call" | custom-call | tf_op jit(solution)/shard_map/pallas_call | solution.py:278
  60.4 2.8 %shard_map.157.terms = bf16[2048,256]{1,0:T(8,128)(2,1)S(1)} custom-call(bf16[2048,1280]{1,0:T(8,128)(2,1)S(1)} %shard_map.149.pick, bf16[4,512,512]{2,1,0:T(8,128)(2,1)S(1)} %shard_map.156.operator, bf16[272,256]{1,0:T(8,128)(2,1)S(1)} %collective-permute-done.2.ghost, bf16[1024,256]{1,0:T(8,128)(2,1)S(1)} %get-tuple-element.29.scaled), custom_call_target="tpu_custom_call" | custom-call | tf_op jit(solution)/shard_map/pallas_call | solution.py:278
  63.3 1.5 %shard_map.158.local = f32[1280,256]{1,0:T(8,128)S(1)} custom-call(bf16[1280,2048]{1,0:T(8,128)(2,1)S(1)} %shard_map.155.place, bf16[2048,256]{1,0:T(8,128)(2,1)S(1)} %shard_map.157.terms), custom_call_target="tpu_custom_call" | custom-call | tf_op jit(solution)/shard_map/pallas_call | solution.py:278
  64.8 0.0 copy-start
  64.9 0.5 shard_map.152.turned
  65.4 0.5 copy-done
  65.9 0.2 copy-done.1
  66.0 1.8 %shard_map.159 = (bf16[256,256]{1,0:T(8,128)(2,1)S(1)}, f32[1024,256]{1,0:T(8,128)S(1)}, bf16[256,256]{1,0:T(8,128)(2,1)}, bf16[2,256,256]{2,1,0:T(8,128)(2,1)S(1)}) custom-call(bf16[1280,640]{1,0:T(8,128)(2,1)S(1)} %shard_map.152.turned, bf16[256,256]{1,0:T(8,128)(2,1)S(1)} %get-tuple-element.37.pair, bf16[256,256]{1,0:T(8,128)(2,1)S(1)} %collective-permute-done.5.near, ...), custom_call_target="tpu_custom_call" | custom-call | tf_op jit(solution)/shard_map/pallas_call | solution.py:278
  67.9 3.7 %collective-permute-start.7 = (bf16[256,256]{1,0:T(8,128)(2,1)S(1)}, bf16[256,256]{1,0:T(8,128)(2,1)S(1)}, u32[]{:S(2)}, u32[]{:S(2)}) collective-permute-start(bf16[256,256]{1,0:T(8,128)(2,1)S(1)} %get-tuple-element.54), channel_id=1, source_target_pairs={{8,16},{16,8},{24,32},{32,24},{40,48},{48,40},{56,64},{64,56},{72,... | collective-permute-start | bytes 393224 | tf_op jit(solution)/shard_map/ppermute | solution.py:312
  71.5 5.8 %all_gather.25.inner = bf16[2,256,256]{2,1,0:T(8,128)(2,1)S(1)} all-gather(bf16[1,256,256]{2,1,0:T(8,128)(2,1)S(1)} %get-tuple-element.55), channel_id=1, replica_groups={{0,8},{16,24},{32,40},{48,56},{64,72},{80,88},{96,104},{112,120},{128,1..., dimensions={0}, use_global_device_ids=true | all-gather | bytes 393216 | tf_op jit(solution)/shard_map/all_gather | solution.py:306
  77.3 1.5 %shard_map.160 = (bf16[1024,256]{1,0:T(8,128)(2,1)}, bf16[1024,256]{1,0:T(8,128)(2,1)S(1)}, bf16[256,256]{1,0:T(8,128)(2,1)S(1)}, bf16[128,256]{1,0:T(8,128)(2,1...) custom-call(f32[1024,256]{1,0:T(8,128)S(1)} %get-tuple-element.39.own, ...), custom_call_target="tpu_custom_call" | custom-call | tf_op jit(solution)/shard_map/pallas_call | solution.py:278
  78.9 4.3 %collective-permute-start.8 = (bf16[256,256]{1,0:T(8,128)(2,1)S(1)}, bf16[256,256]{1,0:T(8,128)(2,1)S(1)}, u32[]{:S(2)}, u32[]{:S(2)}) collective-permute-start(bf16[256,256]{1,0:T(8,128)(2,1)S(1)} %get-tuple-element.44), channel_id=1, source_target_pairs={{8,16},{16,8},{24,32},{32,24},{40,48},{48,40},{56,64},{64,56},{72,... | collective-permute-start | bytes 393224 | tf_op jit(solution)/shard_map/ppermute | solution.py:312
  83.2 2.4 %collective-permute-start.9 = (bf16[128,256]{1,0:T(8,128)(2,1)S(1)}, bf16[128,256]{1,0:T(8,128)(2,1)S(1)}, u32[]{:S(2)}, u32[]{:S(2)}) collective-permute-start(bf16[128,256]{1,0:T(8,128)(2,1)S(1)} %get-tuple-element.45), channel_id=1, source_target_pairs={{0,16},{16,32},{24,8},{32,48},{40,24},{48,64},{56,40},{64,80},{72,... | collective-permute-start | bytes 196616 | tf_op jit(solution)/shard_map/ppermute | solution.py:318
  85.6 7.4 %collective-permute-done.9.far = bf16[128,256]{1,0:T(8,128)(2,1)S(1)} collective-permute-done((bf16[128,256]{1,0:T(8,128)(2,1)S(1)}, bf16[128,256]{1,0:T(8,128)(2,1)S(1)}, u32[]{:S(2)}, u32[]{:S(2)}) %collective-permute-start.9) | collective-permute-done | bytes 65568 | tf_op jit(solution)/shard_map/ppermute | solution.py:318
  93.0 0.1 shard_map.161
  93.1 5.7 %all-gather.2 = bf16[544,256]{1,0:T(8,128)(2,1)S(1)} all-gather(bf16[272,256]{1,0:T(8,128)(2,1)S(1)} %get-tuple-element.47), channel_id=4, replica_groups={{0,8},{16,24},{32,40},{48,56},{64,72},{80,88},{96,104},{112,120},{128,1..., dimensions={0}, use_global_device_ids=true | all-gather | bytes 417792 | tf_op jit(solution)/shard_map/all_gather | solution.py:306
  98.8 0.1 shard_map.162
  99.0 3.3 %collective-permute-start.10 = (bf16[256,256]{1,0:T(8,128)(2,1)S(1)}, bf16[256,256]{1,0:T(8,128)(2,1)S(1)}, u32[]{:S(2)}, u32[]{:S(2)}) collective-permute-start(bf16[256,256]{1,0:T(8,128)(2,1)S(1)} %get-tuple-element.48.pair), channel_id=1, source_target_pairs={{8,16},{16,8},{24,32},{32,24},{40,48},{48,40},{56,64},{64,56},{72,... | collective-permute-start | bytes 393224 | tf_op jit(solution)/shard_map/ppermute | solution.py:312
  102.3 1.9 %collective-permute-start.11 = (bf16[128,256]{1,0:T(8,128)(2,1)S(1)}, bf16[128,256]{1,0:T(8,128)(2,1)S(1)}, u32[]{:S(2)}, u32[]{:S(2)}) collective-permute-start(bf16[128,256]{1,0:T(8,128)(2,1)S(1)} %get-tuple-element.49), channel_id=1, source_target_pairs={{8,24},{16,0},{24,40},{32,16},{40,56},{48,32},{56,72},{64,48},{72,... | collective-permute-start | bytes 196616 | tf_op jit(solution)/shard_map/ppermute | solution.py:318
  104.2 2.8 %shard_map.163.terms = bf16[2048,256]{1,0:T(8,128)(2,1)S(1)} custom-call(bf16[2048,1280]{1,0:T(8,128)(2,1)S(1)} %shard_map.149.pick, bf16[4,512,512]{2,1,0:T(8,128)(2,1)S(1)} %shard_map.156.operator, bf16[256,256]{1,0:T(8,128)(2,1)S(1)} %get-tuple-element.50.ghost, bf16[1024,256]{1,0:T(8,128)(2,1)S(1)} %get-tuple-element.51.scaled), custom_call_target="tpu_custom_call" | custom-call | tf_op jit(solution)/shard_map/pallas_call | solution.py:278
  107.1 1.6 %shard_map.164.local = f32[1280,256]{1,0:T(8,128)S(1)} custom-call(bf16[1280,2048]{1,0:T(8,128)(2,1)S(1)} %shard_map.155.place, bf16[2048,256]{1,0:T(8,128)(2,1)S(1)} %shard_map.163.terms), custom_call_target="tpu_custom_call" | custom-call | tf_op jit(solution)/shard_map/pallas_call | solution.py:278
  108.6 0.0 copy-start.2
  108.6 1.4 %collective-permute-done.11.far = bf16[128,256]{1,0:T(8,128)(2,1)S(1)} collective-permute-done((bf16[128,256]{1,0:T(8,128)(2,1)S(1)}, bf16[128,256]{1,0:T(8,128)(2,1)S(1)}, u32[]{:S(2)}, u32[]{:S(2)}) %collective-permute-start.11) | collective-permute-done | bytes 65568 | tf_op jit(solution)/shard_map/ppermute | solution.py:318
  110.1 0.7 shard_map.165
  110.8 3.9 %collective-permute-start.12 = (bf16[256,256]{1,0:T(8,128)(2,1)S(1)}, bf16[256,256]{1,0:T(8,128)(2,1)S(1)}, u32[]{:S(2)}, u32[]{:S(2)}) collective-permute-start(bf16[256,256]{1,0:T(8,128)(2,1)S(1)} %get-tuple-element.53), channel_id=1, source_target_pairs={{8,0},{16,8},{24,16},{32,24},{40,32},{48,40},{56,48},{64,56},{72,6... | collective-permute-start | bytes 393224 | tf_op jit(solution)/shard_map/ppermute | solution.py:25
  114.7 2.9 %collective-permute-done.12.received = bf16[256,256]{1,0:T(8,128)(2,1)S(1)} collective-permute-done((bf16[256,256]{1,0:T(8,128)(2,1)S(1)}, bf16[256,256]{1,0:T(8,128)(2,1)S(1)}, u32[]{:S(2)}, u32[]{:S(2)}) %collective-permute-start.12) | collective-permute-done | bytes 131104 | tf_op jit(solution)/shard_map/ppermute | solution.py:25
  117.6 1.3 %shard_map.166 = bf16[1024,256]{1,0:T(8,128)(2,1)} custom-call(f32[1024,256]{1,0:T(8,128)S(1)} %get-tuple-element.52.own, bf16[256,256]{1,0:T(8,128)(2,1)S(1)} %collective-permute-done.12.received, bf16[1024,256]{1,0:T(8,128)(2,1)S(1)} %copy-done, bf16[1024,256]{1,0:T(8,128)(2,1)S(1)} %copy-done.2, f32[1,1024]{1,0:T(1,128)S(1)} %bitcast.14, ...), custom_call_target="tpu_custom_call" | custom-call | tf_op jit(solution)/shard_map/pallas_call | solution.py:278
  (23 shorter events, 0.1 us)
Async XLA Ops:
  0.6 6.4 %collective-permute-start = (bf16[4,64,128]{2,1,0:T(8,128)(2,1)}, bf16[4,64,128]{2,1,0:T(8,128)(2,1)S(1)}, u32[]{:S(2)}, u32[]{:S(2)}) collective-permute-start(bf16[4,64,128]{2,1,0:T(8,128)(2,1)} %param.23), channel_id=1, source_target_pairs={{0,2},{1,3},{2,0},{3,1},{4,6},{5,7},{6,4},{7,5},{8,10},{9,11},{10,... | collective-permute-start | bytes 196616 | tf_op jit(solution)/shard_map/ppermute | solution.py:322
  7.9 12.5 %collective-permute-start.1 = (bf16[2,4,64,128]{3,2,1,0:T(8,128)(2,1)S(1)}, bf16[2,4,64,128]{3,2,1,0:T(8,128)(2,1)S(1)}, u32[]{:S(2)}, u32[]{:S(2)}) collective-permute-start(bf16[2,4,64,128]{3,2,1,0:T(8,128)(2,1)S(1)} %pad_maximum_fusion.1), channel_id=1, source_target_pairs={{0,6},{1,7},{2,4},{3,5},{4,2},{5,3},{6,0},{7,1},{8,14},{9,15},{10,... | collective-permute-start | bytes 393224 | tf_op jit(solution)/shard_map/ppermute | solution.py:322
  14.1 14.6 %collective-permute-start.2 = (bf16[272,256]{1,0:T(8,128)(2,1)S(1)}, bf16[272,256]{1,0:T(8,128)(2,1)S(1)}, u32[]{:S(2)}, u32[]{:S(2)}) collective-permute-start(bf16[272,256]{1,0:T(8,128)(2,1)S(1)} %get-tuple-element.28), channel_id=1, source_target_pairs={{0,8},{8,16},{16,24},{24,32},{32,40},{40,48},{48,56},{56,64},{64,7... | collective-permute-start | bytes 417800 | tf_op jit(solution)/shard_map/ppermute | solution.py:25
  18.6 1.8 %copy-start.9 = (bf16[4,64,128]{2,1,0:T(8,128)(2,1)S(1)}, bf16[4,64,128]{2,1,0:T(8,128)(2,1)}, u32[]{:S(2)}) copy-start(bf16[4,64,128]{2,1,0:T(8,128)(2,1)} %param.23) | copy-start | bytes 196612
  18.6 10.1 %copy-start.6 = (s32[4,8]{1,0:T(4,128)S(1)}, s32[4,8]{1,0:T(4,128)}, u32[]{:S(2)}) copy-start(s32[4,8]{1,0:T(4,128)} %owner.1) | copy-start | bytes 388
  18.6 10.1 %copy-start.7 = (s32[4,8]{1,0:T(4,128)S(1)}, s32[4,8]{1,0:T(4,128)}, u32[]{:S(2)}) copy-start(s32[4,8]{1,0:T(4,128)} %slot.1) | copy-start | bytes 388
  28.7 28.0 %copy-start.4 = (s32[4,512]{1,0:T(4,128)S(1)}, s32[4,512]{1,0:T(4,128)}, u32[]{:S(2)}) copy-start(s32[4,512]{1,0:T(4,128)} %nodes.3) | copy-start | bytes 24580
  31.4 13.1 %collective-permute-start.3 = (bf16[256,256]{1,0:T(8,128)(2,1)S(1)}, bf16[256,256]{1,0:T(8,128)(2,1)S(1)}, u32[]{:S(2)}, u32[]{:S(2)}) collective-permute-start(bf16[256,256]{1,0:T(8,128)(2,1)S(1)} %get-tuple-element.32), channel_id=1, source_target_pairs={{8,16},{16,8},{24,32},{32,24},{40,48},{48,40},{56,64},{64,56},{72,... | collective-permute-start | bytes 393224 | tf_op jit(solution)/shard_map/ppermute | solution.py:312
  35.4 9.2 %collective-permute-start.4 = (bf16[128,256]{1,0:T(8,128)(2,1)S(1)}, bf16[128,256]{1,0:T(8,128)(2,1)S(1)}, u32[]{:S(2)}, u32[]{:S(2)}) collective-permute-start(bf16[128,256]{1,0:T(8,128)(2,1)S(1)} %get-tuple-element.33), channel_id=1, source_target_pairs={{0,16},{16,32},{24,8},{32,48},{40,24},{48,64},{56,40},{64,80},{72,... | collective-permute-start | bytes 196616 | tf_op jit(solution)/shard_map/ppermute | solution.py:318
  50.5 14.9 %collective-permute-start.5 = (bf16[256,256]{1,0:T(8,128)(2,1)S(1)}, bf16[256,256]{1,0:T(8,128)(2,1)S(1)}, u32[]{:S(2)}, u32[]{:S(2)}) collective-permute-start(bf16[256,256]{1,0:T(8,128)(2,1)S(1)} %get-tuple-element.37.pair), channel_id=1, source_target_pairs={{8,16},{16,8},{24,32},{32,24},{40,48},{48,40},{56,64},{64,56},{72,... | collective-permute-start | bytes 393224 | tf_op jit(solution)/shard_map/ppermute | solution.py:312
  54.5 3.3 %copy-start.8 = (f32[4]{0:T(128)S(1)}, f32[4]{0:T(128)}, u32[]{:S(2)}) copy-start(f32[4]{0:T(128)} %scale.1) | copy-start | bytes 52
  54.5 10.8 %collective-permute-start.6 = (bf16[128,256]{1,0:T(8,128)(2,1)S(1)}, bf16[128,256]{1,0:T(8,128)(2,1)S(1)}, u32[]{:S(2)}, u32[]{:S(2)}) collective-permute-start(bf16[128,256]{1,0:T(8,128)(2,1)S(1)} %get-tuple-element.38), channel_id=1, source_target_pairs={{8,24},{16,0},{24,40},{32,16},{40,56},{48,32},{56,72},{64,48},{72,... | collective-permute-start | bytes 196616 | tf_op jit(solution)/shard_map/ppermute | solution.py:318
  64.8 1.0 copy-start
  64.8 1.2 %copy-start.1 = (bf16[1024,256]{1,0:T(8,128)(2,1)S(1)}, bf16[1024,256]{1,0:T(8,128)(2,1)}, u32[]{:S(2)}) copy-start(bf16[1024,256]{1,0:T(8,128)(2,1)} %prev.3) | copy-start | bytes 1572868
  64.8 1.2 copy-start.3
  64.8 1.2 copy-start.5
  67.9 9.5 %collective-permute-start.7 = (bf16[256,256]{1,0:T(8,128)(2,1)S(1)}, bf16[256,256]{1,0:T(8,128)(2,1)S(1)}, u32[]{:S(2)}, u32[]{:S(2)}) collective-permute-start(bf16[256,256]{1,0:T(8,128)(2,1)S(1)} %get-tuple-element.54), channel_id=1, source_target_pairs={{8,16},{16,8},{24,32},{32,24},{40,48},{48,40},{56,64},{64,56},{72,... | collective-permute-start | bytes 393224 | tf_op jit(solution)/shard_map/ppermute | solution.py:312
  78.9 14.2 %collective-permute-start.8 = (bf16[256,256]{1,0:T(8,128)(2,1)S(1)}, bf16[256,256]{1,0:T(8,128)(2,1)S(1)}, u32[]{:S(2)}, u32[]{:S(2)}) collective-permute-start(bf16[256,256]{1,0:T(8,128)(2,1)S(1)} %get-tuple-element.44), channel_id=1, source_target_pairs={{8,16},{16,8},{24,32},{32,24},{40,48},{48,40},{56,64},{64,56},{72,... | collective-permute-start | bytes 393224 | tf_op jit(solution)/shard_map/ppermute | solution.py:312
  83.2 9.9 %collective-permute-start.9 = (bf16[128,256]{1,0:T(8,128)(2,1)S(1)}, bf16[128,256]{1,0:T(8,128)(2,1)S(1)}, u32[]{:S(2)}, u32[]{:S(2)}) collective-permute-start(bf16[128,256]{1,0:T(8,128)(2,1)S(1)} %get-tuple-element.45), channel_id=1, source_target_pairs={{0,16},{16,32},{24,8},{32,48},{40,24},{48,64},{56,40},{64,80},{72,... | collective-permute-start | bytes 196616 | tf_op jit(solution)/shard_map/ppermute | solution.py:318
  99.0 11.1 %collective-permute-start.10 = (bf16[256,256]{1,0:T(8,128)(2,1)S(1)}, bf16[256,256]{1,0:T(8,128)(2,1)S(1)}, u32[]{:S(2)}, u32[]{:S(2)}) collective-permute-start(bf16[256,256]{1,0:T(8,128)(2,1)S(1)} %get-tuple-element.48.pair), channel_id=1, source_target_pairs={{8,16},{16,8},{24,32},{32,24},{40,48},{48,40},{56,64},{64,56},{72,... | collective-permute-start | bytes 393224 | tf_op jit(solution)/shard_map/ppermute | solution.py:312
  102.3 7.8 %collective-permute-start.11 = (bf16[128,256]{1,0:T(8,128)(2,1)S(1)}, bf16[128,256]{1,0:T(8,128)(2,1)S(1)}, u32[]{:S(2)}, u32[]{:S(2)}) collective-permute-start(bf16[128,256]{1,0:T(8,128)(2,1)S(1)} %get-tuple-element.49), channel_id=1, source_target_pairs={{8,24},{16,0},{24,40},{32,16},{40,56},{48,32},{56,72},{64,48},{72,... | collective-permute-start | bytes 196616 | tf_op jit(solution)/shard_map/ppermute | solution.py:318
  108.6 9.0 %copy-start.2 = (bf16[1024,256]{1,0:T(8,128)(2,1)S(1)}, bf16[1024,256]{1,0:T(8,128)(2,1)}, u32[]{:S(2)}) copy-start(bf16[1024,256]{1,0:T(8,128)(2,1)} %get-tuple-element.26.first) | copy-start | bytes 1572868
  110.8 6.9 %collective-permute-start.12 = (bf16[256,256]{1,0:T(8,128)(2,1)S(1)}, bf16[256,256]{1,0:T(8,128)(2,1)S(1)}, u32[]{:S(2)}, u32[]{:S(2)}) collective-permute-start(bf16[256,256]{1,0:T(8,128)(2,1)S(1)} %get-tuple-element.53), channel_id=1, source_target_pairs={{8,0},{16,8},{24,16},{32,24},{40,32},{48,40},{56,48},{64,56},{72,6... | collective-permute-start | bytes 393224 | tf_op jit(solution)/shard_map/ppermute | solution.py:25

commit v2 on v1

--- a/solution.py
+++ b/solution.py
@@ -68,7 +68,10 @@
     return lax.rem(lax.axis_index("mesh"), 2) == 0
 
 
-def start_kernel(state, mass, send, coupling, scaled, outgoing, strengths):
+def start_kernel(
+    state, mass, send, coupling, projectors, scaled, outgoing, strengths, kept_projectors
+):
+    kept_projectors[...] = projectors[...]
     atoms, per_atom = coupling.shape
     width = atoms * per_atom
     spread = jnp.concatenate(
@@ -97,7 +100,9 @@
         pick[c * per_cell : (c + 1) * per_cell, :] = hot_rows(row, pick.shape[1])
 
 
-def place_kernel(nodes, place):
+def place_kernel(nodes, send, place, send_pick, send_place):
+    send_pick[...] = hot_rows(send[...], send_pick.shape[1])
+    send_place[...] = hot_columns(send[...], send_place.shape[0])
     cells, per_cell = nodes.shape
     for c in range(cells):
         row = nodes[c : c + 1, :]
@@ -220,32 +225,32 @@
 
 
 def middle_kernel(
-    turned, pair, near, far, local, state, prev, mass, send, returned, own, edge, message
+    turned, pair, near, far, local, state, prev, mass, send_pick, returned, own, edge, message
 ):
-    face = send.shape[1]
+    face = send_pick.shape[0]
     total = apply_out(turned, pair, near, far, local)
     returned[...] = total[0:face, :].astype(BF16)
     own[...] = total[face:, :]
     m = widen(column(mass[...]), state.shape[1])
     current = state[...].astype(F32)
     partial = filter_scale * (m * own[...] - filter_shift * current) - prev[...].astype(F32)
-    edge[...] = dot(hot_rows(send[...], state.shape[0]), (m * partial).astype(BF16)).astype(BF16)
+    edge[...] = dot(send_pick[...], (m * partial).astype(BF16)).astype(BF16)
     left = is_left()
     message[0] = jnp.where(left, edge[...], returned[...])
     message[1] = jnp.where(left, returned[...], edge[...])
 
 
 def next_kernel(
-    own, inner, outer, returned, ghost, state, prev, mass, send, table,
+    own, inner, outer, returned, ghost, state, prev, mass, send_place, table,
     first, scaled, ghost_next, sent, outward, base, field,
 ):
-    face = send.shape[1]
+    face = send_place.shape[1]
     m = widen(column(mass[...]), state.shape[1])
     left = is_left()
     within = jnp.where(left, inner[1], inner[0])
     received = jnp.where(left, within, outer[...])
     edge = jnp.where(left, outer[...], within)
-    owned = own[...] + dot(hot_columns(send[...], state.shape[0]), received)
+    owned = own[...] + dot(send_place[...], received)
     current = state[...].astype(F32)
     one = filter_scale * (m * owned - filter_shift * current) - prev[...].astype(F32)
     first[...] = one.astype(BF16)
@@ -267,9 +272,9 @@
     own[...] = total[face:, :]
 
 
-def last_kernel(own, received, state, first, mass, send, second):
+def last_kernel(own, received, state, first, mass, send_place, second):
     m = widen(column(mass[...]), state.shape[1])
-    owned = own[...] + dot(hot_columns(send[...], state.shape[0]), received[...])
+    owned = own[...] + dot(send_place[...], received[...])
     two = filter_scale * (m * owned - filter_shift * first[...].astype(F32))
     second[...] = (two - state[...].astype(F32)).astype(BF16)
 
@@ -346,22 +351,23 @@
     block = atoms * per_atom
     window = 5 * block
     mass_row = mass.reshape(1, own_rows)
-    other = swap(cell_proj, "band", 2)
     start = call
-    scaled, outgoing, strengths = start(
+    scaled, outgoing, strengths, own_proj = start(
         start_kernel,
         [
             ((own_rows, orbitals), BF16),
             ((face + 16, orbitals), BF16),
             ((16, orbitals), BF16),
+            (cell_proj.shape, BF16),
         ],
-        [leave(block) for block in (state, mass_row, send_rows, coupling)],
-    )
+        [leave(block) for block in (state, mass_row, send_rows, coupling, cell_proj)],
+    )
+    other = swap(own_proj, "band", 2)
     ghost = from_behind(outgoing, "mesh", 1)
 
     (pick,) = call(pick_kernel, [kept((cells * per_cell, extended), BF16)], (leave(cell_nodes),))
     pick = hold(pick)
-    near = jnp.stack([cell_proj, other])
+    near = jnp.stack([own_proj, other])
     far = swap(near, "band", 6)
     (operator,) = call(
         operator_kernel,
@@ -392,8 +398,16 @@
     table = hold(table)
     (turned,) = call(turn_kernel, [kept((extended, window), BF16)], (table,))
     turned = hold(turned)
-    (place,) = call(place_kernel, [kept((extended, cells * per_cell), BF16)], (cell_nodes,))
-    place = hold(place)
+    place, send_pick, send_place = call(
+        place_kernel,
+        [
+            kept((extended, cells * per_cell), BF16),
+            kept((face, own_rows), BF16),
+            kept((own_rows, face), BF16),
+        ],
+        (cell_nodes, send_rows),
+    )
+    place, send_pick, send_place = hold(place), hold(send_pick), hold(send_place)
 
     def atom_values(sums, terms):
         sent, outward, base = sums
@@ -435,14 +449,14 @@
     returned, own, _, message = call(
         middle_kernel,
         [shared, own_wide, shared, ((2, face, orbitals), BF16)],
-        (turned, *values, local, state, prev_state, mass_row, send_rows),
+        (turned, *values, local, state, prev_state, mass_row, send_pick),
     )
     outer = outer_swap(message[1])
     inner = inner_pairs(message[0])
     first, scaled_one, ghost_one, *sums_one = call(
         next_kernel,
         [nodal, nodal, shared] + sums_of,
-        (own, inner, outer, returned, ghost, state, prev_state, mass_row, send_rows, table),
+        (own, inner, outer, returned, ghost, state, prev_state, mass_row, send_place, table),
         scratch=[pltpu.VMEM((extended, orbitals), BF16)],
     )
     terms_one = cell_terms(ghost_one, scaled_one)
@@ -452,7 +466,7 @@
     )
     received_one = from_behind(returned_one, "mesh", -1)
     (second,) = call(
-        last_kernel, [nodal], (own_one, received_one, state, first, mass_row, send_rows)
+        last_kernel, [nodal], (own_one, received_one, state, first, mass_row, send_place)
     )
     return (first, second)
 

time: 120 us -> 120 us (level)
  Pallas kernels: 24.6 us -> 26.2 us
    pallas_call x18, Pallas kernels: 24.6 us -> 26.2 us  [call(): pl.pallas_call(kernel, out_shape=[kept[0](*kept[1:]) if kept else jax.Sha...]
where the time goes in v2:
time: 120 us
  starting transfers between devices  43.9 us (37%)
  waiting for transfers between devices  27.8 us (23%)
  Pallas kernels  26.2 us (22%)
  blocking collectives  19.3 us (16%)
  between operations  1.62 us (1%)
    pallas_call x18, Pallas kernels, call(): pl.pallas_call(kernel, out_shape=[kept[0](*kept[1:]) if kept else jax.Sha...  26.2 us
    ppermute x5, starting transfers between devices, outer_swap(): return lax.ppermute(block, 'mesh', route)  19.3 us
    all_gather x3, blocking collectives, inner_pairs(): return lax.all_gather(block, 'mesh', axis=0, axis_index_groups=groups)  17.1 us
    ppermute x4, waiting for transfers between devices, two_away(): return lax.ppermute(block, 'mesh', [(i, j) for i, j in route if 0 <= j < n])  15.8 us
    ppermute x2, waiting for transfers between devices, from_behind(): return lax.ppermute(block, axis, route)  9.2 us
    ppermute x4, starting transfers between devices, two_away(): return lax.ppermute(block, 'mesh', [(i, j) for i, j in route if 0 <= j < n])  8.88 us
    ppermute x2, starting transfers between devices, swap(): lax.ppermute(block, axis, [(i, i ^ mask) for i in range(lax.axis_size(axi...  8.07 us
    ppermute x2, starting transfers between devices, from_behind(): return lax.ppermute(block, axis, route)  7.64 us
  transfers between devices with their start and end apart: 13, of which 6 were waited for; matrix products, arithmetic and copies ran while one was open for 0% of the time, Pallas kernels for 14%

profile of v2, /device:TPU:24, one launch (start us, length us, event | category | flops | bytes accessed | tf_op | source)
XLA Modules:
  0.0 119.5 jit_solution(16030117466979447665)
XLA Ops:
  0.6 1.6 %shard_map.149 = (bf16[1024,256]{1,0:T(8,128)(2,1)S(1)}, bf16[272,256]{1,0:T(8,128)(2,1)S(1)}, bf16[16,256]{1,0:T(8,128)(2,1)S(1)}, bf16[4,64,128]{2,1,0:T(8,128)(2,1)S(1)}) custom-call(bf16[1024,256]{1,0:T(8,128)(2,1)} %state.7, f32[1,1024]{1,0:T(1,128)} %bitcast.13, s32[1,256]{1,0:T(1,128)} %send.3, f32[8,16]{1,0:T(8,128)} %coupling.1, ...), custom_call_target="tpu_custom_call" | custom-call | tf_op jit(solution)/shard_map/pallas_call | solution.py:283
  2.2 3.4 %collective-permute-start = (bf16[4,64,128]{2,1,0:T(8,128)(2,1)S(1)}, bf16[4,64,128]{2,1,0:T(8,128)(2,1)S(1)}, u32[]{:S(2)}, u32[]{:S(2)}) collective-permute-start(bf16[4,64,128]{2,1,0:T(8,128)(2,1)S(1)} %get-tuple-element.32), channel_id=1, source_target_pairs={{0,2},{1,3},{2,0},{3,1},{4,6},{5,7},{6,4},{7,5},{8,10},{9,11},{10,... | collective-permute-start | bytes 196616 | tf_op jit(solution)/shard_map/ppermute | solution.py:327
  5.6 2.8 %collective-permute-done = bf16[4,64,128]{2,1,0:T(8,128)(2,1)S(1)} collective-permute-done((bf16[4,64,128]{2,1,0:T(8,128)(2,1)S(1)}, bf16[4,64,128]{2,1,0:T(8,128)(2,1)S(1)}, u32[]{:S(2)}, u32[]{:S(2)}) %collective-permute-start) | collective-permute-done | bytes 65568 | tf_op jit(solution)/shard_map/ppermute | solution.py:327
  8.4 4.7 %collective-permute-start.1 = (bf16[2,4,64,128]{3,2,1,0:T(8,128)(2,1)S(1)}, bf16[2,4,64,128]{3,2,1,0:T(8,128)(2,1)S(1)}, u32[]{:S(2)}, u32[]{:S(2)}) collective-permute-start(bf16[2,4,64,128]{3,2,1,0:T(8,128)(2,1)S(1)} %pad_maximum_fusion.1), channel_id=1, source_target_pairs={{0,6},{1,7},{2,4},{3,5},{4,2},{5,3},{6,0},{7,1},{8,14},{9,15},{10,... | collective-permute-start | bytes 393224 | tf_op jit(solution)/shard_map/ppermute | solution.py:327
  13.1 3.8 %collective-permute-start.2 = (bf16[272,256]{1,0:T(8,128)(2,1)S(1)}, bf16[272,256]{1,0:T(8,128)(2,1)S(1)}, u32[]{:S(2)}, u32[]{:S(2)}) collective-permute-start(bf16[272,256]{1,0:T(8,128)(2,1)S(1)} %get-tuple-element.33), channel_id=1, source_target_pairs={{0,8},{8,16},{16,24},{24,32},{32,40},{40,48},{48,56},{56,64},{64,7... | collective-permute-start | bytes 417800 | tf_op jit(solution)/shard_map/ppermute | solution.py:25
  17.6 0.0 copy-start.6
  17.6 0.0 copy-start.7
  17.6 1.7 %shard_map.150.pick = bf16[2048,1280]{1,0:T(8,128)(2,1)S(1)} custom-call(s32[4,512]{1,0:T(4,128)} %nodes.3), custom_call_target="tpu_custom_call" | custom-call | tf_op jit(solution)/shard_map/pallas_call | solution.py:283
  19.3 2.2 %all-gather = bf16[8,4,64,128]{3,2,1,0:T(8,128)(2,1)S(1)} all-gather(bf16[4,4,64,128]{3,2,1,0:T(8,128)(2,1)S(1)} %pad_maximum_fusion), channel_id=2, replica_groups={{0,1},{2,3},{4,5},{6,7},{8,9},{10,11},{12,13},{14,15},{16,17},{18,19},{..., dimensions={0}, use_global_device_ids=true | all-gather | bytes 786432 | tf_op jit(solution)/shard_map/all_gather | solution.py:379
  21.5 6.2 %collective-permute-done.2.ghost = bf16[272,256]{1,0:T(8,128)(2,1)S(1)} collective-permute-done((bf16[272,256]{1,0:T(8,128)(2,1)S(1)}, bf16[272,256]{1,0:T(8,128)(2,1)S(1)}, u32[]{:S(2)}, u32[]{:S(2)}) %collective-permute-start.2) | collective-permute-done | bytes 139296 | tf_op jit(solution)/shard_map/ppermute | solution.py:25
  27.7 2.7 %shard_map.151 = (bf16[640,1280]{1,0:T(8,128)(2,1)S(1)}, bf16[128,256]{1,0:T(8,128)(2,1)S(1)}, bf16[256,256]{1,0:T(8,128)(2,1)S(1)}, f32[256,256]{1,0:T(8,128)S(1)}) custom-call(bf16[2,4,4,64,128]{4,3,2,1,0:T(8,128)(2,1)S(1)} %bitcast.8, bf16[2048,1280]{1,0:T(8,128)(2,1)S(1)} %shard_map.150.pick, s32[4,8]{1,0:T(4,128)S(1)} %copy-done.6, ...), custom_call_target="tpu_custom_call" | custom-call | tf_op jit(solution)/shard_map/pallas_call | solution.py:283
  30.4 3.9 %collective-permute-start.3 = (bf16[256,256]{1,0:T(8,128)(2,1)S(1)}, bf16[256,256]{1,0:T(8,128)(2,1)S(1)}, u32[]{:S(2)}, u32[]{:S(2)}) collective-permute-start(bf16[256,256]{1,0:T(8,128)(2,1)S(1)} %get-tuple-element.37), channel_id=1, source_target_pairs={{8,16},{16,8},{24,32},{32,24},{40,48},{48,40},{56,64},{64,56},{72,... | collective-permute-start | bytes 393224 | tf_op jit(solution)/shard_map/ppermute | solution.py:317
  34.3 1.9 %collective-permute-start.4 = (bf16[128,256]{1,0:T(8,128)(2,1)S(1)}, bf16[128,256]{1,0:T(8,128)(2,1)S(1)}, u32[]{:S(2)}, u32[]{:S(2)}) collective-permute-start(bf16[128,256]{1,0:T(8,128)(2,1)S(1)} %get-tuple-element.38), channel_id=1, source_target_pairs={{0,16},{16,32},{24,8},{32,48},{40,24},{48,64},{56,40},{64,80},{72,... | collective-permute-start | bytes 196616 | tf_op jit(solution)/shard_map/ppermute | solution.py:323
  36.3 7.2 %collective-permute-done.4.far = bf16[128,256]{1,0:T(8,128)(2,1)S(1)} collective-permute-done((bf16[128,256]{1,0:T(8,128)(2,1)S(1)}, bf16[128,256]{1,0:T(8,128)(2,1)S(1)}, u32[]{:S(2)}, u32[]{:S(2)}) %collective-permute-start.4) | collective-permute-done | bytes 65568 | tf_op jit(solution)/shard_map/ppermute | solution.py:323
  43.5 0.1 shard_map.153
  43.6 5.7 %all-gather.1 = bf16[544,256]{1,0:T(8,128)(2,1)S(1)} all-gather(bf16[272,256]{1,0:T(8,128)(2,1)S(1)} %get-tuple-element.41), channel_id=3, replica_groups={{0,8},{16,24},{32,40},{48,56},{64,72},{80,88},{96,104},{112,120},{128,1..., dimensions={0}, use_global_device_ids=true | all-gather | bytes 417792 | tf_op jit(solution)/shard_map/all_gather | solution.py:311
  49.3 0.1 shard_map.154
  49.4 4.0 %collective-permute-start.5 = (bf16[256,256]{1,0:T(8,128)(2,1)S(1)}, bf16[256,256]{1,0:T(8,128)(2,1)S(1)}, u32[]{:S(2)}, u32[]{:S(2)}) collective-permute-start(bf16[256,256]{1,0:T(8,128)(2,1)S(1)} %get-tuple-element.42.pair), channel_id=1, source_target_pairs={{8,16},{16,8},{24,32},{32,24},{40,48},{48,40},{56,64},{64,56},{72,... | collective-permute-start | bytes 393224 | tf_op jit(solution)/shard_map/ppermute | solution.py:317
  53.5 2.3 %collective-permute-start.6 = (bf16[128,256]{1,0:T(8,128)(2,1)S(1)}, bf16[128,256]{1,0:T(8,128)(2,1)S(1)}, u32[]{:S(2)}, u32[]{:S(2)}) collective-permute-start(bf16[128,256]{1,0:T(8,128)(2,1)S(1)} %get-tuple-element.43), channel_id=1, source_target_pairs={{8,24},{16,0},{24,40},{32,16},{40,56},{48,32},{56,72},{64,48},{72,... | collective-permute-start | bytes 196616 | tf_op jit(solution)/shard_map/ppermute | solution.py:323
  55.8 2.7 %shard_map.155 = (bf16[1280,2048]{1,0:T(8,128)(2,1)S(1)}, bf16[256,1024]{1,0:T(8,128)(2,1)S(1)}, bf16[1024,256]{1,0:T(8,128)(2,1)S(1)}) custom-call(s32[4,512]{1,0:T(4,128)S(1)} %copy-done.4, s32[1,256]{1,0:T(1,128)S(1)} %copy-done.5), custom_call_target="tpu_custom_call" | custom-call | tf_op jit(solution)/shard_map/pallas_call | solution.py:283
  58.6 2.6 %shard_map.156.operator = bf16[4,512,512]{2,1,0:T(8,128)(2,1)S(1)} custom-call(f32[4,512]{1,0:T(4,128)} %potential.1, bf16[512,512]{1,0:T(8,128)(2,1)} %stiffness.1, bf16[512,512]{1,0:T(8,128)(2,1)} %shape_values.1, s32[1]{0:T(128)S(6)} %copy.16.live, f32[4]{0:T(128)S(1)} %copy-done.8), custom_call_target="tpu_custom_call" | custom-call | tf_op jit(solution)/shard_map/pallas_call | solution.py:283
  61.2 2.8 %shard_map.157.terms = bf16[2048,256]{1,0:T(8,128)(2,1)S(1)} custom-call(bf16[2048,1280]{1,0:T(8,128)(2,1)S(1)} %shard_map.150.pick, bf16[4,512,512]{2,1,0:T(8,128)(2,1)S(1)} %shard_map.156.operator, bf16[272,256]{1,0:T(8,128)(2,1)S(1)} %collective-permute-done.2.ghost, bf16[1024,256]{1,0:T(8,128)(2,1)S(1)} %get-tuple-element.34.scaled), custom_call_target="tpu_custom_call" | custom-call | tf_op jit(solution)/shard_map/pallas_call | solution.py:283
  64.0 1.5 %shard_map.158.local = f32[1280,256]{1,0:T(8,128)S(1)} custom-call(bf16[1280,2048]{1,0:T(8,128)(2,1)S(1)} %get-tuple-element.44.place, bf16[2048,256]{1,0:T(8,128)(2,1)S(1)} %shard_map.157.terms), custom_call_target="tpu_custom_call" | custom-call | tf_op jit(solution)/shard_map/pallas_call | solution.py:283
  65.6 0.0 copy-start
  65.6 0.0 copy-start.1
  65.6 0.5 shard_map.152.turned
  66.1 0.5 copy-done
  66.6 0.2 copy-done.1
  66.8 1.8 %shard_map.159 = (bf16[256,256]{1,0:T(8,128)(2,1)S(1)}, f32[1024,256]{1,0:T(8,128)S(1)}, bf16[256,256]{1,0:T(8,128)(2,1)}, bf16[2,256,256]{2,1,0:T(8,128)(2,1)S(1)}) custom-call(bf16[1280,640]{1,0:T(8,128)(2,1)S(1)} %shard_map.152.turned, bf16[256,256]{1,0:T(8,128)(2,1)S(1)} %get-tuple-element.42.pair, bf16[256,256]{1,0:T(8,128)(2,1)S(1)} %collective-permute-done.5.near, ...), custom_call_target="tpu_custom_call" | custom-call | tf_op jit(solution)/shard_map/pallas_call | solution.py:283
  68.6 3.7 %collective-permute-start.7 = (bf16[256,256]{1,0:T(8,128)(2,1)S(1)}, bf16[256,256]{1,0:T(8,128)(2,1)S(1)}, u32[]{:S(2)}, u32[]{:S(2)}) collective-permute-start(bf16[256,256]{1,0:T(8,128)(2,1)S(1)} %get-tuple-element.62), channel_id=1, source_target_pairs={{8,16},{16,8},{24,32},{32,24},{40,48},{48,40},{56,64},{64,56},{72,... | collective-permute-start | bytes 393224 | tf_op jit(solution)/shard_map/ppermute | solution.py:317
  72.3 5.6 %all_gather.25.inner = bf16[2,256,256]{2,1,0:T(8,128)(2,1)S(1)} all-gather(bf16[1,256,256]{2,1,0:T(8,128)(2,1)S(1)} %get-tuple-element.63), channel_id=1, replica_groups={{0,8},{16,24},{32,40},{48,56},{64,72},{80,88},{96,104},{112,120},{128,1..., dimensions={0}, use_global_device_ids=true | all-gather | bytes 393216 | tf_op jit(solution)/shard_map/all_gather | solution.py:311
  77.9 1.5 %shard_map.160 = (bf16[1024,256]{1,0:T(8,128)(2,1)}, bf16[1024,256]{1,0:T(8,128)(2,1)S(1)}, bf16[256,256]{1,0:T(8,128)(2,1)S(1)}, bf16[128,256]{1,0:T(8,128)(2,1...) custom-call(f32[1024,256]{1,0:T(8,128)S(1)} %get-tuple-element.46.own, ...), custom_call_target="tpu_custom_call" | custom-call | tf_op jit(solution)/shard_map/pallas_call | solution.py:283
  79.4 4.2 %collective-permute-start.8 = (bf16[256,256]{1,0:T(8,128)(2,1)S(1)}, bf16[256,256]{1,0:T(8,128)(2,1)S(1)}, u32[]{:S(2)}, u32[]{:S(2)}) collective-permute-start(bf16[256,256]{1,0:T(8,128)(2,1)S(1)} %get-tuple-element.52), channel_id=1, source_target_pairs={{8,16},{16,8},{24,32},{32,24},{40,48},{48,40},{56,64},{64,56},{72,... | collective-permute-start | bytes 393224 | tf_op jit(solution)/shard_map/ppermute | solution.py:317
  83.7 2.5 %collective-permute-start.9 = (bf16[128,256]{1,0:T(8,128)(2,1)S(1)}, bf16[128,256]{1,0:T(8,128)(2,1)S(1)}, u32[]{:S(2)}, u32[]{:S(2)}) collective-permute-start(bf16[128,256]{1,0:T(8,128)(2,1)S(1)} %get-tuple-element.53), channel_id=1, source_target_pairs={{0,16},{16,32},{24,8},{32,48},{40,24},{48,64},{56,40},{64,80},{72,... | collective-permute-start | bytes 196616 | tf_op jit(solution)/shard_map/ppermute | solution.py:323
  86.2 7.4 %collective-permute-done.9.far = bf16[128,256]{1,0:T(8,128)(2,1)S(1)} collective-permute-done((bf16[128,256]{1,0:T(8,128)(2,1)S(1)}, bf16[128,256]{1,0:T(8,128)(2,1)S(1)}, u32[]{:S(2)}, u32[]{:S(2)}) %collective-permute-start.9) | collective-permute-done | bytes 65568 | tf_op jit(solution)/shard_map/ppermute | solution.py:323
  93.6 0.1 shard_map.161
  93.6 5.7 %all-gather.2 = bf16[544,256]{1,0:T(8,128)(2,1)S(1)} all-gather(bf16[272,256]{1,0:T(8,128)(2,1)S(1)} %get-tuple-element.55), channel_id=4, replica_groups={{0,8},{16,24},{32,40},{48,56},{64,72},{80,88},{96,104},{112,120},{128,1..., dimensions={0}, use_global_device_ids=true | all-gather | bytes 417792 | tf_op jit(solution)/shard_map/all_gather | solution.py:311
  99.4 0.1 shard_map.162
  99.5 3.4 %collective-permute-start.10 = (bf16[256,256]{1,0:T(8,128)(2,1)S(1)}, bf16[256,256]{1,0:T(8,128)(2,1)S(1)}, u32[]{:S(2)}, u32[]{:S(2)}) collective-permute-start(bf16[256,256]{1,0:T(8,128)(2,1)S(1)} %get-tuple-element.56.pair), channel_id=1, source_target_pairs={{8,16},{16,8},{24,32},{32,24},{40,48},{48,40},{56,64},{64,56},{72,... | collective-permute-start | bytes 393224 | tf_op jit(solution)/shard_map/ppermute | solution.py:317
  102.9 2.1 %collective-permute-start.11 = (bf16[128,256]{1,0:T(8,128)(2,1)S(1)}, bf16[128,256]{1,0:T(8,128)(2,1)S(1)}, u32[]{:S(2)}, u32[]{:S(2)}) collective-permute-start(bf16[128,256]{1,0:T(8,128)(2,1)S(1)} %get-tuple-element.57), channel_id=1, source_target_pairs={{8,24},{16,0},{24,40},{32,16},{40,56},{48,32},{56,72},{64,48},{72,... | collective-permute-start | bytes 196616 | tf_op jit(solution)/shard_map/ppermute | solution.py:323
  105.1 2.8 %shard_map.163.terms = bf16[2048,256]{1,0:T(8,128)(2,1)S(1)} custom-call(bf16[2048,1280]{1,0:T(8,128)(2,1)S(1)} %shard_map.150.pick, bf16[4,512,512]{2,1,0:T(8,128)(2,1)S(1)} %shard_map.156.operator, bf16[256,256]{1,0:T(8,128)(2,1)S(1)} %get-tuple-element.58.ghost, bf16[1024,256]{1,0:T(8,128)(2,1)S(1)} %get-tuple-element.59.scaled), custom_call_target="tpu_custom_call" | custom-call | tf_op jit(solution)/shard_map/pallas_call | solution.py:283
  107.9 1.6 %shard_map.164.local = f32[1280,256]{1,0:T(8,128)S(1)} custom-call(bf16[1280,2048]{1,0:T(8,128)(2,1)S(1)} %get-tuple-element.44.place, bf16[2048,256]{1,0:T(8,128)(2,1)S(1)} %shard_map.163.terms), custom_call_target="tpu_custom_call" | custom-call | tf_op jit(solution)/shard_map/pallas_call | solution.py:283
  109.5 0.0 copy-start.2
  109.5 1.2 %collective-permute-done.11.far = bf16[128,256]{1,0:T(8,128)(2,1)S(1)} collective-permute-done((bf16[128,256]{1,0:T(8,128)(2,1)S(1)}, bf16[128,256]{1,0:T(8,128)(2,1)S(1)}, u32[]{:S(2)}, u32[]{:S(2)}) %collective-permute-start.11) | collective-permute-done | bytes 65568 | tf_op jit(solution)/shard_map/ppermute | solution.py:323
  110.7 0.7 shard_map.165
  111.4 3.8 %collective-permute-start.12 = (bf16[256,256]{1,0:T(8,128)(2,1)S(1)}, bf16[256,256]{1,0:T(8,128)(2,1)S(1)}, u32[]{:S(2)}, u32[]{:S(2)}) collective-permute-start(bf16[256,256]{1,0:T(8,128)(2,1)S(1)} %get-tuple-element.61), channel_id=1, source_target_pairs={{8,0},{16,8},{24,16},{32,24},{40,32},{48,40},{56,48},{64,56},{72,6... | collective-permute-start | bytes 393224 | tf_op jit(solution)/shard_map/ppermute | solution.py:25
  115.2 3.0 %collective-permute-done.12.received = bf16[256,256]{1,0:T(8,128)(2,1)S(1)} collective-permute-done((bf16[256,256]{1,0:T(8,128)(2,1)S(1)}, bf16[256,256]{1,0:T(8,128)(2,1)S(1)}, u32[]{:S(2)}, u32[]{:S(2)}) %collective-permute-start.12) | collective-permute-done | bytes 131104 | tf_op jit(solution)/shard_map/ppermute | solution.py:25
  118.3 1.2 %shard_map.166 = bf16[1024,256]{1,0:T(8,128)(2,1)} custom-call(f32[1024,256]{1,0:T(8,128)S(1)} %get-tuple-element.60.own, bf16[256,256]{1,0:T(8,128)(2,1)S(1)} %collective-permute-done.12.received, bf16[1024,256]{1,0:T(8,128)(2,1)S(1)} %copy-done, bf16[1024,256]{1,0:T(8,128)(2,1)S(1)} %copy-done.2, f32[1,1024]{1,0:T(1,128)S(1)} %bitcast.16, ...), custom_call_target="tpu_custom_call" | custom-call | tf_op jit(solution)/shard_map/pallas_call | solution.py:283
  (21 shorter events, 0.1 us)
Async XLA Ops:
  2.2 6.2 %collective-permute-start = (bf16[4,64,128]{2,1,0:T(8,128)(2,1)S(1)}, bf16[4,64,128]{2,1,0:T(8,128)(2,1)S(1)}, u32[]{:S(2)}, u32[]{:S(2)}) collective-permute-start(bf16[4,64,128]{2,1,0:T(8,128)(2,1)S(1)} %get-tuple-element.32), channel_id=1, source_target_pairs={{0,2},{1,3},{2,0},{3,1},{4,6},{5,7},{6,4},{7,5},{8,10},{9,11},{10,... | collective-permute-start | bytes 196616 | tf_op jit(solution)/shard_map/ppermute | solution.py:327
  8.4 10.9 %collective-permute-start.1 = (bf16[2,4,64,128]{3,2,1,0:T(8,128)(2,1)S(1)}, bf16[2,4,64,128]{3,2,1,0:T(8,128)(2,1)S(1)}, u32[]{:S(2)}, u32[]{:S(2)}) collective-permute-start(bf16[2,4,64,128]{3,2,1,0:T(8,128)(2,1)S(1)} %pad_maximum_fusion.1), channel_id=1, source_target_pairs={{0,6},{1,7},{2,4},{3,5},{4,2},{5,3},{6,0},{7,1},{8,14},{9,15},{10,... | collective-permute-start | bytes 393224 | tf_op jit(solution)/shard_map/ppermute | solution.py:327
  13.1 14.6 %collective-permute-start.2 = (bf16[272,256]{1,0:T(8,128)(2,1)S(1)}, bf16[272,256]{1,0:T(8,128)(2,1)S(1)}, u32[]{:S(2)}, u32[]{:S(2)}) collective-permute-start(bf16[272,256]{1,0:T(8,128)(2,1)S(1)} %get-tuple-element.33), channel_id=1, source_target_pairs={{0,8},{8,16},{16,24},{24,32},{32,40},{40,48},{48,56},{56,64},{64,7... | collective-permute-start | bytes 417800 | tf_op jit(solution)/shard_map/ppermute | solution.py:25
  17.6 10.1 %copy-start.6 = (s32[4,8]{1,0:T(4,128)S(1)}, s32[4,8]{1,0:T(4,128)}, u32[]{:S(2)}) copy-start(s32[4,8]{1,0:T(4,128)} %owner.1) | copy-start | bytes 388
  17.6 10.1 %copy-start.7 = (s32[4,8]{1,0:T(4,128)S(1)}, s32[4,8]{1,0:T(4,128)}, u32[]{:S(2)}) copy-start(s32[4,8]{1,0:T(4,128)} %slot.1) | copy-start | bytes 388
  27.7 28.1 %copy-start.4 = (s32[4,512]{1,0:T(4,128)S(1)}, s32[4,512]{1,0:T(4,128)}, u32[]{:S(2)}) copy-start(s32[4,512]{1,0:T(4,128)} %nodes.3) | copy-start | bytes 24580
  27.7 28.1 %copy-start.5 = (s32[1,256]{1,0:T(1,128)S(1)}, s32[1,256]{1,0:T(1,128)}, u32[]{:S(2)}) copy-start(s32[1,256]{1,0:T(1,128)} %send.3) | copy-start | bytes 3076
  27.7 30.9 %copy-start.8 = (f32[4]{0:T(128)S(1)}, f32[4]{0:T(128)}, u32[]{:S(2)}) copy-start(f32[4]{0:T(128)} %scale.1) | copy-start | bytes 52
  30.4 13.1 %collective-permute-start.3 = (bf16[256,256]{1,0:T(8,128)(2,1)S(1)}, bf16[256,256]{1,0:T(8,128)(2,1)S(1)}, u32[]{:S(2)}, u32[]{:S(2)}) collective-permute-start(bf16[256,256]{1,0:T(8,128)(2,1)S(1)} %get-tuple-element.37), channel_id=1, source_target_pairs={{8,16},{16,8},{24,32},{32,24},{40,48},{48,40},{56,64},{64,56},{72,... | collective-permute-start | bytes 393224 | tf_op jit(solution)/shard_map/ppermute | solution.py:317
  34.3 9.2 %collective-permute-start.4 = (bf16[128,256]{1,0:T(8,128)(2,1)S(1)}, bf16[128,256]{1,0:T(8,128)(2,1)S(1)}, u32[]{:S(2)}, u32[]{:S(2)}) collective-permute-start(bf16[128,256]{1,0:T(8,128)(2,1)S(1)} %get-tuple-element.38), channel_id=1, source_target_pairs={{0,16},{16,32},{24,8},{32,48},{40,24},{48,64},{56,40},{64,80},{72,... | collective-permute-start | bytes 196616 | tf_op jit(solution)/shard_map/ppermute | solution.py:323
  49.4 16.7 %collective-permute-start.5 = (bf16[256,256]{1,0:T(8,128)(2,1)S(1)}, bf16[256,256]{1,0:T(8,128)(2,1)S(1)}, u32[]{:S(2)}, u32[]{:S(2)}) collective-permute-start(bf16[256,256]{1,0:T(8,128)(2,1)S(1)} %get-tuple-element.42.pair), channel_id=1, source_target_pairs={{8,16},{16,8},{24,32},{32,24},{40,48},{48,40},{56,64},{64,56},{72,... | collective-permute-start | bytes 393224 | tf_op jit(solution)/shard_map/ppermute | solution.py:317
  53.5 12.6 %collective-permute-start.6 = (bf16[128,256]{1,0:T(8,128)(2,1)S(1)}, bf16[128,256]{1,0:T(8,128)(2,1)S(1)}, u32[]{:S(2)}, u32[]{:S(2)}) collective-permute-start(bf16[128,256]{1,0:T(8,128)(2,1)S(1)} %get-tuple-element.43), channel_id=1, source_target_pairs={{8,24},{16,0},{24,40},{32,16},{40,56},{48,32},{56,72},{64,48},{72,... | collective-permute-start | bytes 196616 | tf_op jit(solution)/shard_map/ppermute | solution.py:323
  65.6 1.0 copy-start
  65.6 1.2 copy-start.1
  65.6 1.2 copy-start.3
  68.6 9.3 %collective-permute-start.7 = (bf16[256,256]{1,0:T(8,128)(2,1)S(1)}, bf16[256,256]{1,0:T(8,128)(2,1)S(1)}, u32[]{:S(2)}, u32[]{:S(2)}) collective-permute-start(bf16[256,256]{1,0:T(8,128)(2,1)S(1)} %get-tuple-element.62), channel_id=1, source_target_pairs={{8,16},{16,8},{24,32},{32,24},{40,48},{48,40},{56,64},{64,56},{72,... | collective-permute-start | bytes 393224 | tf_op jit(solution)/shard_map/ppermute | solution.py:317
  79.4 14.1 %collective-permute-start.8 = (bf16[256,256]{1,0:T(8,128)(2,1)S(1)}, bf16[256,256]{1,0:T(8,128)(2,1)S(1)}, u32[]{:S(2)}, u32[]{:S(2)}) collective-permute-start(bf16[256,256]{1,0:T(8,128)(2,1)S(1)} %get-tuple-element.52), channel_id=1, source_target_pairs={{8,16},{16,8},{24,32},{32,24},{40,48},{48,40},{56,64},{64,56},{72,... | collective-permute-start | bytes 393224 | tf_op jit(solution)/shard_map/ppermute | solution.py:317
  83.7 9.9 %collective-permute-start.9 = (bf16[128,256]{1,0:T(8,128)(2,1)S(1)}, bf16[128,256]{1,0:T(8,128)(2,1)S(1)}, u32[]{:S(2)}, u32[]{:S(2)}) collective-permute-start(bf16[128,256]{1,0:T(8,128)(2,1)S(1)} %get-tuple-element.53), channel_id=1, source_target_pairs={{0,16},{16,32},{24,8},{32,48},{40,24},{48,64},{56,40},{64,80},{72,... | collective-permute-start | bytes 196616 | tf_op jit(solution)/shard_map/ppermute | solution.py:323
  99.5 11.2 %collective-permute-start.10 = (bf16[256,256]{1,0:T(8,128)(2,1)S(1)}, bf16[256,256]{1,0:T(8,128)(2,1)S(1)}, u32[]{:S(2)}, u32[]{:S(2)}) collective-permute-start(bf16[256,256]{1,0:T(8,128)(2,1)S(1)} %get-tuple-element.56.pair), channel_id=1, source_target_pairs={{8,16},{16,8},{24,32},{32,24},{40,48},{48,40},{56,64},{64,56},{72,... | collective-permute-start | bytes 393224 | tf_op jit(solution)/shard_map/ppermute | solution.py:317
  102.9 7.8 %collective-permute-start.11 = (bf16[128,256]{1,0:T(8,128)(2,1)S(1)}, bf16[128,256]{1,0:T(8,128)(2,1)S(1)}, u32[]{:S(2)}, u32[]{:S(2)}) collective-permute-start(bf16[128,256]{1,0:T(8,128)(2,1)S(1)} %get-tuple-element.57), channel_id=1, source_target_pairs={{8,24},{16,0},{24,40},{32,16},{40,56},{48,32},{56,72},{64,48},{72,... | collective-permute-start | bytes 196616 | tf_op jit(solution)/shard_map/ppermute | solution.py:323
  109.5 8.8 %copy-start.2 = (bf16[1024,256]{1,0:T(8,128)(2,1)S(1)}, bf16[1024,256]{1,0:T(8,128)(2,1)}, u32[]{:S(2)}) copy-start(bf16[1024,256]{1,0:T(8,128)(2,1)} %get-tuple-element.30.first) | copy-start | bytes 1572868
  111.4 6.9 %collective-permute-start.12 = (bf16[256,256]{1,0:T(8,128)(2,1)S(1)}, bf16[256,256]{1,0:T(8,128)(2,1)S(1)}, u32[]{:S(2)}, u32[]{:S(2)}) collective-permute-start(bf16[256,256]{1,0:T(8,128)(2,1)S(1)} %get-tuple-element.61), channel_id=1, source_target_pairs={{8,0},{16,8},{24,16},{32,24},{40,32},{48,40},{56,48},{64,56},{72,6... | collective-permute-start | bytes 393224 | tf_op jit(solution)/shard_map/ppermute | solution.py:25

commit v3 on v2

--- a/solution.py
+++ b/solution.py
@@ -146,8 +146,8 @@
             for core in range(2):
                 band = (x ^ flip) * 2 + core
                 rows = pl.ds(pl.multiple_of(band * share, share), share)
-                nodes[rows, :] = projectors[core, i, c].astype(F32)
-        block = jnp.transpose(nodes[...]).astype(BF16)
+                nodes[rows, :] = projectors[core, i, c]
+        block = jnp.transpose(nodes[...])
         at_nodes = dot(block, pick[c * per_cell : (c + 1) * per_cell, :])
         at_nodes = at_nodes * jnp.where(c < live[0], 1.0, 0.0)
         for j in range(APC):
@@ -362,7 +362,7 @@
         ],
         [leave(block) for block in (state, mass_row, send_rows, coupling, cell_proj)],
     )
-    other = swap(own_proj, "band", 2)
+    other = swap(cell_proj, "band", 2)
     ghost = from_behind(outgoing, "mesh", 1)
 
     (pick,) = call(pick_kernel, [kept((cells * per_cell, extended), BF16)], (leave(cell_nodes),))
@@ -392,7 +392,7 @@
         scratch=[
             pltpu.VMEM((window, extended), F32),
             pltpu.VMEM((extended, orbitals), BF16),
-            pltpu.VMEM((per_cell, block), F32),
+            pltpu.VMEM((per_cell, block), BF16),
         ],
     )
     table = hold(table)

time: 120 us -> 119 us (level)
  waiting for transfers between devices: 27.8 us -> 26.4 us
    ppermute x2, waiting for transfers between devices: 2.75 us -> 1.37 us  [swap(): lax.ppermute(block, axis, [(i, i ^ mask) for i in range(lax.axis_size(axi...]
  transfers between devices with their start and end apart: 13 -> 13, of which waited for: 6 -> 6; matrix products, arithmetic and copies ran while one was open for 0% -> 0% of each run, Pallas kernels for 14% -> 15%
where the time goes in v3:
time: 119 us; the launch traced here: 118 us
  starting transfers between devices  43.9 us (37%)
  waiting for transfers between devices  26.4 us (22%)
  Pallas kernels  26.1 us (22%)
  blocking collectives  19.3 us (16%)
  between operations  1.62 us (1%)
    pallas_call x18, Pallas kernels, call(): pl.pallas_call(kernel, out_shape=[kept[0](*kept[1:]) if kept else jax.Sha...  26.1 us
    ppermute x5, starting transfers between devices, outer_swap(): return lax.ppermute(block, 'mesh', route)  19.3 us
    all_gather x3, blocking collectives, inner_pairs(): return lax.all_gather(block, 'mesh', axis=0, axis_index_groups=groups)  17.1 us
    ppermute x4, waiting for transfers between devices, two_away(): return lax.ppermute(block, 'mesh', [(i, j) for i, j in route if 0 <= j < n])  15.8 us
    ppermute x2, waiting for transfers between devices, from_behind(): return lax.ppermute(block, axis, route)  9.2 us
    ppermute x4, starting transfers between devices, two_away(): return lax.ppermute(block, 'mesh', [(i, j) for i, j in route if 0 <= j < n])  8.88 us
    ppermute x2, starting transfers between devices, swap(): lax.ppermute(block, axis, [(i, i ^ mask) for i in range(lax.axis_size(axi...  8.07 us
    ppermute x2, starting transfers between devices, from_behind(): return lax.ppermute(block, axis, route)  7.64 us
  transfers between devices with their start and end apart: 13, of which 6 were waited for; matrix products, arithmetic and copies ran while one was open for 0% of the time, Pallas kernels for 15%

profile of v3, /device:TPU:24, one launch (start us, length us, event | category | flops | bytes accessed | tf_op | source)
XLA Modules:
  0.0 118.0 jit_solution(8756518303542630424)
XLA Ops:
  0.6 3.4 %collective-permute-start = (bf16[4,64,128]{2,1,0:T(8,128)(2,1)}, bf16[4,64,128]{2,1,0:T(8,128)(2,1)S(1)}, u32[]{:S(2)}, u32[]{:S(2)}) collective-permute-start(bf16[4,64,128]{2,1,0:T(8,128)(2,1)} %projectors.1), channel_id=1, source_target_pairs={{0,2},{1,3},{2,0},{3,1},{4,6},{5,7},{6,4},{7,5},{8,10},{9,11},{10,... | collective-permute-start | bytes 196616 | tf_op jit(solution)/shard_map/ppermute | solution.py:327
  4.0 1.6 %shard_map.149 = (bf16[1024,256]{1,0:T(8,128)(2,1)S(1)}, bf16[272,256]{1,0:T(8,128)(2,1)S(1)}, bf16[16,256]{1,0:T(8,128)(2,1)S(1)}, bf16[4,64,128]{2,1,0:T(8,128)(2,1)S(1)}) custom-call(bf16[1024,256]{1,0:T(8,128)(2,1)} %state.7, f32[1,1024]{1,0:T(1,128)} %bitcast.13, s32[1,256]{1,0:T(1,128)} %send.3, f32[8,16]{1,0:T(8,128)} %coupling.1, ...), custom_call_target="tpu_custom_call" | custom-call | tf_op jit(solution)/shard_map/pallas_call | solution.py:283
  5.6 1.4 %collective-permute-done = bf16[4,64,128]{2,1,0:T(8,128)(2,1)S(1)} collective-permute-done((bf16[4,64,128]{2,1,0:T(8,128)(2,1)}, bf16[4,64,128]{2,1,0:T(8,128)(2,1)S(1)}, u32[]{:S(2)}, u32[]{:S(2)}) %collective-permute-start) | collective-permute-done | bytes 65568 | tf_op jit(solution)/shard_map/ppermute | solution.py:327
  7.0 4.7 %collective-permute-start.1 = (bf16[2,4,64,128]{3,2,1,0:T(8,128)(2,1)S(1)}, bf16[2,4,64,128]{3,2,1,0:T(8,128)(2,1)S(1)}, u32[]{:S(2)}, u32[]{:S(2)}) collective-permute-start(bf16[2,4,64,128]{3,2,1,0:T(8,128)(2,1)S(1)} %pad_maximum_fusion.1), channel_id=1, source_target_pairs={{0,6},{1,7},{2,4},{3,5},{4,2},{5,3},{6,0},{7,1},{8,14},{9,15},{10,... | collective-permute-start | bytes 393224 | tf_op jit(solution)/shard_map/ppermute | solution.py:327
  11.7 3.8 %collective-permute-start.2 = (bf16[272,256]{1,0:T(8,128)(2,1)S(1)}, bf16[272,256]{1,0:T(8,128)(2,1)S(1)}, u32[]{:S(2)}, u32[]{:S(2)}) collective-permute-start(bf16[272,256]{1,0:T(8,128)(2,1)S(1)} %get-tuple-element.33), channel_id=1, source_target_pairs={{0,8},{8,16},{16,24},{24,32},{32,40},{40,48},{48,56},{56,64},{64,7... | collective-permute-start | bytes 417800 | tf_op jit(solution)/shard_map/ppermute | solution.py:25
  16.2 0.0 copy-start.6
  16.2 0.0 copy-start.7
  16.2 1.7 %shard_map.150.pick = bf16[2048,1280]{1,0:T(8,128)(2,1)S(1)} custom-call(s32[4,512]{1,0:T(4,128)} %nodes.3), custom_call_target="tpu_custom_call" | custom-call | tf_op jit(solution)/shard_map/pallas_call | solution.py:283
  18.0 2.2 %all-gather = bf16[8,4,64,128]{3,2,1,0:T(8,128)(2,1)S(1)} all-gather(bf16[4,4,64,128]{3,2,1,0:T(8,128)(2,1)S(1)} %pad_maximum_fusion), channel_id=2, replica_groups={{0,1},{2,3},{4,5},{6,7},{8,9},{10,11},{12,13},{14,15},{16,17},{18,19},{..., dimensions={0}, use_global_device_ids=true | all-gather | bytes 786432 | tf_op jit(solution)/shard_map/all_gather | solution.py:379
  20.1 6.2 %collective-permute-done.2.ghost = bf16[272,256]{1,0:T(8,128)(2,1)S(1)} collective-permute-done((bf16[272,256]{1,0:T(8,128)(2,1)S(1)}, bf16[272,256]{1,0:T(8,128)(2,1)S(1)}, u32[]{:S(2)}, u32[]{:S(2)}) %collective-permute-start.2) | collective-permute-done | bytes 139296 | tf_op jit(solution)/shard_map/ppermute | solution.py:25
  26.3 0.0 copy-start.8
  26.3 2.6 %shard_map.151 = (bf16[640,1280]{1,0:T(8,128)(2,1)S(1)}, bf16[128,256]{1,0:T(8,128)(2,1)S(1)}, bf16[256,256]{1,0:T(8,128)(2,1)S(1)}, f32[256,256]{1,0:T(8,128)S(1)}) custom-call(bf16[2,4,4,64,128]{4,3,2,1,0:T(8,128)(2,1)S(1)} %bitcast.8, bf16[2048,1280]{1,0:T(8,128)(2,1)S(1)} %shard_map.150.pick, s32[4,8]{1,0:T(4,128)S(1)} %copy-done.6, ...), custom_call_target="tpu_custom_call" | custom-call | tf_op jit(solution)/shard_map/pallas_call | solution.py:283
  28.9 3.9 %collective-permute-start.3 = (bf16[256,256]{1,0:T(8,128)(2,1)S(1)}, bf16[256,256]{1,0:T(8,128)(2,1)S(1)}, u32[]{:S(2)}, u32[]{:S(2)}) collective-permute-start(bf16[256,256]{1,0:T(8,128)(2,1)S(1)} %get-tuple-element.37), channel_id=1, source_target_pairs={{8,16},{16,8},{24,32},{32,24},{40,48},{48,40},{56,64},{64,56},{72,... | collective-permute-start | bytes 393224 | tf_op jit(solution)/shard_map/ppermute | solution.py:317
  32.8 1.9 %collective-permute-start.4 = (bf16[128,256]{1,0:T(8,128)(2,1)S(1)}, bf16[128,256]{1,0:T(8,128)(2,1)S(1)}, u32[]{:S(2)}, u32[]{:S(2)}) collective-permute-start(bf16[128,256]{1,0:T(8,128)(2,1)S(1)} %get-tuple-element.38), channel_id=1, source_target_pairs={{0,16},{16,32},{24,8},{32,48},{40,24},{48,64},{56,40},{64,80},{72,... | collective-permute-start | bytes 196616 | tf_op jit(solution)/shard_map/ppermute | solution.py:323
  34.8 7.2 %collective-permute-done.4.far = bf16[128,256]{1,0:T(8,128)(2,1)S(1)} collective-permute-done((bf16[128,256]{1,0:T(8,128)(2,1)S(1)}, bf16[128,256]{1,0:T(8,128)(2,1)S(1)}, u32[]{:S(2)}, u32[]{:S(2)}) %collective-permute-start.4) | collective-permute-done | bytes 65568 | tf_op jit(solution)/shard_map/ppermute | solution.py:323
  42.0 0.1 shard_map.153
  42.1 5.7 %all-gather.1 = bf16[544,256]{1,0:T(8,128)(2,1)S(1)} all-gather(bf16[272,256]{1,0:T(8,128)(2,1)S(1)} %get-tuple-element.41), channel_id=3, replica_groups={{0,8},{16,24},{32,40},{48,56},{64,72},{80,88},{96,104},{112,120},{128,1..., dimensions={0}, use_global_device_ids=true | all-gather | bytes 417792 | tf_op jit(solution)/shard_map/all_gather | solution.py:311
  47.8 0.1 shard_map.154
  47.9 4.0 %collective-permute-start.5 = (bf16[256,256]{1,0:T(8,128)(2,1)S(1)}, bf16[256,256]{1,0:T(8,128)(2,1)S(1)}, u32[]{:S(2)}, u32[]{:S(2)}) collective-permute-start(bf16[256,256]{1,0:T(8,128)(2,1)S(1)} %get-tuple-element.42.pair), channel_id=1, source_target_pairs={{8,16},{16,8},{24,32},{32,24},{40,48},{48,40},{56,64},{64,56},{72,... | collective-permute-start | bytes 393224 | tf_op jit(solution)/shard_map/ppermute | solution.py:317
  52.0 2.3 %collective-permute-start.6 = (bf16[128,256]{1,0:T(8,128)(2,1)S(1)}, bf16[128,256]{1,0:T(8,128)(2,1)S(1)}, u32[]{:S(2)}, u32[]{:S(2)}) collective-permute-start(bf16[128,256]{1,0:T(8,128)(2,1)S(1)} %get-tuple-element.43), channel_id=1, source_target_pairs={{8,24},{16,0},{24,40},{32,16},{40,56},{48,32},{56,72},{64,48},{72,... | collective-permute-start | bytes 196616 | tf_op jit(solution)/shard_map/ppermute | solution.py:323
  54.3 2.7 %shard_map.155 = (bf16[1280,2048]{1,0:T(8,128)(2,1)S(1)}, bf16[256,1024]{1,0:T(8,128)(2,1)S(1)}, bf16[1024,256]{1,0:T(8,128)(2,1)S(1)}) custom-call(s32[4,512]{1,0:T(4,128)S(1)} %copy-done.4, s32[1,256]{1,0:T(1,128)S(1)} %copy-done.5), custom_call_target="tpu_custom_call" | custom-call | tf_op jit(solution)/shard_map/pallas_call | solution.py:283
  57.1 2.6 %shard_map.156.operator = bf16[4,512,512]{2,1,0:T(8,128)(2,1)S(1)} custom-call(f32[4,512]{1,0:T(4,128)} %potential.1, bf16[512,512]{1,0:T(8,128)(2,1)} %stiffness.1, bf16[512,512]{1,0:T(8,128)(2,1)} %shape_values.1, s32[1]{0:T(128)S(6)} %copy.16.live, f32[4]{0:T(128)S(1)} %copy-done.8), custom_call_target="tpu_custom_call" | custom-call | tf_op jit(solution)/shard_map/pallas_call | solution.py:283
  59.7 2.8 %shard_map.157.terms = bf16[2048,256]{1,0:T(8,128)(2,1)S(1)} custom-call(bf16[2048,1280]{1,0:T(8,128)(2,1)S(1)} %shard_map.150.pick, bf16[4,512,512]{2,1,0:T(8,128)(2,1)S(1)} %shard_map.156.operator, bf16[272,256]{1,0:T(8,128)(2,1)S(1)} %collective-permute-done.2.ghost, bf16[1024,256]{1,0:T(8,128)(2,1)S(1)} %get-tuple-element.34.scaled), custom_call_target="tpu_custom_call" | custom-call | tf_op jit(solution)/shard_map/pallas_call | solution.py:283
  62.5 1.5 %shard_map.158.local = f32[1280,256]{1,0:T(8,128)S(1)} custom-call(bf16[1280,2048]{1,0:T(8,128)(2,1)S(1)} %get-tuple-element.44.place, bf16[2048,256]{1,0:T(8,128)(2,1)S(1)} %shard_map.157.terms), custom_call_target="tpu_custom_call" | custom-call | tf_op jit(solution)/shard_map/pallas_call | solution.py:283
  64.1 0.0 copy-start.3
  64.1 0.5 shard_map.152.turned
  64.6 0.5 copy-done
  65.1 0.2 copy-done.1
  65.3 1.8 %shard_map.159 = (bf16[256,256]{1,0:T(8,128)(2,1)S(1)}, f32[1024,256]{1,0:T(8,128)S(1)}, bf16[256,256]{1,0:T(8,128)(2,1)}, bf16[2,256,256]{2,1,0:T(8,128)(2,1)S(1)}) custom-call(bf16[1280,640]{1,0:T(8,128)(2,1)S(1)} %shard_map.152.turned, bf16[256,256]{1,0:T(8,128)(2,1)S(1)} %get-tuple-element.42.pair, bf16[256,256]{1,0:T(8,128)(2,1)S(1)} %collective-permute-done.5.near, ...), custom_call_target="tpu_custom_call" | custom-call | tf_op jit(solution)/shard_map/pallas_call | solution.py:283
  67.1 3.7 %collective-permute-start.7 = (bf16[256,256]{1,0:T(8,128)(2,1)S(1)}, bf16[256,256]{1,0:T(8,128)(2,1)S(1)}, u32[]{:S(2)}, u32[]{:S(2)}) collective-permute-start(bf16[256,256]{1,0:T(8,128)(2,1)S(1)} %get-tuple-element.62), channel_id=1, source_target_pairs={{8,16},{16,8},{24,32},{32,24},{40,48},{48,40},{56,64},{64,56},{72,... | collective-permute-start | bytes 393224 | tf_op jit(solution)/shard_map/ppermute | solution.py:317
  70.8 5.6 %all_gather.25.inner = bf16[2,256,256]{2,1,0:T(8,128)(2,1)S(1)} all-gather(bf16[1,256,256]{2,1,0:T(8,128)(2,1)S(1)} %get-tuple-element.63), channel_id=1, replica_groups={{0,8},{16,24},{32,40},{48,56},{64,72},{80,88},{96,104},{112,120},{128,1..., dimensions={0}, use_global_device_ids=true | all-gather | bytes 393216 | tf_op jit(solution)/shard_map/all_gather | solution.py:311
  76.5 1.5 %shard_map.160 = (bf16[1024,256]{1,0:T(8,128)(2,1)}, bf16[1024,256]{1,0:T(8,128)(2,1)S(1)}, bf16[256,256]{1,0:T(8,128)(2,1)S(1)}, bf16[128,256]{1,0:T(8,128)(2,1...) custom-call(f32[1024,256]{1,0:T(8,128)S(1)} %get-tuple-element.46.own, ...), custom_call_target="tpu_custom_call" | custom-call | tf_op jit(solution)/shard_map/pallas_call | solution.py:283
  78.0 4.2 %collective-permute-start.8 = (bf16[256,256]{1,0:T(8,128)(2,1)S(1)}, bf16[256,256]{1,0:T(8,128)(2,1)S(1)}, u32[]{:S(2)}, u32[]{:S(2)}) collective-permute-start(bf16[256,256]{1,0:T(8,128)(2,1)S(1)} %get-tuple-element.52), channel_id=1, source_target_pairs={{8,16},{16,8},{24,32},{32,24},{40,48},{48,40},{56,64},{64,56},{72,... | collective-permute-start | bytes 393224 | tf_op jit(solution)/shard_map/ppermute | solution.py:317
  82.2 2.5 %collective-permute-start.9 = (bf16[128,256]{1,0:T(8,128)(2,1)S(1)}, bf16[128,256]{1,0:T(8,128)(2,1)S(1)}, u32[]{:S(2)}, u32[]{:S(2)}) collective-permute-start(bf16[128,256]{1,0:T(8,128)(2,1)S(1)} %get-tuple-element.53), channel_id=1, source_target_pairs={{0,16},{16,32},{24,8},{32,48},{40,24},{48,64},{56,40},{64,80},{72,... | collective-permute-start | bytes 196616 | tf_op jit(solution)/shard_map/ppermute | solution.py:323
  84.7 7.4 %collective-permute-done.9.far = bf16[128,256]{1,0:T(8,128)(2,1)S(1)} collective-permute-done((bf16[128,256]{1,0:T(8,128)(2,1)S(1)}, bf16[128,256]{1,0:T(8,128)(2,1)S(1)}, u32[]{:S(2)}, u32[]{:S(2)}) %collective-permute-start.9) | collective-permute-done | bytes 65568 | tf_op jit(solution)/shard_map/ppermute | solution.py:323
  92.1 0.1 shard_map.161
  92.2 5.7 %all-gather.2 = bf16[544,256]{1,0:T(8,128)(2,1)S(1)} all-gather(bf16[272,256]{1,0:T(8,128)(2,1)S(1)} %get-tuple-element.55), channel_id=4, replica_groups={{0,8},{16,24},{32,40},{48,56},{64,72},{80,88},{96,104},{112,120},{128,1..., dimensions={0}, use_global_device_ids=true | all-gather | bytes 417792 | tf_op jit(solution)/shard_map/all_gather | solution.py:311
  97.9 0.1 shard_map.162
  98.0 3.4 %collective-permute-start.10 = (bf16[256,256]{1,0:T(8,128)(2,1)S(1)}, bf16[256,256]{1,0:T(8,128)(2,1)S(1)}, u32[]{:S(2)}, u32[]{:S(2)}) collective-permute-start(bf16[256,256]{1,0:T(8,128)(2,1)S(1)} %get-tuple-element.56.pair), channel_id=1, source_target_pairs={{8,16},{16,8},{24,32},{32,24},{40,48},{48,40},{56,64},{64,56},{72,... | collective-permute-start | bytes 393224 | tf_op jit(solution)/shard_map/ppermute | solution.py:317
  101.5 2.1 %collective-permute-start.11 = (bf16[128,256]{1,0:T(8,128)(2,1)S(1)}, bf16[128,256]{1,0:T(8,128)(2,1)S(1)}, u32[]{:S(2)}, u32[]{:S(2)}) collective-permute-start(bf16[128,256]{1,0:T(8,128)(2,1)S(1)} %get-tuple-element.57), channel_id=1, source_target_pairs={{8,24},{16,0},{24,40},{32,16},{40,56},{48,32},{56,72},{64,48},{72,... | collective-permute-start | bytes 196616 | tf_op jit(solution)/shard_map/ppermute | solution.py:323
  103.6 2.8 %shard_map.163.terms = bf16[2048,256]{1,0:T(8,128)(2,1)S(1)} custom-call(bf16[2048,1280]{1,0:T(8,128)(2,1)S(1)} %shard_map.150.pick, bf16[4,512,512]{2,1,0:T(8,128)(2,1)S(1)} %shard_map.156.operator, bf16[256,256]{1,0:T(8,128)(2,1)S(1)} %get-tuple-element.58.ghost, bf16[1024,256]{1,0:T(8,128)(2,1)S(1)} %get-tuple-element.59.scaled), custom_call_target="tpu_custom_call" | custom-call | tf_op jit(solution)/shard_map/pallas_call | solution.py:283
  106.4 1.6 %shard_map.164.local = f32[1280,256]{1,0:T(8,128)S(1)} custom-call(bf16[1280,2048]{1,0:T(8,128)(2,1)S(1)} %get-tuple-element.44.place, bf16[2048,256]{1,0:T(8,128)(2,1)S(1)} %shard_map.163.terms), custom_call_target="tpu_custom_call" | custom-call | tf_op jit(solution)/shard_map/pallas_call | solution.py:283
  108.0 0.0 copy-start.2
  108.0 1.2 %collective-permute-done.11.far = bf16[128,256]{1,0:T(8,128)(2,1)S(1)} collective-permute-done((bf16[128,256]{1,0:T(8,128)(2,1)S(1)}, bf16[128,256]{1,0:T(8,128)(2,1)S(1)}, u32[]{:S(2)}, u32[]{:S(2)}) %collective-permute-start.11) | collective-permute-done | bytes 65568 | tf_op jit(solution)/shard_map/ppermute | solution.py:323
  109.2 0.7 shard_map.165
  109.9 3.8 %collective-permute-start.12 = (bf16[256,256]{1,0:T(8,128)(2,1)S(1)}, bf16[256,256]{1,0:T(8,128)(2,1)S(1)}, u32[]{:S(2)}, u32[]{:S(2)}) collective-permute-start(bf16[256,256]{1,0:T(8,128)(2,1)S(1)} %get-tuple-element.61), channel_id=1, source_target_pairs={{8,0},{16,8},{24,16},{32,24},{40,32},{48,40},{56,48},{64,56},{72,6... | collective-permute-start | bytes 393224 | tf_op jit(solution)/shard_map/ppermute | solution.py:25
  113.7 3.0 %collective-permute-done.12.received = bf16[256,256]{1,0:T(8,128)(2,1)S(1)} collective-permute-done((bf16[256,256]{1,0:T(8,128)(2,1)S(1)}, bf16[256,256]{1,0:T(8,128)(2,1)S(1)}, u32[]{:S(2)}, u32[]{:S(2)}) %collective-permute-start.12) | collective-permute-done | bytes 131104 | tf_op jit(solution)/shard_map/ppermute | solution.py:25
  116.8 1.2 %shard_map.166 = bf16[1024,256]{1,0:T(8,128)(2,1)} custom-call(f32[1024,256]{1,0:T(8,128)S(1)} %get-tuple-element.60.own, bf16[256,256]{1,0:T(8,128)(2,1)S(1)} %collective-permute-done.12.received, bf16[1024,256]{1,0:T(8,128)(2,1)S(1)} %copy-done, bf16[1024,256]{1,0:T(8,128)(2,1)S(1)} %copy-done.2, f32[1,1024]{1,0:T(1,128)S(1)} %bitcast.16, ...), custom_call_target="tpu_custom_call" | custom-call | tf_op jit(solution)/shard_map/pallas_call | solution.py:283
  (21 shorter events, 0.1 us)
Async XLA Ops:
  0.6 6.4 %collective-permute-start = (bf16[4,64,128]{2,1,0:T(8,128)(2,1)}, bf16[4,64,128]{2,1,0:T(8,128)(2,1)S(1)}, u32[]{:S(2)}, u32[]{:S(2)}) collective-permute-start(bf16[4,64,128]{2,1,0:T(8,128)(2,1)} %projectors.1), channel_id=1, source_target_pairs={{0,2},{1,3},{2,0},{3,1},{4,6},{5,7},{6,4},{7,5},{8,10},{9,11},{10,... | collective-permute-start | bytes 196616 | tf_op jit(solution)/shard_map/ppermute | solution.py:327
  7.0 10.9 %collective-permute-start.1 = (bf16[2,4,64,128]{3,2,1,0:T(8,128)(2,1)S(1)}, bf16[2,4,64,128]{3,2,1,0:T(8,128)(2,1)S(1)}, u32[]{:S(2)}, u32[]{:S(2)}) collective-permute-start(bf16[2,4,64,128]{3,2,1,0:T(8,128)(2,1)S(1)} %pad_maximum_fusion.1), channel_id=1, source_target_pairs={{0,6},{1,7},{2,4},{3,5},{4,2},{5,3},{6,0},{7,1},{8,14},{9,15},{10,... | collective-permute-start | bytes 393224 | tf_op jit(solution)/shard_map/ppermute | solution.py:327
  11.7 14.6 %collective-permute-start.2 = (bf16[272,256]{1,0:T(8,128)(2,1)S(1)}, bf16[272,256]{1,0:T(8,128)(2,1)S(1)}, u32[]{:S(2)}, u32[]{:S(2)}) collective-permute-start(bf16[272,256]{1,0:T(8,128)(2,1)S(1)} %get-tuple-element.33), channel_id=1, source_target_pairs={{0,8},{8,16},{16,24},{24,32},{32,40},{40,48},{48,56},{56,64},{64,7... | collective-permute-start | bytes 417800 | tf_op jit(solution)/shard_map/ppermute | solution.py:25
  16.2 10.1 %copy-start.6 = (s32[4,8]{1,0:T(4,128)S(1)}, s32[4,8]{1,0:T(4,128)}, u32[]{:S(2)}) copy-start(s32[4,8]{1,0:T(4,128)} %owner.1) | copy-start | bytes 388
  16.2 10.1 %copy-start.7 = (s32[4,8]{1,0:T(4,128)S(1)}, s32[4,8]{1,0:T(4,128)}, u32[]{:S(2)}) copy-start(s32[4,8]{1,0:T(4,128)} %slot.1) | copy-start | bytes 388
  26.3 28.0 %copy-start.4 = (s32[4,512]{1,0:T(4,128)S(1)}, s32[4,512]{1,0:T(4,128)}, u32[]{:S(2)}) copy-start(s32[4,512]{1,0:T(4,128)} %nodes.3) | copy-start | bytes 24580
  26.3 28.0 %copy-start.5 = (s32[1,256]{1,0:T(1,128)S(1)}, s32[1,256]{1,0:T(1,128)}, u32[]{:S(2)}) copy-start(s32[1,256]{1,0:T(1,128)} %send.3) | copy-start | bytes 3076
  26.3 30.8 %copy-start.8 = (f32[4]{0:T(128)S(1)}, f32[4]{0:T(128)}, u32[]{:S(2)}) copy-start(f32[4]{0:T(128)} %scale.1) | copy-start | bytes 52
  28.9 13.1 %collective-permute-start.3 = (bf16[256,256]{1,0:T(8,128)(2,1)S(1)}, bf16[256,256]{1,0:T(8,128)(2,1)S(1)}, u32[]{:S(2)}, u32[]{:S(2)}) collective-permute-start(bf16[256,256]{1,0:T(8,128)(2,1)S(1)} %get-tuple-element.37), channel_id=1, source_target_pairs={{8,16},{16,8},{24,32},{32,24},{40,48},{48,40},{56,64},{64,56},{72,... | collective-permute-start | bytes 393224 | tf_op jit(solution)/shard_map/ppermute | solution.py:317
  32.8 9.2 %collective-permute-start.4 = (bf16[128,256]{1,0:T(8,128)(2,1)S(1)}, bf16[128,256]{1,0:T(8,128)(2,1)S(1)}, u32[]{:S(2)}, u32[]{:S(2)}) collective-permute-start(bf16[128,256]{1,0:T(8,128)(2,1)S(1)} %get-tuple-element.38), channel_id=1, source_target_pairs={{0,16},{16,32},{24,8},{32,48},{40,24},{48,64},{56,40},{64,80},{72,... | collective-permute-start | bytes 196616 | tf_op jit(solution)/shard_map/ppermute | solution.py:323
  47.9 16.7 %collective-permute-start.5 = (bf16[256,256]{1,0:T(8,128)(2,1)S(1)}, bf16[256,256]{1,0:T(8,128)(2,1)S(1)}, u32[]{:S(2)}, u32[]{:S(2)}) collective-permute-start(bf16[256,256]{1,0:T(8,128)(2,1)S(1)} %get-tuple-element.42.pair), channel_id=1, source_target_pairs={{8,16},{16,8},{24,32},{32,24},{40,48},{48,40},{56,64},{64,56},{72,... | collective-permute-start | bytes 393224 | tf_op jit(solution)/shard_map/ppermute | solution.py:317
  52.0 12.6 %collective-permute-start.6 = (bf16[128,256]{1,0:T(8,128)(2,1)S(1)}, bf16[128,256]{1,0:T(8,128)(2,1)S(1)}, u32[]{:S(2)}, u32[]{:S(2)}) collective-permute-start(bf16[128,256]{1,0:T(8,128)(2,1)S(1)} %get-tuple-element.43), channel_id=1, source_target_pairs={{8,24},{16,0},{24,40},{32,16},{40,56},{48,32},{56,72},{64,48},{72,... | collective-permute-start | bytes 196616 | tf_op jit(solution)/shard_map/ppermute | solution.py:323
  64.1 1.0 copy-start
  64.1 1.2 %copy-start.1 = (bf16[1024,256]{1,0:T(8,128)(2,1)S(1)}, bf16[1024,256]{1,0:T(8,128)(2,1)}, u32[]{:S(2)}) copy-start(bf16[1024,256]{1,0:T(8,128)(2,1)} %prev.3) | copy-start | bytes 1572868
  64.1 1.2 %copy-start.3 = (f32[1024]{0:T(1024)S(1)}, f32[1024]{0:T(1024)}, u32[]{:S(2)}) copy-start(f32[1024]{0:T(1024)} %param.16) | copy-start | bytes 12292
  67.1 9.3 %collective-permute-start.7 = (bf16[256,256]{1,0:T(8,128)(2,1)S(1)}, bf16[256,256]{1,0:T(8,128)(2,1)S(1)}, u32[]{:S(2)}, u32[]{:S(2)}) collective-permute-start(bf16[256,256]{1,0:T(8,128)(2,1)S(1)} %get-tuple-element.62), channel_id=1, source_target_pairs={{8,16},{16,8},{24,32},{32,24},{40,48},{48,40},{56,64},{64,56},{72,... | collective-permute-start | bytes 393224 | tf_op jit(solution)/shard_map/ppermute | solution.py:317
  78.0 14.1 %collective-permute-start.8 = (bf16[256,256]{1,0:T(8,128)(2,1)S(1)}, bf16[256,256]{1,0:T(8,128)(2,1)S(1)}, u32[]{:S(2)}, u32[]{:S(2)}) collective-permute-start(bf16[256,256]{1,0:T(8,128)(2,1)S(1)} %get-tuple-element.52), channel_id=1, source_target_pairs={{8,16},{16,8},{24,32},{32,24},{40,48},{48,40},{56,64},{64,56},{72,... | collective-permute-start | bytes 393224 | tf_op jit(solution)/shard_map/ppermute | solution.py:317
  82.2 9.9 %collective-permute-start.9 = (bf16[128,256]{1,0:T(8,128)(2,1)S(1)}, bf16[128,256]{1,0:T(8,128)(2,1)S(1)}, u32[]{:S(2)}, u32[]{:S(2)}) collective-permute-start(bf16[128,256]{1,0:T(8,128)(2,1)S(1)} %get-tuple-element.53), channel_id=1, source_target_pairs={{0,16},{16,32},{24,8},{32,48},{40,24},{48,64},{56,40},{64,80},{72,... | collective-permute-start | bytes 196616 | tf_op jit(solution)/shard_map/ppermute | solution.py:323
  98.0 11.2 %collective-permute-start.10 = (bf16[256,256]{1,0:T(8,128)(2,1)S(1)}, bf16[256,256]{1,0:T(8,128)(2,1)S(1)}, u32[]{:S(2)}, u32[]{:S(2)}) collective-permute-start(bf16[256,256]{1,0:T(8,128)(2,1)S(1)} %get-tuple-element.56.pair), channel_id=1, source_target_pairs={{8,16},{16,8},{24,32},{32,24},{40,48},{48,40},{56,64},{64,56},{72,... | collective-permute-start | bytes 393224 | tf_op jit(solution)/shard_map/ppermute | solution.py:317
  101.5 7.8 %collective-permute-start.11 = (bf16[128,256]{1,0:T(8,128)(2,1)S(1)}, bf16[128,256]{1,0:T(8,128)(2,1)S(1)}, u32[]{:S(2)}, u32[]{:S(2)}) collective-permute-start(bf16[128,256]{1,0:T(8,128)(2,1)S(1)} %get-tuple-element.57), channel_id=1, source_target_pairs={{8,24},{16,0},{24,40},{32,16},{40,56},{48,32},{56,72},{64,48},{72,... | collective-permute-start | bytes 196616 | tf_op jit(solution)/shard_map/ppermute | solution.py:323
  108.0 8.8 %copy-start.2 = (bf16[1024,256]{1,0:T(8,128)(2,1)S(1)}, bf16[1024,256]{1,0:T(8,128)(2,1)}, u32[]{:S(2)}) copy-start(bf16[1024,256]{1,0:T(8,128)(2,1)} %get-tuple-element.30.first) | copy-start | bytes 1572868
  109.9 6.9 %collective-permute-start.12 = (bf16[256,256]{1,0:T(8,128)(2,1)S(1)}, bf16[256,256]{1,0:T(8,128)(2,1)S(1)}, u32[]{:S(2)}, u32[]{:S(2)}) collective-permute-start(bf16[256,256]{1,0:T(8,128)(2,1)S(1)} %get-tuple-element.61), channel_id=1, source_target_pairs={{8,0},{16,8},{24,16},{32,24},{40,32},{48,40},{56,48},{64,56},{72,6... | collective-permute-start | bytes 393224 | tf_op jit(solution)/shard_map/ppermute | solution.py:25

commit v4 on v1

--- a/solution.py
+++ b/solution.py
@@ -68,7 +68,10 @@
     return lax.rem(lax.axis_index("mesh"), 2) == 0
 
 
-def start_kernel(state, mass, send, coupling, scaled, outgoing, strengths):
+def start_kernel(
+    state, mass, send, coupling, projectors, scaled, outgoing, strengths, kept_projectors
+):
+    kept_projectors[...] = projectors[...]
     atoms, per_atom = coupling.shape
     width = atoms * per_atom
     spread = jnp.concatenate(
@@ -141,8 +144,8 @@
             for core in range(2):
                 band = (x ^ flip) * 2 + core
                 rows = pl.ds(pl.multiple_of(band * share, share), share)
-                nodes[rows, :] = projectors[core, i, c].astype(F32)
-        block = jnp.transpose(nodes[...]).astype(BF16)
+                nodes[rows, :] = projectors[core, i, c]
+        block = jnp.transpose(nodes[...])
         at_nodes = dot(block, pick[c * per_cell : (c + 1) * per_cell, :])
         at_nodes = at_nodes * jnp.where(c < live[0], 1.0, 0.0)
         for j in range(APC):
@@ -346,27 +349,28 @@
     block = atoms * per_atom
     window = 5 * block
     mass_row = mass.reshape(1, own_rows)
-    other = swap(cell_proj, "band", 2)
     start = call
-    scaled, outgoing, strengths = start(
+    scaled, outgoing, strengths, own_proj = start(
         start_kernel,
         [
             ((own_rows, orbitals), BF16),
             ((face + 16, orbitals), BF16),
             ((16, orbitals), BF16),
+            (cell_proj.shape, BF16),
         ],
-        [leave(block) for block in (state, mass_row, send_rows, coupling)],
-    )
+        [leave(block) for block in (state, mass_row, send_rows, coupling, cell_proj)],
+    )
+    other = swap(cell_proj, "band", 2)
     ghost = from_behind(outgoing, "mesh", 1)
 
     (pick,) = call(pick_kernel, [kept((cells * per_cell, extended), BF16)], (leave(cell_nodes),))
     pick = hold(pick)
-    near = jnp.stack([cell_proj, other])
+    near = jnp.stack([own_proj, other])
     far = swap(near, "band", 6)
     (operator,) = call(
         operator_kernel,
         [kept((cells, per_cell, per_cell), BF16)],
-        (leave(potential), leave(stiffness), leave(shape_values), cell_live, cell_scale),
+        (potential, stiffness, shape_values, cell_live, cell_scale),
         specs=[VMEM, VMEM, VMEM, SMEM, SMEM],
     )
     operator = hold(operator)
@@ -386,7 +390,7 @@
         scratch=[
             pltpu.VMEM((window, extended), F32),
             pltpu.VMEM((extended, orbitals), BF16),
-            pltpu.VMEM((per_cell, block), F32),
+            pltpu.VMEM((per_cell, block), BF16),
         ],
     )
     table = hold(table)

time: 120 us -> 117 us (0.975)
  waiting for transfers between devices: 28.1 us -> 26.6 us
    ppermute x2, waiting for transfers between devices: 2.97 us -> 1.37 us  [swap(): lax.ppermute(block, axis, [(i, i ^ mask) for i in range(lax.axis_size(axi...]
  transfers between devices with their start and end apart: 13 -> 13, of which waited for: 6 -> 6; matrix products, arithmetic and copies ran while one was open for 0% -> 0% of each run, Pallas kernels for 14% -> 13%
where the time goes in v4:
time: 117 us; the launch traced here: 116 us
  starting transfers between devices  43.6 us (37%)
  waiting for transfers between devices  26.6 us (23%)
  Pallas kernels  23.8 us (20%)
  blocking collectives  19.4 us (17%)
  between operations  1.66 us (1%)
    pallas_call x18, Pallas kernels, call(): pl.pallas_call(kernel, out_shape=[kept[0](*kept[1:]) if kept else jax.Sha...  23.8 us
    ppermute x5, starting transfers between devices, outer_swap(): return lax.ppermute(block, 'mesh', route)  19.3 us
    all_gather x3, blocking collectives, inner_pairs(): return lax.all_gather(block, 'mesh', axis=0, axis_index_groups=groups)  17.3 us
    ppermute x4, waiting for transfers between devices, two_away(): return lax.ppermute(block, 'mesh', [(i, j) for i, j in route if 0 <= j < n])  16 us
    ppermute x2, waiting for transfers between devices, from_behind(): return lax.ppermute(block, axis, route)  9.18 us
    ppermute x4, starting transfers between devices, two_away(): return lax.ppermute(block, 'mesh', [(i, j) for i, j in route if 0 <= j < n])  8.6 us
    ppermute x2, starting transfers between devices, swap(): lax.ppermute(block, axis, [(i, i ^ mask) for i in range(lax.axis_size(axi...  8.07 us
    ppermute x2, starting transfers between devices, from_behind(): return lax.ppermute(block, axis, route)  7.66 us
  transfers between devices with their start and end apart: 13, of which 6 were waited for; matrix products, arithmetic and copies ran while one was open for 0% of the time, Pallas kernels for 13%

profile of v4, /device:TPU:24, one launch (start us, length us, event | category | flops | bytes accessed | tf_op | source)
XLA Modules:
  0.0 116.0 jit_solution(12031756492340182103)
XLA Ops:
  0.6 3.4 %collective-permute-start = (bf16[4,64,128]{2,1,0:T(8,128)(2,1)}, bf16[4,64,128]{2,1,0:T(8,128)(2,1)S(1)}, u32[]{:S(2)}, u32[]{:S(2)}) collective-permute-start(bf16[4,64,128]{2,1,0:T(8,128)(2,1)} %projectors.1), channel_id=1, source_target_pairs={{0,2},{1,3},{2,0},{3,1},{4,6},{5,7},{6,4},{7,5},{8,10},{9,11},{10,... | collective-permute-start | bytes 196616 | tf_op jit(solution)/shard_map/ppermute | solution.py:325
  4.0 1.6 %shard_map.149 = (bf16[1024,256]{1,0:T(8,128)(2,1)S(1)}, bf16[272,256]{1,0:T(8,128)(2,1)S(1)}, bf16[16,256]{1,0:T(8,128)(2,1)S(1)}, bf16[4,64,128]{2,1,0:T(8,128)(2,1)S(1)}) custom-call(bf16[1024,256]{1,0:T(8,128)(2,1)} %state.7, f32[1,1024]{1,0:T(1,128)} %bitcast.13, s32[1,256]{1,0:T(1,128)} %send.7, f32[8,16]{1,0:T(8,128)} %coupling.1, ...), custom_call_target="tpu_custom_call" | custom-call | tf_op jit(solution)/shard_map/pallas_call | solution.py:281
  5.6 1.4 %collective-permute-done = bf16[4,64,128]{2,1,0:T(8,128)(2,1)S(1)} collective-permute-done((bf16[4,64,128]{2,1,0:T(8,128)(2,1)}, bf16[4,64,128]{2,1,0:T(8,128)(2,1)S(1)}, u32[]{:S(2)}, u32[]{:S(2)}) %collective-permute-start) | collective-permute-done | bytes 65568 | tf_op jit(solution)/shard_map/ppermute | solution.py:325
  7.0 4.7 %collective-permute-start.1 = (bf16[2,4,64,128]{3,2,1,0:T(8,128)(2,1)S(1)}, bf16[2,4,64,128]{3,2,1,0:T(8,128)(2,1)S(1)}, u32[]{:S(2)}, u32[]{:S(2)}) collective-permute-start(bf16[2,4,64,128]{3,2,1,0:T(8,128)(2,1)S(1)} %pad_maximum_fusion.1), channel_id=1, source_target_pairs={{0,6},{1,7},{2,4},{3,5},{4,2},{5,3},{6,0},{7,1},{8,14},{9,15},{10,... | collective-permute-start | bytes 393224 | tf_op jit(solution)/shard_map/ppermute | solution.py:325
  11.7 3.8 %collective-permute-start.2 = (bf16[272,256]{1,0:T(8,128)(2,1)S(1)}, bf16[272,256]{1,0:T(8,128)(2,1)S(1)}, u32[]{:S(2)}, u32[]{:S(2)}) collective-permute-start(bf16[272,256]{1,0:T(8,128)(2,1)S(1)} %get-tuple-element.30), channel_id=1, source_target_pairs={{0,8},{8,16},{16,24},{24,32},{32,40},{40,48},{48,56},{56,64},{64,7... | collective-permute-start | bytes 417800 | tf_op jit(solution)/shard_map/ppermute | solution.py:25
  16.2 0.0 copy-start.10
  16.2 1.7 %shard_map.150.pick = bf16[2048,1280]{1,0:T(8,128)(2,1)S(1)} custom-call(s32[4,512]{1,0:T(4,128)} %nodes.3), custom_call_target="tpu_custom_call" | custom-call | tf_op jit(solution)/shard_map/pallas_call | solution.py:281
  18.0 2.2 %all-gather = bf16[8,4,64,128]{3,2,1,0:T(8,128)(2,1)S(1)} all-gather(bf16[4,4,64,128]{3,2,1,0:T(8,128)(2,1)S(1)} %pad_maximum_fusion), channel_id=2, replica_groups={{0,1},{2,3},{4,5},{6,7},{8,9},{10,11},{12,13},{14,15},{16,17},{18,19},{..., dimensions={0}, use_global_device_ids=true | all-gather | bytes 786432 | tf_op jit(solution)/shard_map/all_gather | solution.py:377
  20.1 6.2 %collective-permute-done.2.ghost = bf16[272,256]{1,0:T(8,128)(2,1)S(1)} collective-permute-done((bf16[272,256]{1,0:T(8,128)(2,1)S(1)}, bf16[272,256]{1,0:T(8,128)(2,1)S(1)}, u32[]{:S(2)}, u32[]{:S(2)}) %collective-permute-start.2) | collective-permute-done | bytes 139296 | tf_op jit(solution)/shard_map/ppermute | solution.py:25
  26.3 2.6 %shard_map.151 = (bf16[640,1280]{1,0:T(8,128)(2,1)S(1)}, bf16[128,256]{1,0:T(8,128)(2,1)S(1)}, bf16[256,256]{1,0:T(8,128)(2,1)S(1)}, f32[256,256]{1,0:T(8,128)S(1)}) custom-call(bf16[2,4,4,64,128]{4,3,2,1,0:T(8,128)(2,1)S(1)} %bitcast.8, bf16[2048,1280]{1,0:T(8,128)(2,1)S(1)} %shard_map.150.pick, s32[4,8]{1,0:T(4,128)S(1)} %copy-done.9, ...), custom_call_target="tpu_custom_call" | custom-call | tf_op jit(solution)/shard_map/pallas_call | solution.py:281
  28.9 3.9 %collective-permute-start.3 = (bf16[256,256]{1,0:T(8,128)(2,1)S(1)}, bf16[256,256]{1,0:T(8,128)(2,1)S(1)}, u32[]{:S(2)}, u32[]{:S(2)}) collective-permute-start(bf16[256,256]{1,0:T(8,128)(2,1)S(1)} %get-tuple-element.34), channel_id=1, source_target_pairs={{8,16},{16,8},{24,32},{32,24},{40,48},{48,40},{56,64},{64,56},{72,... | collective-permute-start | bytes 393224 | tf_op jit(solution)/shard_map/ppermute | solution.py:315
  32.8 1.9 %collective-permute-start.4 = (bf16[128,256]{1,0:T(8,128)(2,1)S(1)}, bf16[128,256]{1,0:T(8,128)(2,1)S(1)}, u32[]{:S(2)}, u32[]{:S(2)}) collective-permute-start(bf16[128,256]{1,0:T(8,128)(2,1)S(1)} %get-tuple-element.35), channel_id=1, source_target_pairs={{0,16},{16,32},{24,8},{32,48},{40,24},{48,64},{56,40},{64,80},{72,... | collective-permute-start | bytes 196616 | tf_op jit(solution)/shard_map/ppermute | solution.py:321
  34.8 7.2 %collective-permute-done.4.far = bf16[128,256]{1,0:T(8,128)(2,1)S(1)} collective-permute-done((bf16[128,256]{1,0:T(8,128)(2,1)S(1)}, bf16[128,256]{1,0:T(8,128)(2,1)S(1)}, u32[]{:S(2)}, u32[]{:S(2)}) %collective-permute-start.4) | collective-permute-done | bytes 65568 | tf_op jit(solution)/shard_map/ppermute | solution.py:321
  42.0 0.1 shard_map.153
  42.1 5.7 %all-gather.1 = bf16[544,256]{1,0:T(8,128)(2,1)S(1)} all-gather(bf16[272,256]{1,0:T(8,128)(2,1)S(1)} %get-tuple-element.38), channel_id=3, replica_groups={{0,8},{16,24},{32,40},{48,56},{64,72},{80,88},{96,104},{112,120},{128,1..., dimensions={0}, use_global_device_ids=true | all-gather | bytes 417792 | tf_op jit(solution)/shard_map/all_gather | solution.py:309
  47.8 0.1 shard_map.154
  47.9 4.0 %collective-permute-start.5 = (bf16[256,256]{1,0:T(8,128)(2,1)S(1)}, bf16[256,256]{1,0:T(8,128)(2,1)S(1)}, u32[]{:S(2)}, u32[]{:S(2)}) collective-permute-start(bf16[256,256]{1,0:T(8,128)(2,1)S(1)} %get-tuple-element.39.pair), channel_id=1, source_target_pairs={{8,16},{16,8},{24,32},{32,24},{40,48},{48,40},{56,64},{64,56},{72,... | collective-permute-start | bytes 393224 | tf_op jit(solution)/shard_map/ppermute | solution.py:315
  52.0 0.0 copy-start.3
  52.0 0.0 copy-start.4
  52.0 2.3 %collective-permute-start.6 = (bf16[128,256]{1,0:T(8,128)(2,1)S(1)}, bf16[128,256]{1,0:T(8,128)(2,1)S(1)}, u32[]{:S(2)}, u32[]{:S(2)}) collective-permute-start(bf16[128,256]{1,0:T(8,128)(2,1)S(1)} %get-tuple-element.40), channel_id=1, source_target_pairs={{8,24},{16,0},{24,40},{32,16},{40,56},{48,32},{56,72},{64,48},{72,... | collective-permute-start | bytes 196616 | tf_op jit(solution)/shard_map/ppermute | solution.py:321
  54.3 1.1 shard_map.155.place
  55.5 1.9 %shard_map.156.operator = bf16[4,512,512]{2,1,0:T(8,128)(2,1)S(1)} custom-call(f32[4,512]{1,0:T(4,128)S(1)} %copy-done.8, bf16[512,512]{1,0:T(8,128)(2,1)S(1)} %copy-done.3, bf16[512,512]{1,0:T(8,128)(2,1)S(1)} %copy-done.4, s32[1]{0:T(128)S(6)} %copy.16.live, f32[4]{0:T(128)S(1)} %copy-done.11), custom_call_target="tpu_custom_call" | custom-call | tf_op jit(solution)/shard_map/pallas_call | solution.py:281
  57.4 2.8 %shard_map.157.terms = bf16[2048,256]{1,0:T(8,128)(2,1)S(1)} custom-call(bf16[2048,1280]{1,0:T(8,128)(2,1)S(1)} %shard_map.150.pick, bf16[4,512,512]{2,1,0:T(8,128)(2,1)S(1)} %shard_map.156.operator, bf16[272,256]{1,0:T(8,128)(2,1)S(1)} %collective-permute-done.2.ghost, bf16[1024,256]{1,0:T(8,128)(2,1)S(1)} %get-tuple-element.31.scaled), custom_call_target="tpu_custom_call" | custom-call | tf_op jit(solution)/shard_map/pallas_call | solution.py:281
  60.2 1.6 %shard_map.158.local = f32[1280,256]{1,0:T(8,128)S(1)} custom-call(bf16[1280,2048]{1,0:T(8,128)(2,1)S(1)} %shard_map.155.place, bf16[2048,256]{1,0:T(8,128)(2,1)S(1)} %shard_map.157.terms), custom_call_target="tpu_custom_call" | custom-call | tf_op jit(solution)/shard_map/pallas_call | solution.py:281
  61.8 0.0 copy-start
  61.9 0.5 shard_map.152.turned
  62.4 0.5 copy-done
  62.8 0.2 copy-done.1
  63.0 1.8 %shard_map.159 = (bf16[256,256]{1,0:T(8,128)(2,1)S(1)}, f32[1024,256]{1,0:T(8,128)S(1)}, bf16[256,256]{1,0:T(8,128)(2,1)}, bf16[2,256,256]{2,1,0:T(8,128)(2,1)S(1)}) custom-call(bf16[1280,640]{1,0:T(8,128)(2,1)S(1)} %shard_map.152.turned, bf16[256,256]{1,0:T(8,128)(2,1)S(1)} %get-tuple-element.39.pair, bf16[256,256]{1,0:T(8,128)(2,1)S(1)} %collective-permute-done.5.near, ...), custom_call_target="tpu_custom_call" | custom-call | tf_op jit(solution)/shard_map/pallas_call | solution.py:281
  64.9 3.7 %collective-permute-start.7 = (bf16[256,256]{1,0:T(8,128)(2,1)S(1)}, bf16[256,256]{1,0:T(8,128)(2,1)S(1)}, u32[]{:S(2)}, u32[]{:S(2)}) collective-permute-start(bf16[256,256]{1,0:T(8,128)(2,1)S(1)} %get-tuple-element.56), channel_id=1, source_target_pairs={{8,16},{16,8},{24,32},{32,24},{40,48},{48,40},{56,64},{64,56},{72,... | collective-permute-start | bytes 393224 | tf_op jit(solution)/shard_map/ppermute | solution.py:315
  68.6 5.8 %all_gather.25.inner = bf16[2,256,256]{2,1,0:T(8,128)(2,1)S(1)} all-gather(bf16[1,256,256]{2,1,0:T(8,128)(2,1)S(1)} %get-tuple-element.57), channel_id=1, replica_groups={{0,8},{16,24},{32,40},{48,56},{64,72},{80,88},{96,104},{112,120},{128,1..., dimensions={0}, use_global_device_ids=true | all-gather | bytes 393216 | tf_op jit(solution)/shard_map/all_gather | solution.py:309
  74.4 1.5 %shard_map.160 = (bf16[1024,256]{1,0:T(8,128)(2,1)}, bf16[1024,256]{1,0:T(8,128)(2,1)S(1)}, bf16[256,256]{1,0:T(8,128)(2,1)S(1)}, bf16[128,256]{1,0:T(8,128)(2,1...) custom-call(f32[1024,256]{1,0:T(8,128)S(1)} %get-tuple-element.41.own, ...), custom_call_target="tpu_custom_call" | custom-call | tf_op jit(solution)/shard_map/pallas_call | solution.py:281
  75.9 4.2 %collective-permute-start.8 = (bf16[256,256]{1,0:T(8,128)(2,1)S(1)}, bf16[256,256]{1,0:T(8,128)(2,1)S(1)}, u32[]{:S(2)}, u32[]{:S(2)}) collective-permute-start(bf16[256,256]{1,0:T(8,128)(2,1)S(1)} %get-tuple-element.46), channel_id=1, source_target_pairs={{8,16},{16,8},{24,32},{32,24},{40,48},{48,40},{56,64},{64,56},{72,... | collective-permute-start | bytes 393224 | tf_op jit(solution)/shard_map/ppermute | solution.py:315
  80.2 2.5 %collective-permute-start.9 = (bf16[128,256]{1,0:T(8,128)(2,1)S(1)}, bf16[128,256]{1,0:T(8,128)(2,1)S(1)}, u32[]{:S(2)}, u32[]{:S(2)}) collective-permute-start(bf16[128,256]{1,0:T(8,128)(2,1)S(1)} %get-tuple-element.47), channel_id=1, source_target_pairs={{0,16},{16,32},{24,8},{32,48},{40,24},{48,64},{56,40},{64,80},{72,... | collective-permute-start | bytes 196616 | tf_op jit(solution)/shard_map/ppermute | solution.py:321
  82.7 7.4 %collective-permute-done.9.far = bf16[128,256]{1,0:T(8,128)(2,1)S(1)} collective-permute-done((bf16[128,256]{1,0:T(8,128)(2,1)S(1)}, bf16[128,256]{1,0:T(8,128)(2,1)S(1)}, u32[]{:S(2)}, u32[]{:S(2)}) %collective-permute-start.9) | collective-permute-done | bytes 65568 | tf_op jit(solution)/shard_map/ppermute | solution.py:321
  90.0 0.1 shard_map.161
  90.1 5.7 %all-gather.2 = bf16[544,256]{1,0:T(8,128)(2,1)S(1)} all-gather(bf16[272,256]{1,0:T(8,128)(2,1)S(1)} %get-tuple-element.49), channel_id=4, replica_groups={{0,8},{16,24},{32,40},{48,56},{64,72},{80,88},{96,104},{112,120},{128,1..., dimensions={0}, use_global_device_ids=true | all-gather | bytes 417792 | tf_op jit(solution)/shard_map/all_gather | solution.py:309
  95.8 0.1 shard_map.162
  96.0 3.4 %collective-permute-start.10 = (bf16[256,256]{1,0:T(8,128)(2,1)S(1)}, bf16[256,256]{1,0:T(8,128)(2,1)S(1)}, u32[]{:S(2)}, u32[]{:S(2)}) collective-permute-start(bf16[256,256]{1,0:T(8,128)(2,1)S(1)} %get-tuple-element.50.pair), channel_id=1, source_target_pairs={{8,16},{16,8},{24,32},{32,24},{40,48},{48,40},{56,64},{64,56},{72,... | collective-permute-start | bytes 393224 | tf_op jit(solution)/shard_map/ppermute | solution.py:315
  99.4 1.9 %collective-permute-start.11 = (bf16[128,256]{1,0:T(8,128)(2,1)S(1)}, bf16[128,256]{1,0:T(8,128)(2,1)S(1)}, u32[]{:S(2)}, u32[]{:S(2)}) collective-permute-start(bf16[128,256]{1,0:T(8,128)(2,1)S(1)} %get-tuple-element.51), channel_id=1, source_target_pairs={{8,24},{16,0},{24,40},{32,16},{40,56},{48,32},{56,72},{64,48},{72,... | collective-permute-start | bytes 196616 | tf_op jit(solution)/shard_map/ppermute | solution.py:321
  101.3 2.8 %shard_map.163.terms = bf16[2048,256]{1,0:T(8,128)(2,1)S(1)} custom-call(bf16[2048,1280]{1,0:T(8,128)(2,1)S(1)} %shard_map.150.pick, bf16[4,512,512]{2,1,0:T(8,128)(2,1)S(1)} %shard_map.156.operator, bf16[256,256]{1,0:T(8,128)(2,1)S(1)} %get-tuple-element.52.ghost, bf16[1024,256]{1,0:T(8,128)(2,1)S(1)} %get-tuple-element.53.scaled), custom_call_target="tpu_custom_call" | custom-call | tf_op jit(solution)/shard_map/pallas_call | solution.py:281
  104.2 1.6 %shard_map.164.local = f32[1280,256]{1,0:T(8,128)S(1)} custom-call(bf16[1280,2048]{1,0:T(8,128)(2,1)S(1)} %shard_map.155.place, bf16[2048,256]{1,0:T(8,128)(2,1)S(1)} %shard_map.163.terms), custom_call_target="tpu_custom_call" | custom-call | tf_op jit(solution)/shard_map/pallas_call | solution.py:281
  105.7 0.0 copy-start.2
  105.7 1.4 %collective-permute-done.11.far = bf16[128,256]{1,0:T(8,128)(2,1)S(1)} collective-permute-done((bf16[128,256]{1,0:T(8,128)(2,1)S(1)}, bf16[128,256]{1,0:T(8,128)(2,1)S(1)}, u32[]{:S(2)}, u32[]{:S(2)}) %collective-permute-start.11) | collective-permute-done | bytes 65568 | tf_op jit(solution)/shard_map/ppermute | solution.py:321
  107.2 0.7 shard_map.165
  107.9 3.8 %collective-permute-start.12 = (bf16[256,256]{1,0:T(8,128)(2,1)S(1)}, bf16[256,256]{1,0:T(8,128)(2,1)S(1)}, u32[]{:S(2)}, u32[]{:S(2)}) collective-permute-start(bf16[256,256]{1,0:T(8,128)(2,1)S(1)} %get-tuple-element.55), channel_id=1, source_target_pairs={{8,0},{16,8},{24,16},{32,24},{40,32},{48,40},{56,48},{64,56},{72,6... | collective-permute-start | bytes 393224 | tf_op jit(solution)/shard_map/ppermute | solution.py:25
  111.7 3.0 %collective-permute-done.12.received = bf16[256,256]{1,0:T(8,128)(2,1)S(1)} collective-permute-done((bf16[256,256]{1,0:T(8,128)(2,1)S(1)}, bf16[256,256]{1,0:T(8,128)(2,1)S(1)}, u32[]{:S(2)}, u32[]{:S(2)}) %collective-permute-start.12) | collective-permute-done | bytes 131104 | tf_op jit(solution)/shard_map/ppermute | solution.py:25
  114.7 1.3 %shard_map.166 = bf16[1024,256]{1,0:T(8,128)(2,1)} custom-call(f32[1024,256]{1,0:T(8,128)S(1)} %get-tuple-element.54.own, bf16[256,256]{1,0:T(8,128)(2,1)S(1)} %collective-permute-done.12.received, bf16[1024,256]{1,0:T(8,128)(2,1)S(1)} %copy-done, bf16[1024,256]{1,0:T(8,128)(2,1)S(1)} %copy-done.2, f32[1,1024]{1,0:T(1,128)S(1)} %bitcast.16, ...), custom_call_target="tpu_custom_call" | custom-call | tf_op jit(solution)/shard_map/pallas_call | solution.py:281
  (27 shorter events, 0.1 us)
Async XLA Ops:
  0.6 6.4 %collective-permute-start = (bf16[4,64,128]{2,1,0:T(8,128)(2,1)}, bf16[4,64,128]{2,1,0:T(8,128)(2,1)S(1)}, u32[]{:S(2)}, u32[]{:S(2)}) collective-permute-start(bf16[4,64,128]{2,1,0:T(8,128)(2,1)} %projectors.1), channel_id=1, source_target_pairs={{0,2},{1,3},{2,0},{3,1},{4,6},{5,7},{6,4},{7,5},{8,10},{9,11},{10,... | collective-permute-start | bytes 196616 | tf_op jit(solution)/shard_map/ppermute | solution.py:325
  7.0 10.9 %collective-permute-start.1 = (bf16[2,4,64,128]{3,2,1,0:T(8,128)(2,1)S(1)}, bf16[2,4,64,128]{3,2,1,0:T(8,128)(2,1)S(1)}, u32[]{:S(2)}, u32[]{:S(2)}) collective-permute-start(bf16[2,4,64,128]{3,2,1,0:T(8,128)(2,1)S(1)} %pad_maximum_fusion.1), channel_id=1, source_target_pairs={{0,6},{1,7},{2,4},{3,5},{4,2},{5,3},{6,0},{7,1},{8,14},{9,15},{10,... | collective-permute-start | bytes 393224 | tf_op jit(solution)/shard_map/ppermute | solution.py:325
  11.7 14.6 %collective-permute-start.2 = (bf16[272,256]{1,0:T(8,128)(2,1)S(1)}, bf16[272,256]{1,0:T(8,128)(2,1)S(1)}, u32[]{:S(2)}, u32[]{:S(2)}) collective-permute-start(bf16[272,256]{1,0:T(8,128)(2,1)S(1)} %get-tuple-element.30), channel_id=1, source_target_pairs={{0,8},{8,16},{16,24},{24,32},{32,40},{40,48},{48,56},{56,64},{64,7... | collective-permute-start | bytes 417800 | tf_op jit(solution)/shard_map/ppermute | solution.py:25
  16.2 10.1 %copy-start.9 = (s32[4,8]{1,0:T(4,128)S(1)}, s32[4,8]{1,0:T(4,128)}, u32[]{:S(2)}) copy-start(s32[4,8]{1,0:T(4,128)} %owner.1) | copy-start | bytes 388
  16.2 10.1 %copy-start.10 = (s32[4,8]{1,0:T(4,128)S(1)}, s32[4,8]{1,0:T(4,128)}, u32[]{:S(2)}) copy-start(s32[4,8]{1,0:T(4,128)} %slot.1) | copy-start | bytes 388
  26.3 28.0 %copy-start.6 = (s32[4,512]{1,0:T(4,128)S(1)}, s32[4,512]{1,0:T(4,128)}, u32[]{:S(2)}) copy-start(s32[4,512]{1,0:T(4,128)} %nodes.3) | copy-start | bytes 24580
  28.9 13.1 %collective-permute-start.3 = (bf16[256,256]{1,0:T(8,128)(2,1)S(1)}, bf16[256,256]{1,0:T(8,128)(2,1)S(1)}, u32[]{:S(2)}, u32[]{:S(2)}) collective-permute-start(bf16[256,256]{1,0:T(8,128)(2,1)S(1)} %get-tuple-element.34), channel_id=1, source_target_pairs={{8,16},{16,8},{24,32},{32,24},{40,48},{48,40},{56,64},{64,56},{72,... | collective-permute-start | bytes 393224 | tf_op jit(solution)/shard_map/ppermute | solution.py:315
  32.8 9.2 %collective-permute-start.4 = (bf16[128,256]{1,0:T(8,128)(2,1)S(1)}, bf16[128,256]{1,0:T(8,128)(2,1)S(1)}, u32[]{:S(2)}, u32[]{:S(2)}) collective-permute-start(bf16[128,256]{1,0:T(8,128)(2,1)S(1)} %get-tuple-element.35), channel_id=1, source_target_pairs={{0,16},{16,32},{24,8},{32,48},{40,24},{48,64},{56,40},{64,80},{72,... | collective-permute-start | bytes 196616 | tf_op jit(solution)/shard_map/ppermute | solution.py:321
  47.9 14.4 %collective-permute-start.5 = (bf16[256,256]{1,0:T(8,128)(2,1)S(1)}, bf16[256,256]{1,0:T(8,128)(2,1)S(1)}, u32[]{:S(2)}, u32[]{:S(2)}) collective-permute-start(bf16[256,256]{1,0:T(8,128)(2,1)S(1)} %get-tuple-element.39.pair), channel_id=1, source_target_pairs={{8,16},{16,8},{24,32},{32,24},{40,48},{48,40},{56,64},{64,56},{72,... | collective-permute-start | bytes 393224 | tf_op jit(solution)/shard_map/ppermute | solution.py:315
  52.0 3.5 %copy-start.3 = (bf16[512,512]{1,0:T(8,128)(2,1)S(1)}, bf16[512,512]{1,0:T(8,128)(2,1)}, u32[]{:S(2)}) copy-start(bf16[512,512]{1,0:T(8,128)(2,1)} %stiffness.1) | copy-start | bytes 1572868
  52.0 3.5 %copy-start.4 = (bf16[512,512]{1,0:T(8,128)(2,1)S(1)}, bf16[512,512]{1,0:T(8,128)(2,1)}, u32[]{:S(2)}) copy-start(bf16[512,512]{1,0:T(8,128)(2,1)} %shape_values.1) | copy-start | bytes 1572868
  52.0 3.5 %copy-start.8 = (f32[4,512]{1,0:T(4,128)S(1)}, f32[4,512]{1,0:T(4,128)}, u32[]{:S(2)}) copy-start(f32[4,512]{1,0:T(4,128)} %potential.1) | copy-start | bytes 24580
  52.0 3.4 %copy-start.11 = (f32[4]{0:T(128)S(1)}, f32[4]{0:T(128)}, u32[]{:S(2)}) copy-start(f32[4]{0:T(128)} %scale.1) | copy-start | bytes 52
  52.0 10.3 %collective-permute-start.6 = (bf16[128,256]{1,0:T(8,128)(2,1)S(1)}, bf16[128,256]{1,0:T(8,128)(2,1)S(1)}, u32[]{:S(2)}, u32[]{:S(2)}) collective-permute-start(bf16[128,256]{1,0:T(8,128)(2,1)S(1)} %get-tuple-element.40), channel_id=1, source_target_pairs={{8,24},{16,0},{24,40},{32,16},{40,56},{48,32},{56,72},{64,48},{72,... | collective-permute-start | bytes 196616 | tf_op jit(solution)/shard_map/ppermute | solution.py:321
  61.8 1.0 copy-start
  61.8 1.2 %copy-start.1 = (bf16[1024,256]{1,0:T(8,128)(2,1)S(1)}, bf16[1024,256]{1,0:T(8,128)(2,1)}, u32[]{:S(2)}) copy-start(bf16[1024,256]{1,0:T(8,128)(2,1)} %prev.3) | copy-start | bytes 1572868
  61.8 1.2 %copy-start.5 = (f32[1024]{0:T(1024)S(1)}, f32[1024]{0:T(1024)}, u32[]{:S(2)}) copy-start(f32[1024]{0:T(1024)} %param.16) | copy-start | bytes 12292
  61.8 1.2 %copy-start.7 = (s32[1,256]{1,0:T(1,128)S(1)}, s32[1,256]{1,0:T(1,128)}, u32[]{:S(2)}) copy-start(s32[1,256]{1,0:T(1,128)} %send.7) | copy-start | bytes 3076
  64.9 9.5 %collective-permute-start.7 = (bf16[256,256]{1,0:T(8,128)(2,1)S(1)}, bf16[256,256]{1,0:T(8,128)(2,1)S(1)}, u32[]{:S(2)}, u32[]{:S(2)}) collective-permute-start(bf16[256,256]{1,0:T(8,128)(2,1)S(1)} %get-tuple-element.56), channel_id=1, source_target_pairs={{8,16},{16,8},{24,32},{32,24},{40,48},{48,40},{56,64},{64,56},{72,... | collective-permute-start | bytes 393224 | tf_op jit(solution)/shard_map/ppermute | solution.py:315
  75.9 14.1 %collective-permute-start.8 = (bf16[256,256]{1,0:T(8,128)(2,1)S(1)}, bf16[256,256]{1,0:T(8,128)(2,1)S(1)}, u32[]{:S(2)}, u32[]{:S(2)}) collective-permute-start(bf16[256,256]{1,0:T(8,128)(2,1)S(1)} %get-tuple-element.46), channel_id=1, source_target_pairs={{8,16},{16,8},{24,32},{32,24},{40,48},{48,40},{56,64},{64,56},{72,... | collective-permute-start | bytes 393224 | tf_op jit(solution)/shard_map/ppermute | solution.py:315
  80.2 9.9 %collective-permute-start.9 = (bf16[128,256]{1,0:T(8,128)(2,1)S(1)}, bf16[128,256]{1,0:T(8,128)(2,1)S(1)}, u32[]{:S(2)}, u32[]{:S(2)}) collective-permute-start(bf16[128,256]{1,0:T(8,128)(2,1)S(1)} %get-tuple-element.47), channel_id=1, source_target_pairs={{0,16},{16,32},{24,8},{32,48},{40,24},{48,64},{56,40},{64,80},{72,... | collective-permute-start | bytes 196616 | tf_op jit(solution)/shard_map/ppermute | solution.py:321
  96.0 11.2 %collective-permute-start.10 = (bf16[256,256]{1,0:T(8,128)(2,1)S(1)}, bf16[256,256]{1,0:T(8,128)(2,1)S(1)}, u32[]{:S(2)}, u32[]{:S(2)}) collective-permute-start(bf16[256,256]{1,0:T(8,128)(2,1)S(1)} %get-tuple-element.50.pair), channel_id=1, source_target_pairs={{8,16},{16,8},{24,32},{32,24},{40,48},{48,40},{56,64},{64,56},{72,... | collective-permute-start | bytes 393224 | tf_op jit(solution)/shard_map/ppermute | solution.py:315
  99.4 7.8 %collective-permute-start.11 = (bf16[128,256]{1,0:T(8,128)(2,1)S(1)}, bf16[128,256]{1,0:T(8,128)(2,1)S(1)}, u32[]{:S(2)}, u32[]{:S(2)}) collective-permute-start(bf16[128,256]{1,0:T(8,128)(2,1)S(1)} %get-tuple-element.51), channel_id=1, source_target_pairs={{8,24},{16,0},{24,40},{32,16},{40,56},{48,32},{56,72},{64,48},{72,... | collective-permute-start | bytes 196616 | tf_op jit(solution)/shard_map/ppermute | solution.py:321
  105.7 9.0 %copy-start.2 = (bf16[1024,256]{1,0:T(8,128)(2,1)S(1)}, bf16[1024,256]{1,0:T(8,128)(2,1)}, u32[]{:S(2)}) copy-start(bf16[1024,256]{1,0:T(8,128)(2,1)} %get-tuple-element.27.first) | copy-start | bytes 1572868
  107.9 6.9 %collective-permute-start.12 = (bf16[256,256]{1,0:T(8,128)(2,1)S(1)}, bf16[256,256]{1,0:T(8,128)(2,1)S(1)}, u32[]{:S(2)}, u32[]{:S(2)}) collective-permute-start(bf16[256,256]{1,0:T(8,128)(2,1)S(1)} %get-tuple-element.55), channel_id=1, source_target_pairs={{8,0},{16,8},{24,16},{32,24},{40,32},{48,40},{56,48},{64,56},{72,6... | collective-permute-start | bytes 393224 | tf_op jit(solution)/shard_map/ppermute | solution.py:25
